TPU v7x, 256 devices: a whole 4x4x8 slice. The times are simulated.
256 devices in a mesh: expert: 64 (over y, z, x_lo), pair: 4 (over x_hi, core).
Axes of the slice: x: 4 (x_hi: 2, x_lo: 2; x = x_hi * 2 + x_lo), y: 4, z: 8, core: 2. Of those that a mesh axis runs over, the one named last changes fastest.
Arguments:
- policy_tokens: bfloat16 [3072, 2048], P('expert'), may hold values from -6 to 6
- policy_cotangent: bfloat16 [3072, 2048], P('expert'), may hold values from -6 to 6
- frozen_tokens: bfloat16 [3072, 2048], P('expert'), may hold values from -6 to 6
- policy_route: int32 [3072, 8], P('expert'), may hold values from 0 to 127, all different within a row; in each aligned block of 48 rows (0 to 47, 48 to 95, ...) at most 4 rows name the same one
- policy_gates: float32 [3072, 8], P('expert'), may hold values from 0.1 to 1
- frozen_route: int32 [3072, 8], P('expert'), may hold values from 0 to 127, all different within a row; in each aligned block of 48 rows (0 to 47, 48 to 95, ...) at most 4 rows name the same one
- frozen_gates: float32 [3072, 8], P('expert'), may hold values from 0.1 to 1
- w_gate: bfloat16 [128, 2048, 768], P('expert', None, 'pair'), may hold values from -0.125 to 0.125
- w_up: bfloat16 [128, 2048, 768], P('expert', None, 'pair'), may hold values from -0.125 to 0.125
- w_down: bfloat16 [128, 768, 2048], P('expert', 'pair'), may hold values from -0.21875 to 0.21875
- adapter_down: bfloat16 [128, 768, 64], P('expert', 'pair'), may hold values from -0.21875 to 0.21875
- adapter_up: bfloat16 [128, 64, 2048], P('expert'), may hold values from -0.75 to 0.75
Outputs:
- frozen_out: bfloat16 [3072, 2048], P('expert', 'pair')
- input_grad: bfloat16 [3072, 2048], P('expert', 'pair')
- adapter_down_grad: float32 [128, 768, 64], P('expert', 'pair')
- adapter_up_grad: float32 [128, 64, 2048], P('expert')
Inputs may be any that keep to these rules, and one draw needn't show every extreme that they name: `policy_route`: each row names 8 different experts; among the rows of one device no expert is named by more than 4 rows. `frozen_route`: each row names 8 different experts; among the rows of one device no expert is named by more than 4 rows.
All inputs are finite; a program needn't handle non-finite values.
Results may differ from a plain program's by a relative error of at most 0.012.
Values may be sent and summed in bfloat16 or wider, within the bound.
No kernel may reach another device: no remote copies, remote signals or barrier semaphores. Data moves between devices by JAX's collectives and lax.ppermute only.
A program may use at most 64 MiB of HBM per device.

v0:
```python
import jax
import jax.numpy as jnp
from jax import lax
from jax.sharding import PartitionSpec as P

CAP = 256


adapter_scale = 2.0


def gathered_total(value, axis):
    return lax.all_gather(value, axis).astype(jnp.float32).sum(0)


def slot_tables(route, gates, experts, slot_count):
    chosen = route.reshape(-1)
    expert_ids = jnp.arange(experts, dtype=jnp.int32)
    one_hot = (chosen[:, None] == expert_ids[None, :]).astype(jnp.int32)
    earlier = jnp.cumsum(one_hot, axis=0) - one_hot
    position = jnp.sum(earlier * one_hot, axis=1)
    target = chosen * slot_count + position
    slot_ids = jnp.arange(experts * slot_count, dtype=jnp.int32)
    matched = (slot_ids[:, None] == target[None, :]).astype(jnp.float32)
    matched = matched.reshape(experts * slot_count, route.shape[0], route.shape[1])
    member_table = jnp.sum(matched, axis=2)
    gate_table = jnp.sum(matched * gates[None, :, :], axis=2)
    return (member_table, gate_table)


def send_rows(member_table, tokens, buffer_shape):
    sent = jnp.dot(member_table.astype(jnp.bfloat16), tokens, preferred_element_type=jnp.float32)
    return sent.astype(jnp.bfloat16).reshape(buffer_shape)


def projections(rows, w_gate, w_up):
    gate_pre = jnp.einsum("nesd,edf->nesf", rows, w_gate, preferred_element_type=jnp.float32)
    up_pre = jnp.einsum("nesd,edf->nesf", rows, w_up, preferred_element_type=jnp.float32)
    sigmoid_gate = jax.nn.sigmoid(gate_pre)
    activated = gate_pre * sigmoid_gate
    hidden = (activated * up_pre).astype(jnp.bfloat16)
    return (gate_pre, up_pre, sigmoid_gate, activated, hidden)


def combine(partial_rows, table):
    highest = lax.Precision.HIGHEST
    rounded = lax.optimization_barrier(partial_rows.astype(jnp.bfloat16))
    shares = lax.psum_scatter(
        rounded.astype(jnp.float32).astype(jnp.bfloat16), "pair", scatter_dimension=3, tiled=True
    ).astype(jnp.float32)
    returned = lax.all_to_all(
        shares.astype(jnp.bfloat16), "expert", split_axis=0, concat_axis=0, tiled=True
    ).astype(shares.dtype)
    rows = returned.reshape(-1, returned.shape[3])
    result = jnp.dot(table.T, rows, precision=highest)
    return result.astype(jnp.bfloat16)


def frozen_pass(frozen_tokens, frozen_route, frozen_gates, w_gate, w_up, w_down):
    groups = lax.axis_size("expert")
    slot_count = CAP // groups
    experts = w_gate.shape[0] * groups
    member_table, gate_table = slot_tables(frozen_route, frozen_gates, experts, slot_count)
    buffer_shape = (groups, w_gate.shape[0], slot_count, frozen_tokens.shape[1])
    rows = lax.all_to_all(
        send_rows(member_table, frozen_tokens, buffer_shape),
        "expert",
        split_axis=0,
        concat_axis=0,
        tiled=True,
    )
    gate_pre, up_pre, sigmoid_gate, activated, hidden = projections(rows, w_gate, w_up)
    partial_rows = jnp.einsum("nesf,efd->nesd", hidden, w_down, preferred_element_type=jnp.float32)
    return combine(partial_rows, gate_table)


def policy_pass(
    policy_tokens,
    policy_cotangent,
    policy_route,
    policy_gates,
    w_gate,
    w_up,
    w_down,
    adapter_down,
    adapter_up,
):
    groups = lax.axis_size("expert")
    slot_count = CAP // groups
    experts = w_gate.shape[0] * groups
    member_table, gate_table = slot_tables(policy_route, policy_gates, experts, slot_count)
    buffer_shape = (groups, w_gate.shape[0], slot_count, policy_tokens.shape[1])
    token_send = send_rows(member_table, policy_tokens, buffer_shape)
    cot_send = jnp.dot(
        gate_table, policy_cotangent.astype(jnp.float32), precision=lax.Precision.HIGHEST
    )
    cot_send = cot_send.astype(jnp.bfloat16).reshape(buffer_shape)
    rows, cot_rows = (
        lax.all_to_all(token_send, "expert", split_axis=0, concat_axis=0, tiled=True),
        lax.all_to_all(cot_send, "expert", split_axis=0, concat_axis=0, tiled=True),
    )
    gate_pre, up_pre, sigmoid_gate, activated, hidden = projections(rows, w_gate, w_up)
    inner_part = jnp.einsum(
        "nesf,efr->nesr", hidden, adapter_down, preferred_element_type=jnp.float32
    )
    inner = (
        gathered_total(inner_part.astype(jnp.bfloat16), "pair")
        .astype(jnp.float32)
        .astype(jnp.bfloat16)
    )
    up_grad_adapter = adapter_scale * jnp.einsum(
        "nesr,nesd->erd", inner, cot_rows, preferred_element_type=jnp.float32
    )
    inner_grad = adapter_scale * jnp.einsum(
        "nesd,erd->nesr", cot_rows, adapter_up, preferred_element_type=jnp.float32
    )
    inner_grad = inner_grad.astype(jnp.bfloat16)
    down_grad_adapter = jnp.einsum(
        "nesf,nesr->efr", hidden, inner_grad, preferred_element_type=jnp.float32
    )
    hidden_grad = jnp.einsum("nesd,efd->nesf", cot_rows, w_down, preferred_element_type=jnp.float32)
    hidden_grad = hidden_grad + jnp.einsum(
        "nesr,efr->nesf", inner_grad, adapter_down, preferred_element_type=jnp.float32
    )
    gate_grad = (
        hidden_grad * up_pre * sigmoid_gate * (1.0 + gate_pre * (1.0 - sigmoid_gate))
    ).astype(jnp.bfloat16)
    up_grad = (hidden_grad * activated).astype(jnp.bfloat16)
    row_grad = jnp.einsum("nesf,edf->nesd", gate_grad, w_gate, preferred_element_type=jnp.float32)
    row_grad = row_grad + jnp.einsum(
        "nesf,edf->nesd", up_grad, w_up, preferred_element_type=jnp.float32
    )
    input_grad = combine(row_grad, member_table)
    return (input_grad, down_grad_adapter, up_grad_adapter)


def per_device(
    policy_tokens,
    policy_cotangent,
    frozen_tokens,
    policy_route,
    policy_gates,
    frozen_route,
    frozen_gates,
    w_gate,
    w_up,
    w_down,
    adapter_down,
    adapter_up,
):
    input_grad, down_grad_adapter, up_grad_adapter = policy_pass(
        policy_tokens,
        policy_cotangent,
        policy_route,
        policy_gates,
        w_gate,
        w_up,
        w_down,
        adapter_down,
        adapter_up,
    )
    frozen_out = frozen_pass(frozen_tokens, frozen_route, frozen_gates, w_gate, w_up, w_down)
    return (frozen_out, input_grad, down_grad_adapter, up_grad_adapter)


def solution(mesh):
    in_specs = (
        P("expert", None),
        P("expert", None),
        P("expert", None),
        P("expert", None),
        P("expert", None),
        P("expert", None),
        P("expert", None),
        P("expert", None, "pair"),
        P("expert", None, "pair"),
        P("expert", "pair", None),
        P("expert", "pair", None),
        P("expert", None, None),
    )
    out_specs = (
        P("expert", "pair"),
        P("expert", "pair"),
        P("expert", "pair", None),
        P("expert", None, None),
    )
    return jax.shard_map(
        per_device, mesh=mesh, in_specs=in_specs, out_specs=out_specs, check_vma=False
    )
```

profile of v0, /device:TPU:32, one launch (start us, length us, event | category | flops | bytes accessed | tf_op | source)
XLA Modules:
  0.0 289.1 jit_solution(5765034669563204222)
XLA Ops:
  7.2 0.9 copy.104
  11.2 3.2 %convolution_convert_fusion.1 = bf16[512,2048]{1,0:T(8,128)(2,1)} fusion(f32[512,48]{0,1:T(8,128)S(1)} %get-tuple-element.4, bf16[48,2048]{1,0:T(8,128)(2,1)S(1)} %copy-done.7), kind=kOutput, calls=%fused_computation.2 | convolution fusion | flops 605028352 | bytes 2392064 | tf_op jit(solution)/shard_map/dot_general | solution.py:94
  14.4 4.1 %reshape.99 = bf16[64,2,4,2048]{3,2,1,0:T(4,128)(2,1)} reshape(bf16[512,2048]{1,0:T(8,128)(2,1)} %convolution_convert_fusion.1) | data formatting | bytes 4194304 | tf_op jit(solution)/shard_map/reshape | solution.py:97
  18.5 13.0 %all-to-all-start.2 = ((bf16[64,2,4,2048]{3,2,1,0:T(4,128)(2,1)}), bf16[64,2,4,2048]{3,2,1,0:T(4,128)(2,1)}, u32[]{:S(2)}, u32[]{:S(2)}) async-start(bf16[64,2,4,2048]{3,2,1,0:T(4,128)(2,1)} %reshape.99), calls=%async_computation.3 | async-start | bytes 4194304 | tf_op jit(solution)/shard_map/all_to_all | solution.py:100
  31.6 2.1 convolution_convert_fusion
  33.6 4.1 %reshape.100 = bf16[64,2,4,2048]{3,2,1,0:T(4,128)(2,1)} reshape(bf16[512,2048]{1,0:T(8,128)(2,1)} %convolution_convert_fusion) | data formatting | bytes 4194304 | tf_op jit(solution)/shard_map/reshape | solution.py:33
  37.8 43.8 %all-to-all-done.2 = bf16[64,2,4,2048]{3,2,1,0:T(4,128)(2,1)} async-done(((bf16[64,2,4,2048]{3,2,1,0:T(4,128)(2,1)}), bf16[64,2,4,2048]{3,2,1,0:T(4,128)(2,1)}, u32[]{:S(2)}, u32[]{:S(2)}) %all-to-all-start.2) | async-done | bytes 2097184 | tf_op jit(solution)/shard_map/all_to_all | solution.py:100
  81.6 7.4 %all-to-all-start.3 = ((bf16[64,2,4,2048]{3,2,1,0:T(4,128)(2,1)}), bf16[64,2,4,2048]{3,2,1,0:T(4,128)(2,1)}, u32[]{:S(2)}, u32[]{:S(2)}) async-start(bf16[64,2,4,2048]{3,2,1,0:T(4,128)(2,1)} %reshape.100), calls=%async_computation.4 | async-start | bytes 4194304 | tf_op jit(solution)/shard_map/all_to_all | solution.py:99
  90.3 1.2 convert_reduce_fusion.1
  91.5 2.1 convolution_convert_fusion.3
  93.6 4.2 %reshape.96 = bf16[64,2,4,2048]{3,2,1,0:T(4,128)(2,1)} reshape(bf16[512,2048]{1,0:T(8,128)(2,1)} %convolution_convert_fusion.3) | data formatting | bytes 4194304 | tf_op jit(solution)/shard_map/reshape | solution.py:33
  97.8 4.1 %fusion.62 = bf16[64,2,4,64]{3,0,2,1:T(8,128)(2,1)S(1)} fusion(bf16[64,2,4,2048]{3,2,1,0:T(4,128)(2,1)} %all-to-all-done.2, bf16[2,64,2048]{2,1,0:T(8,128)(2,1)S(1)} %copy-done.13), kind=kOutput, calls=%fused_computation.42 | convolution fusion | flops 134283264 | bytes 2686976 | tf_op jit(solution)/shard_map/nesd,erd->nesr/dot_general | solution.py:114
  101.9 4.2 %fusion.14 = f32[2,64,4,192]{3,1,2,0:T(8,128)S(1)} fusion(bf16[64,2,4,2048]{3,2,1,0:T(4,128)(2,1)} %all-to-all-done.2, bf16[2,192,2048]{2,1,0:T(8,128)(2,1)S(1)} %copy-done.12), kind=kOutput, calls=%fused_computation.20 | convolution fusion | flops 402653184 | bytes 4063232 | tf_op jit(solution)/shard_map/nesd,efd->nesf/dot_general | solution.py:121
  106.3 32.0 %all-to-all-done.3 = bf16[64,2,4,2048]{3,2,1,0:T(4,128)(2,1)} async-done(((bf16[64,2,4,2048]{3,2,1,0:T(4,128)(2,1)}), bf16[64,2,4,2048]{3,2,1,0:T(4,128)(2,1)}, u32[]{:S(2)}, u32[]{:S(2)}) %all-to-all-start.3) | async-done | bytes 2097184 | tf_op jit(solution)/shard_map/all_to_all | solution.py:99
  138.3 7.5 %all-to-all-start = ((bf16[64,2,4,2048]{3,2,1,0:T(4,128)(2,1)}), bf16[64,2,4,2048]{3,2,1,0:T(4,128)(2,1)}, u32[]{:S(2)}, u32[]{:S(2)}) async-start(bf16[64,2,4,2048]{3,2,1,0:T(4,128)(2,1)} %reshape.96), calls=%async_computation | async-start | bytes 4194304 | tf_op jit(solution)/shard_map/all_to_all | solution.py:65
  146.1 4.5 %fusion.40 = f32[64,2,4,192]{3,0,2,1:T(8,128)S(1)} fusion(bf16[2,2048,192]{1,2,0:T(8,128)(2,1)} %param.19, bf16[64,2,4,2048]{3,2,1,0:T(4,128)(2,1)} %all-to-all-done.3), kind=kOutput, calls=%fused_computation.34 | convolution fusion | flops 402653184 | bytes 4063232 | tf_op jit(solution)/shard_map/nesd,edf->nesf/dot_general | solution.py:37
  150.6 4.2 %multiply_convert_fusion = (bf16[64,2,4,192]{3,0,2,1:T(8,128)(2,1)S(1)}, f32[64,2,4,192]{3,0,2,1:T(8,128)S(1)}) fusion(f32[64,2,4,192]{3,0,2,1:T(8,128)S(1)} %fusion.40, bf16[2,2048,192]{1,2,0:T(8,128)(2,1)S(1)} %copy-done, bf16[64,2,4,2048]{3,2,1,0:T(4,128)(2,1)} %all-to-all-done.3), kind=kOutput, calls=%fused_computation.54 | convolution fusion | flops 403243008 | bytes 4653056 | tf_op jit(solution)/shard_map/nesd,edf->nesf/dot_general | solution.py:38
  154.9 0.8 fusion.16
  155.7 2.1 fusion.1
  158.2 36.9 %all-to-all-done = bf16[64,2,4,2048]{3,2,1,0:T(4,128)(2,1)} async-done(((bf16[64,2,4,2048]{3,2,1,0:T(4,128)(2,1)}), bf16[64,2,4,2048]{3,2,1,0:T(4,128)(2,1)}, u32[]{:S(2)}, u32[]{:S(2)}) %all-to-all-start) | async-done | bytes 2097184 | tf_op jit(solution)/shard_map/all_to_all | solution.py:65
  195.1 4.9 %fusion.25 = f32[64,2,4,192]{3,0,2,1:T(8,128)} fusion(bf16[2,2048,192]{1,2,0:T(8,128)(2,1)S(1)} %copy-done.2, bf16[64,2,4,2048]{3,2,1,0:T(4,128)(2,1)} %all-to-all-done), kind=kOutput, calls=%fused_computation.31 | convolution fusion | flops 402653184 | bytes 4063232 | tf_op jit(solution)/shard_map/nesd,edf->nesf/dot_general | solution.py:37
  199.9 6.8 %fusion = bf16[64,2,4,2048]{3,0,2,1:T(8,128)(2,1)} fusion(bf16[2,192,2048]{2,1,0:T(8,128)(2,1)} %param.21, bf16[2,2048,192]{1,2,0:T(8,128)(2,1)S(1)} %copy-done, bf16[64,2,4,2048]{3,2,1,0:T(4,128)(2,1)} %all-to-all-done, f32[64,2,4,192]{3,0,2,1:T(8,128)} %fusion.25), kind=kOutput, calls=%fused_computation.5 | convolution fusion | flops 806944768 | bytes 7733248 | tf_op jit(solution)/shard_map/nesf,efd->nesd/dot_general | solution.py:73
  206.8 2.2 copy.115
  209.0 7.4 %all-to-all-start.4 = ((bf16[64,2,4,512]{3,2,1,0:T(4,128)(2,1)}), bf16[64,2,4,512]{3,2,1,0:T(4,128)(2,1)S(1)}, u32[]{:S(2)}, u32[]{:S(2)}) async-start(bf16[64,2,4,512]{3,2,1,0:T(4,128)(2,1)} %copy.115), calls=%async_computation.6 | async-start | bytes 1048576 | tf_op jit(solution)/shard_map/all_to_all | solution.py:51
  216.4 32.6 %reduce-scatter.3.cloned.1.call-done = bf16[64,2,4,512]{3,0,2,1:T(8,128)(2,1)} async-done(((bf16[64,2,4,2048]{3,0,2,1:T(8,128)(2,1)}), bf16[64,2,4,512]{3,0,2,1:T(8,128)(2,1)}) %reduce-scatter.3.cloned.1.call-update) | async-done | bytes 524304 | tf_op jit(solution)/shard_map/reduce_scatter | solution.py:48
  249.1 2.2 copy.103
  251.3 10.5 %all-to-all-start.1 = ((bf16[64,2,4,512]{3,2,1,0:T(4,128)(2,1)}), bf16[64,2,4,512]{3,2,1,0:T(4,128)(2,1)S(1)}, u32[]{:S(2)}, u32[]{:S(2)}) async-start(bf16[64,2,4,512]{3,2,1,0:T(4,128)(2,1)} %copy.103), calls=%async_computation.2 | async-start | bytes 1048576 | tf_op jit(solution)/shard_map/all_to_all | solution.py:51
  262.0 10.3 %all-gather = bf16[256,2,4,64]{3,0,2,1:T(8,128)(2,1)S(1)} all-gather(bf16[64,2,4,64]{3,0,2,1:T(8,128)(2,1)S(1)} %fusion.65), channel_id=2, replica_groups=mesh['expert'=64,'pair'=4] {'pair'}, dimensions={0}, use_global_device_ids=true | all-gather | bytes 327680 | tf_op jit(solution)/shard_map/all_gather | solution.py:13
  273.1 1.8 convolution_bitcast_fusion.1
  274.9 5.1 %fusion.2 = f32[2,64,2048]{2,1,0:T(8,128)} fusion(bf16[64,2,4,64]{3,0,2,1:T(8,128)(2,1)} %reduce_sum.78, bf16[64,2,4,2048]{3,2,1,0:T(4,128)(2,1)} %all-to-all-done.2), kind=kOutput, calls=%fused_computation.8 | convolution fusion | flops 134479872 | bytes 3211264 | tf_op jit(solution)/shard_map/nesr,nesd->erd/dot_general | solution.py:111
  280.1 1.0 convolution_convert_fusion.5
  281.2 1.0 convolution_convert_fusion.6
  (70 shorter events, 6.4 us)
Async XLA Ops:
  7.2 143.5 %copy-start = (bf16[2,2048,192]{1,2,0:T(8,128)(2,1)S(1)}, bf16[2,2048,192]{1,2,0:T(8,128)(2,1)}, u32[]{:S(2)}) copy-start(bf16[2,2048,192]{1,2,0:T(8,128)(2,1)} %param.20) | copy-start | bytes 4718596
  7.2 4.0 %copy-start.7 = (bf16[48,2048]{1,0:T(8,128)(2,1)S(1)}, bf16[48,2048]{1,0:T(8,128)(2,1)}, u32[]{:S(2)}) copy-start(bf16[48,2048]{1,0:T(8,128)(2,1)} %param.13) | copy-start | bytes 589828
  18.5 13.0 %copy-start.8 = (bf16[48,2048]{1,0:T(8,128)(2,1)S(1)}, bf16[48,2048]{1,0:T(8,128)(2,1)}, u32[]{:S(2)}) copy-start(bf16[48,2048]{1,0:T(8,128)(2,1)} %param.12) | copy-start | bytes 589828
  18.5 63.1 %all-to-all-start.2 = ((bf16[64,2,4,2048]{3,2,1,0:T(4,128)(2,1)}), bf16[64,2,4,2048]{3,2,1,0:T(4,128)(2,1)}, u32[]{:S(2)}, u32[]{:S(2)}) async-start(bf16[64,2,4,2048]{3,2,1,0:T(4,128)(2,1)} %reshape.99), calls=%async_computation.3 | async-start | bytes 4194304 | tf_op jit(solution)/shard_map/all_to_all | solution.py:100
  37.8 51.3 %copy-start.10 = (s32[48,8]{0,1:T(8,128)S(1)}, s32[48,8]{0,1:T(8,128)}, u32[]{:S(2)}) copy-start(s32[48,8]{0,1:T(8,128)} %param.17) | copy-start | bytes 4612
  37.8 51.5 %copy-start.11 = (f32[48,8]{0,1:T(8,128)S(1)}, f32[48,8]{0,1:T(8,128)}, u32[]{:S(2)}) copy-start(f32[48,8]{0,1:T(8,128)} %param.18) | copy-start | bytes 4612
  37.8 53.7 %copy-start.9 = (bf16[48,2048]{1,0:T(8,128)(2,1)S(1)}, bf16[48,2048]{1,0:T(8,128)(2,1)}, u32[]{:S(2)}) copy-start(bf16[48,2048]{1,0:T(8,128)(2,1)} %param.14) | copy-start | bytes 589828
  81.6 56.7 %all-to-all-start.3 = ((bf16[64,2,4,2048]{3,2,1,0:T(4,128)(2,1)}), bf16[64,2,4,2048]{3,2,1,0:T(4,128)(2,1)}, u32[]{:S(2)}, u32[]{:S(2)}) async-start(bf16[64,2,4,2048]{3,2,1,0:T(4,128)(2,1)} %reshape.100), calls=%async_computation.4 | async-start | bytes 4194304 | tf_op jit(solution)/shard_map/all_to_all | solution.py:99
  93.6 4.2 %copy-start.13 = (bf16[2,64,2048]{2,1,0:T(8,128)(2,1)S(1)}, bf16[2,64,2048]{2,1,0:T(8,128)(2,1)}, u32[]{:S(2)}) copy-start(bf16[2,64,2048]{2,1,0:T(8,128)(2,1)} %param.23) | copy-start | bytes 1572868
  97.8 4.1 %copy-start.12 = (bf16[2,192,2048]{2,1,0:T(8,128)(2,1)S(1)}, bf16[2,192,2048]{2,1,0:T(8,128)(2,1)}, u32[]{:S(2)}) copy-start(bf16[2,192,2048]{2,1,0:T(8,128)(2,1)} %param.21) | copy-start | bytes 4718596
  101.9 4.2 %copy-start.3 = (bf16[64,2,4,64]{3,0,2,1:T(8,128)(2,1)}, bf16[64,2,4,64]{3,0,2,1:T(8,128)(2,1)S(1)}, u32[]{:S(2)}) copy-start(bf16[64,2,4,64]{3,0,2,1:T(8,128)(2,1)S(1)} %fusion.62) | copy-start | bytes 196612
  101.9 4.2 %copy-start.5 = (bf16[2,192,64]{1,2,0:T(8,128)(2,1)S(1)}, bf16[2,192,64]{1,2,0:T(8,128)(2,1)}, u32[]{:S(2)}) copy-start(bf16[2,192,64]{1,2,0:T(8,128)(2,1)} %param.22) | copy-start | bytes 147460
  138.3 56.7 %all-to-all-start = ((bf16[64,2,4,2048]{3,2,1,0:T(4,128)(2,1)}), bf16[64,2,4,2048]{3,2,1,0:T(4,128)(2,1)}, u32[]{:S(2)}, u32[]{:S(2)}) async-start(bf16[64,2,4,2048]{3,2,1,0:T(4,128)(2,1)} %reshape.96), calls=%async_computation | async-start | bytes 4194304 | tf_op jit(solution)/shard_map/all_to_all | solution.py:65
  145.8 61.0 %reduce-scatter.5.cloned.1.call-start = ((), (), s32[]{:S(2)}) async-start(), calls=%async_computation.8 | async-start | bytes 2621440 | tf_op jit(solution)/shard_map/reduce_scatter | solution.py:48
  150.6 4.3 %copy-start.1 = (bf16[2,2048,192]{1,2,0:T(8,128)(2,1)S(1)}, bf16[2,2048,192]{1,2,0:T(8,128)(2,1)}, u32[]{:S(2)}) copy-start(bf16[2,2048,192]{1,2,0:T(8,128)(2,1)} %param.19) | copy-start | bytes 4718596
  157.9 37.2 %copy-start.2 = (bf16[2,2048,192]{1,2,0:T(8,128)(2,1)S(1)}, bf16[2,2048,192]{1,2,0:T(8,128)(2,1)}, u32[]{:S(2)}) copy-start(bf16[2,2048,192]{1,2,0:T(8,128)(2,1)} %param.19) | copy-start | bytes 4718596
  157.9 91.2 %reduce-scatter.3.cloned.1.call-start = ((), (), s32[]{:S(2)}) async-start(), calls=%async_computation.7 | async-start | bytes 2621440 | tf_op jit(solution)/shard_map/reduce_scatter | solution.py:48
  206.7 55.1 %copy-start.6 = (bf16[2,192,64]{1,2,0:T(8,128)(2,1)S(1)}, bf16[2,192,64]{1,2,0:T(8,128)(2,1)}, u32[]{:S(2)}) copy-start(bf16[2,192,64]{1,2,0:T(8,128)(2,1)} %param.22) | copy-start | bytes 147460
  209.0 42.3 %all-to-all-start.4 = ((bf16[64,2,4,512]{3,2,1,0:T(4,128)(2,1)}), bf16[64,2,4,512]{3,2,1,0:T(4,128)(2,1)S(1)}, u32[]{:S(2)}, u32[]{:S(2)}) async-start(bf16[64,2,4,512]{3,2,1,0:T(4,128)(2,1)} %copy.115), calls=%async_computation.6 | async-start | bytes 1048576 | tf_op jit(solution)/shard_map/all_to_all | solution.py:51
  251.3 29.8 %all-to-all-start.1 = ((bf16[64,2,4,512]{3,2,1,0:T(4,128)(2,1)}), bf16[64,2,4,512]{3,2,1,0:T(4,128)(2,1)S(1)}, u32[]{:S(2)}, u32[]{:S(2)}) async-start(bf16[64,2,4,512]{3,2,1,0:T(4,128)(2,1)} %copy.103), calls=%async_computation.2 | async-start | bytes 1048576 | tf_op jit(solution)/shard_map/all_to_all | solution.py:51
  280.0 1.3 copy-start.4
Sparse Core Ops, SparseCore 0:
  158.0 46.0 reduce-scatter.4
  206.9 42.0 reduce-scatter.2
where the time goes:
time: 292 us; the launch traced here: 289 us
  waiting for transfers between devices  145 us (50%)
  matrix products  48.3 us (17%)
  starting transfers between devices  46.4 us (16%)
  local copies, waits for them, and re-layouts  20.1 us (7%)
  between operations  14.3 us (5%)
  blocking collectives  10.3 us (4%)
  other arithmetic  4.2 us (1%)
    all_to_all x1, waiting for transfers between devices, policy_pass(): lax.all_to_all(cot_send, 'expert', split_axis=0, concat_axis=0, tiled=True)  43.8 us
    all_to_all x1, waiting for transfers between devices, frozen_pass(): lax.all_to_all(send_rows(member_table, frozen_tokens, buffer_shape), 'exp...  36.9 us
    reduce_scatter x2, waiting for transfers between devices, combine(): lax.psum_scatter(rounded.astype(jnp.float32).astype(jnp.bfloat16), 'pair'...  32.6 us
    all_to_all x1, waiting for transfers between devices, policy_pass(): lax.all_to_all(token_send, 'expert', split_axis=0, concat_axis=0, tiled=T...  32 us
    all_to_all x2, starting transfers between devices, combine(): lax.all_to_all(shares.astype(jnp.bfloat16), 'expert', split_axis=0, conca...  17.9 us
    all_to_all x1, starting transfers between devices, policy_pass(): lax.all_to_all(cot_send, 'expert', split_axis=0, concat_axis=0, tiled=True)  13 us
    all_gather x1, blocking collectives, gathered_total(): return lax.all_gather(value, axis).astype(jnp.float32).sum(0)  10.3 us
    dot_general x2, matrix products, projections(): jnp.einsum('nesd,edf->nesf', rows, w_gate, preferred_element_type=jnp.flo...  9.43 us
  transfers between devices with their start and end apart: 7, of which 4 were waited for; matrix products, arithmetic and copies ran while one was open for 21% of the time, Pallas kernels for 0%

commit v1 on v0

v1 whole, which is shorter than its diff:
```python
import functools
import jax
import jax.numpy as jnp
from jax import lax
from jax.experimental import pallas as pl
from jax.experimental.pallas import tpu as pltpu
from jax.sharding import Mesh, PartitionSpec as P

BF = jnp.bfloat16
F32 = jnp.float32
SCALE = 2.0
SLOT = 4
PEERS = 32
TOK = 48
Q = 512


def nt(a, b):
    return lax.dot_general(a, b, (((1,), (1,)), ((), ())), preferred_element_type=F32)


def nn(a, b):
    return lax.dot_general(a, b, (((1,), (0,)), ((), ())), preferred_element_type=F32)


def tn(a, b):
    return lax.dot_general(a, b, (((0,), (0,)), ((), ())), preferred_element_type=F32)


def vmem_call(body, outs, args, flops=0, smem=1):
    specs = [pl.BlockSpec(memory_space=pltpu.SMEM)] * smem
    specs += [pl.BlockSpec(memory_space=pltpu.VMEM)] * (len(args) - smem)
    moved = sum(a.size * a.dtype.itemsize for a in args)
    moved += sum(o.size * o.dtype.itemsize for o in outs)
    return pl.pallas_call(
        body,
        out_shape=outs,
        in_specs=specs,
        out_specs=[pl.BlockSpec(memory_space=pltpu.VMEM)] * len(outs),
        compiler_params=pltpu.CompilerParams(vmem_limit_bytes=60 << 20),
        cost_estimate=pl.CostEstimate(flops=flops, bytes_accessed=moved, transcendentals=0),
    )(*args)


def tables(where_ref, meta, route_at, gate_at):
    rows = 2 * TOK
    cols = PEERS * 2 * SLOT
    col = lax.broadcasted_iota(jnp.int32, (rows, cols), 1)
    row = lax.broadcasted_iota(jnp.int32, (rows, cols), 0)
    expert = (4 * (col // 8) + where_ref[0]).astype(F32)
    named = jnp.zeros((rows, cols), F32)
    gate = jnp.zeros((rows, cols), F32)
    for k in range(8):
        match = meta[:, route_at + k : route_at + k + 1] == expert
        named = named + jnp.where(match, 1.0, 0.0)
        gate = gate + jnp.where(match, meta[:, gate_at + k : gate_at + k + 1], 0.0)
    r0 = lax.broadcasted_iota(jnp.int32, (rows, rows), 0)
    r1 = lax.broadcasted_iota(jnp.int32, (rows, rows), 1)
    earlier = jnp.where((r1 < r0) & ((r1 < TOK) == (r0 < TOK)), 1.0, 0.0)
    position = nn(earlier.astype(BF), named.astype(BF))
    here = (position == (col % SLOT).astype(F32)) & (((col // SLOT) % 2) == (row // TOK))
    member = jnp.where(here, named, 0.0)
    return member, jnp.where(here, gate, 0.0)


def pieces(x):
    hi = x.astype(BF)
    rest = x - hi.astype(F32)
    mid = rest.astype(BF)
    return hi, mid, (rest - mid.astype(F32)).astype(BF)


def select_body(where_ref, meta_a, meta_b, own, other, sent, member_p, gates_f):
    meta = jnp.concatenate([meta_a[...], meta_b[...]], axis=0)
    mem_p, gate_p = tables(where_ref, meta, 0, 8)
    mem_f, gate_f = tables(where_ref, meta, 16, 24)
    member_p[...] = mem_p.astype(BF)
    hi, mid, low = pieces(gate_f)
    gates_f[0] = hi
    gates_f[1] = mid
    gates_f[2] = low
    both = [jnp.concatenate([own[i], other[i]], axis=0) for i in range(3)]
    shape = (PEERS, 8, 2 * Q)
    sent[:, 0:8, :] = tn(mem_p.astype(BF), both[0]).astype(BF).reshape(shape)
    sent[:, 8:16, :] = tn(mem_f.astype(BF), both[1]).astype(BF).reshape(shape)
    hi, mid, low = pieces(gate_p)
    cot = tn(low, both[2]) + tn(mid, both[2]) + tn(hi, both[2])
    sent[:, 16:24, :] = cot.astype(BF).reshape(shape)


def main_body(
    where_ref, mine, theirs, wg, wu, wd, ad, au, wg2, wu2, wd2, ad2,
    grad_rows, frozen_rows, inner_part, down_grad, down_grad2,
):
    c, e = where_ref[1], where_ref[2]
    rows = PEERS * 8

    def block(ref, i, h):
        return ref[:, 8 * i : 8 * i + 8, h * Q : (h + 1) * Q].reshape(rows, Q)

    def contract(i, weight, index):
        total = None
        for ref, core in ((mine, c), (theirs, 1 - c)):
            for h in range(2):
                at = pl.ds(pl.multiple_of((2 * h + core) * Q, Q), Q)
                w = weight[:, at] if index is None else weight[index, :, at]
                part = nt(block(ref, i, h), w)
                total = part if total is None else total + part
        return total

    inner_grad = (SCALE * contract(2, au, e)).astype(BF)
    inner = None
    grads, frozen = [], []
    for n, (g, u, d, a, index) in enumerate(((wg, wu, wd, ad, e), (wg2, wu2, wd2, ad2, None))):
        gate_pre = contract(1, g, index)
        up_pre = contract(1, u, index)
        frozen.append((gate_pre * jax.nn.sigmoid(gate_pre) * up_pre).astype(BF))
        gate_pre = contract(0, g, index)
        up_pre = contract(0, u, index)
        sigmoid = jax.nn.sigmoid(gate_pre)
        activated = gate_pre * sigmoid
        hidden = (activated * up_pre).astype(BF)
        adapter = a[...] if index is None else a[index]
        part = nt(hidden, adapter)
        inner = part if inner is None else inner + part
        out = down_grad if n == 0 else down_grad2
        out[...] = tn(inner_grad, hidden)
        hidden_grad = contract(2, d, index) + nn(inner_grad, adapter)
        gate_grad = (hidden_grad * up_pre * sigmoid * (1.0 + gate_pre * (1.0 - sigmoid))).astype(BF)
        grads.append((gate_grad, (hidden_grad * activated).astype(BF)))
    inner_part[...] = inner

    def take(weight, index, at):
        return weight[:, at] if index is None else weight[index, :, at]

    for q in range(4):
        at = slice(q * Q, (q + 1) * Q)
        frozen_rows[:, at] = (
            nn(frozen[0], take(wd, e, at)) + nn(frozen[1], take(wd2, None, at))
        ).astype(BF)
        total = nn(grads[0][0], take(wg, e, at)) + nn(grads[0][1], take(wu, e, at))
        total = total + nn(grads[1][0], take(wg2, None, at)) + nn(grads[1][1], take(wu2, None, at))
        grad_rows[:, at] = total.astype(BF)


def combine_body(member_p, gates_f, back, out):
    rows = PEERS * 8
    out[0] = (
        nn(gates_f[2], back[:, 8:16, :].reshape(rows, 2 * Q))
        + nn(gates_f[1], back[:, 8:16, :].reshape(rows, 2 * Q))
        + nn(gates_f[0], back[:, 8:16, :].reshape(rows, 2 * Q))
    )
    out[1] = nn(member_p[...], back[:, 0:8, :].reshape(rows, 2 * Q))


def swap(x, axis):
    return lax.ppermute(x, axis, [(0, 1), (1, 0)])


def swap_both(x):
    return lax.ppermute(x, ("xl", "xh"), [(i, 3 - i) for i in range(4)])


def exchange(x):
    return lax.all_to_all(x, ("y", "z"), split_axis=0, concat_axis=0, tiled=True)


def pick(c, a, b):
    return jnp.where(c == 0, a, b)


def per_device(
    policy_tokens, policy_cotangent, frozen_tokens, policy_route, policy_gates,
    frozen_route, frozen_gates, w_gate, w_up, w_down, adapter_down, adapter_up,
):
    c, xh, xl = lax.axis_index("core"), lax.axis_index("xh"), lax.axis_index("xl")
    where = jnp.stack([2 * xl + xh, c, xh]).astype(jnp.int32)
    wg, wu = w_gate.swapaxes(1, 2), w_up.swapaxes(1, 2)
    ad = adapter_down.swapaxes(1, 2)

    def away(w):
        return lax.dynamic_index_in_dim(w, 1 - xh, 0, keepdims=False)

    def half(x):
        return jnp.concatenate(
            [pick(c, x[:, 0:Q], x[:, Q : 2 * Q]), pick(c, x[:, 2 * Q : 3 * Q], x[:, 3 * Q :])], axis=1
        )

    meta = jnp.concatenate(
        [policy_route.astype(F32), policy_gates, frozen_route.astype(F32), frozen_gates], axis=1
    )
    own = jnp.stack([half(policy_tokens), half(frozen_tokens), half(policy_cotangent)])
    meta_b, other = swap(meta, "xl"), swap(own, "xl")
    wg2, wu2, wd2, ad2 = [swap(away(w), "xh") for w in (wg, wu, w_down, ad)]

    sent, member_p, gates_f = vmem_call(
        select_body,
        [
            jax.ShapeDtypeStruct((PEERS, 24, 2 * Q), BF),
            jax.ShapeDtypeStruct((2 * TOK, 256), BF),
            jax.ShapeDtypeStruct((3, 2 * TOK, 256), BF),
        ],
        [where, meta, meta_b, own, other],
        flops=10**9,
    )
    mine = exchange(sent)
    theirs = swap(mine, "core")
    rows = PEERS * 8
    grad_rows, frozen_rows, inner_part, down_grad, down_grad2 = vmem_call(
        main_body,
        [
            jax.ShapeDtypeStruct((rows, 4 * Q), BF),
            jax.ShapeDtypeStruct((rows, 4 * Q), BF),
            jax.ShapeDtypeStruct((rows, 64), F32),
            jax.ShapeDtypeStruct((64, 192), F32),
            jax.ShapeDtypeStruct((64, 192), F32),
        ],
        [where, mine, theirs, wg, wu, w_down, ad, adapter_up, wg2, wu2, wd2, ad2],
        flops=4 * 10**9,
    )

    def half_rows(x, core):
        return jnp.concatenate(
            [pick(core, x[:, 0:Q], x[:, Q : 2 * Q]), pick(core, x[:, 2 * Q : 3 * Q], x[:, 3 * Q :])], axis=1
        ).reshape(PEERS, 8, 2 * Q)

    give = jnp.concatenate([half_rows(grad_rows, 1 - c), half_rows(frozen_rows, 1 - c)], axis=1)
    keep = jnp.concatenate([half_rows(grad_rows, c), half_rows(frozen_rows, c)], axis=1)
    got = swap(give, "core")
    total = (keep.astype(F32) + got.astype(F32)).astype(BF)
    back = exchange(total)
    (both,) = vmem_call(
        combine_body,
        [jax.ShapeDtypeStruct((2, 2 * TOK, 2 * Q), F32)],
        [member_p, gates_f, back],
        flops=10**8,
        smem=0,
    )

    def part(j, h):
        return both[:, j * TOK : (j + 1) * TOK, h * Q : (h + 1) * Q]

    def quarter(j, h):
        return pick(h, part(j, 0), part(j, 1))

    outs = quarter(0, xh) + swap(quarter(0, 1 - xh), "xh")
    outs = outs + swap(quarter(1, xh), "xl") + swap_both(quarter(1, 1 - xh))
    outs = outs.astype(BF)

    inner = (inner_part + swap(inner_part, "core")).astype(BF)
    cot = mine[:, 16:24, :].reshape(rows, 2 * Q)
    up_half = SCALE * tn(inner, cot)
    up_other = swap(up_half, "core")
    lo, hi = pick(c, up_half, up_other), pick(c, up_other, up_half)
    up_own = jnp.concatenate([lo[:, :Q], hi[:, :Q], lo[:, Q:], hi[:, Q:]], axis=1)
    up_away = swap(up_own, "xh")
    up_grad = jnp.stack([pick(xh, up_own, up_away), pick(xh, up_away, up_own)])
    down_away = swap(down_grad2, "xh")
    down = jnp.stack([pick(xh, down_grad, down_away), pick(xh, down_away, down_grad)]).swapaxes(1, 2)
    return outs[0], outs[1], down, up_grad


def solution(mesh):
    fine = Mesh(mesh.devices.reshape(4, 8, 2, 2, 2), ("y", "z", "xl", "xh", "core"))
    ex, pr = ("y", "z", "xl"), ("xh", "core")
    in_specs = (P(ex, None),) * 7 + (
        P(ex, None, pr), P(ex, None, pr), P(ex, pr, None), P(ex, pr, None), P(ex, None, None),
    )
    out_specs = (P(ex, pr), P(ex, pr), P(ex, pr, None), P(ex, None, None))
    return jax.shard_map(
        per_device, mesh=fine, in_specs=in_specs, out_specs=out_specs, check_vma=False
    )
```

time: 292 us -> 195 us (0.67)
  waiting for transfers between devices: 145 us -> 83.3 us
  matrix products: 48.3 us -> 1.27 us
  blocking collectives: 10.3 us -> 50.6 us
  starting transfers between devices: 46.4 us -> 22.3 us
  Pallas kernels: 0 us -> 17.4 us
  between operations: 14.3 us -> 0.98 us
  local copies, waits for them, and re-layouts: 20.1 us -> 8.49 us
  other arithmetic: 4.2 us -> 10.2 us
    all_to_all x5 -> x1, waiting for transfers between devices: 113 us -> 7.96 us  [exchange(): lax.all_to_all(x, ('y', 'z'), split_axis=0, concat_axis=0, tiled=True)]
    ppermute x0 -> x15, waiting for transfers between devices: none -> 75.4 us  [the longest x14 75.1 us: swap(): return lax.ppermute(x, axis, [(0, 1), (1, 0)])]
    all_to_all x0 -> x1, blocking collectives: none -> 50.6 us  [exchange(): lax.all_to_all(x, ('y', 'z'), split_axis=0, concat_axis=0, tiled=True)]
    dot_general x17 -> x1, matrix products: 48.3 us -> 1.27 us  [tn(): lax.dot_general(a, b, (((0,), (0,)), ((), ())), preferred_element_type=F32)]
    all_to_all x5 -> x1, starting transfers between devices: 45.8 us -> 4.84 us  [exchange(): lax.all_to_all(x, ('y', 'z'), split_axis=0, concat_axis=0, tiled=True)]
    reduce_scatter x2 -> x0, waiting for transfers between devices: 32.6 us -> none  [combine(): lax.psum_scatter(rounded.astype(jnp.float32).astype(jnp.bfloat16), 'pair'...]
    ppermute x0 -> x15, starting transfers between devices: none -> 17.5 us  [the longest x14 17 us: swap(): return lax.ppermute(x, axis, [(0, 1), (1, 0)])]
    pallas_call x0 -> x3, Pallas kernels: none -> 17.4 us  [vmem_call(): pl.pallas_call(body, out_shape=outs, in_specs=specs, out_specs=[pl.BlockS...]
  transfers between devices with their start and end apart: 7 -> 16, of which waited for: 4 -> 9; matrix products, arithmetic and copies ran while one was open for 21% -> 5% of each run, Pallas kernels for 0% -> 0%
where the time goes in v1:
time: 195 us
  waiting for transfers between devices  83.3 us (43%)
  blocking collectives  50.6 us (26%)
  starting transfers between devices  22.3 us (11%)
  Pallas kernels  17.4 us (9%)
  other arithmetic  10.2 us (5%)
  local copies, waits for them, and re-layouts  8.49 us (4%)
    ppermute x14, waiting for transfers between devices, swap(): return lax.ppermute(x, axis, [(0, 1), (1, 0)])  75.1 us
    all_to_all x1, blocking collectives, exchange(): lax.all_to_all(x, ('y', 'z'), split_axis=0, concat_axis=0, tiled=True)  50.6 us
    pallas_call x3, Pallas kernels, vmem_call(): pl.pallas_call(body, out_shape=outs, in_specs=specs, out_specs=[pl.BlockS...  17.4 us
    ppermute x14, starting transfers between devices, swap(): return lax.ppermute(x, axis, [(0, 1), (1, 0)])  17 us
    all_to_all x1, waiting for transfers between devices, exchange(): lax.all_to_all(x, ('y', 'z'), split_axis=0, concat_axis=0, tiled=True)  7.96 us
    select_n x6, other arithmetic, pick(): return jnp.where(c == 0, a, b)  5.76 us
    all_to_all x1, starting transfers between devices, exchange(): lax.all_to_all(x, ('y', 'z'), split_axis=0, concat_axis=0, tiled=True)  4.84 us
    squeeze x4, local copies, waits for them, and re-layouts, away(): return lax.dynamic_index_in_dim(w, 1 - xh, 0, keepdims=False)  3.94 us
  transfers between devices with their start and end apart: 16, of which 9 were waited for; matrix products, arithmetic and copies ran while one was open for 5% of the time, Pallas kernels for 0%

profile of v1, /device:TPU:32, one launch (start us, length us, event | category | flops | bytes accessed | tf_op | source)
XLA Modules:
  0.0 194.6 jit_solution(5866780238136763989)
XLA Ops:
  0.7 0.9 slice_select_fusion.8
  1.6 0.9 slice_select_fusion.4
  2.5 0.9 slice_select_fusion.6
  3.5 1.6 collective-permute-start.1
  6.8 6.1 %collective-permute-done.meta_b = f32[48,32]{1,0:T(8,128)S(1)} collective-permute-done((f32[48,32]{1,0:T(8,128)S(1)}, f32[48,32]{1,0:T(8,128)S(1)}, u32[]{:S(2)}, u32[]{:S(2)}) %collective-permute-start) | collective-permute-done | bytes 6176 | tf_op jit(solution)/shard_map/ppermute | solution.py:157
  13.4 0.7 copy-done.13
  14.2 3.7 %shard_map.147 = (bf16[32,24,1024]{2,1,0:T(8,128)(2,1)}, bf16[96,256]{1,0:T(8,128)(2,1)}, bf16[3,96,256]{2,1,0:T(8,128)(2,1)}) custom-call(s32[3]{0:T(128)} %pad_add_fusion.where_ref, f32[48,32]{1,0:T(8,128)} %copy-done.7, f32[48,32]{1,0:T(8,128)} %copy-done.16, bf16[3,48,1024]{2,1,0:T(8,128)(2,1)} %copy-done.4, bf16[3,48,1024]{2,1,0:T(8,128)(2,1)} %copy-done.13), custom_call_target="tpu_custom_call" | custom-call | flops 1000000000 | bytes 2371596 | tf_op jit(solution)/shard_map/pallas_call | solution.py:35
  17.9 50.6 %all_to_all.10.mine = bf16[32,24,1024]{2,1,0:T(8,128)(2,1)S(1)} all-to-all(bf16[32,24,1024]{2,1,0:T(8,128)(2,1)} %get-tuple-element.14), channel_id=1, replica_groups=mesh['y'=4,'z'=8,'xl'=2,'xh'=2,'core'=2] {'y','z'}, dimensions={0} | all-to-all | bytes 3145728 | tf_op jit(solution)/shard_map/all_to_all | solution.py:165
  68.5 1.8 dynamic-slice_bitcast_fusion
  70.3 3.1 %collective-permute-start.5 = (bf16[192,2048]{1,0:T(8,128)(2,1)S(1)}, bf16[192,2048]{1,0:T(8,128)(2,1)}, u32[]{:S(2)}, u32[]{:S(2)}) collective-permute-start(bf16[192,2048]{1,0:T(8,128)(2,1)S(1)} %dynamic-slice_bitcast_fusion), channel_id=1, source_target_pairs={{0,2},{2,0},{1,3},{3,1},{4,6},{6,4},{5,7},{7,5},{8,10},{10,8},{9,1... | collective-permute-start | bytes 2359304 | tf_op jit(solution)/shard_map/ppermute | solution.py:157
  73.4 1.2 dynamic-slice_bitcast_fusion.1
  75.2 1.0 dynamic-slice_bitcast_fusion.2
  76.2 3.0 %collective-permute-start.3 = (bf16[192,2048]{1,0:T(8,128)(2,1)}, bf16[192,2048]{1,0:T(8,128)(2,1)}, u32[]{:S(2)}, u32[]{:S(2)}) collective-permute-start(bf16[192,2048]{1,0:T(8,128)(2,1)} %dynamic-slice_bitcast_fusion.2), channel_id=1, source_target_pairs={{0,2},{2,0},{1,3},{3,1},{4,6},{6,4},{5,7},{7,5},{8,10},{10,8},{9,1... | collective-permute-start | bytes 2359304 | tf_op jit(solution)/shard_map/ppermute | solution.py:157
  79.7 46.1 %collective-permute-done.6.ad2 = bf16[64,192]{1,0:T(8,128)(2,1)S(1)} collective-permute-done((bf16[64,192]{1,0:T(8,128)(2,1)S(1)}, bf16[64,192]{1,0:T(8,128)(2,1)S(1)}, u32[]{:S(2)}, u32[]{:S(2)}) %collective-permute-start.6) | collective-permute-done | bytes 24608 | tf_op jit(solution)/shard_map/ppermute | solution.py:157
  126.4 11.0 %shard_map.148 = (bf16[256,2048]{1,0:T(8,128)(2,1)}, bf16[256,2048]{1,0:T(8,128)(2,1)}, f32[256,64]{1,0:T(8,128)}, f32[64,192]{1,0:T(8,128)}, f32[64,192]{1,0:T(8,128)}) custom-call(s32[3]{0:T(128)} %pad_add_fusion.where_ref, bf16[32,24,1024]{2,1,0:T(8,128)(2,1)} %copy-done.2, bf16[32,24,1024]{2,1,0:T(8,128)(2,1)} %collective-permute-done.2.theirs, ...), custom_call_target="tpu_custom_call" | custom-call | flops 4000000000 | bytes 13082636 | tf_op jit(solution)/shard_map/pallas_call | solution.py:35
  137.4 1.7 broadcast_select_fusion.5
  140.2 1.9 collective-permute-done.7
  142.0 1.4 add_convert_fusion
  143.4 4.8 %all-to-all-start.1 = ((bf16[32,16,1024]{2,1,0:T(8,128)(2,1)}), bf16[32,16,1024]{2,1,0:T(8,128)(2,1)S(1)}, u32[]{:S(2)}, u32[]{:S(2)}) async-start(bf16[32,16,1024]{2,1,0:T(8,128)(2,1)} %add_convert_fusion), calls=%async_computation.1 | async-start | bytes 2097152 | tf_op jit(solution)/shard_map/all_to_all | solution.py:165
  148.3 1.3 convolution_multiply_fusion
  149.7 1.5 collective-permute-done.13
  151.4 3.1 %collective-permute-start.14 = (f32[64,2048]{1,0:T(8,128)S(1)}, f32[64,2048]{1,0:T(8,128)S(1)}, u32[]{:S(2)}, u32[]{:S(2)}) collective-permute-start(f32[64,2048]{1,0:T(8,128)S(1)} %pad_maximum_fusion.2), channel_id=1, source_target_pairs={{0,2},{2,0},{1,3},{3,1},{4,6},{6,4},{5,7},{7,5},{8,10},{10,8},{9,1... | collective-permute-start | bytes 1572872 | tf_op jit(solution)/shard_map/ppermute | solution.py:157
  155.0 13.3 %collective-permute-done.11 = f32[64,192]{1,0:T(8,128)S(1)} collective-permute-done((f32[64,192]{1,0:T(8,128)S(1)}, f32[64,192]{1,0:T(8,128)S(1)}, u32[]{:S(2)}, u32[]{:S(2)}) %collective-permute-start.11) | collective-permute-done | bytes 49184 | tf_op jit(solution)/shard_map/ppermute | solution.py:157
  168.3 0.7 maximum_bitcast_fusion.4
  169.1 8.0 %all-to-all-done.1.back = bf16[32,16,1024]{2,1,0:T(8,128)(2,1)S(1)} async-done(((bf16[32,16,1024]{2,1,0:T(8,128)(2,1)}), bf16[32,16,1024]{2,1,0:T(8,128)(2,1)S(1)}, u32[]{:S(2)}, u32[]{:S(2)}) %all-to-all-start.1) | async-done | bytes 1048608 | tf_op jit(solution)/shard_map/all_to_all | solution.py:165
  177.1 1.0 copy-done.1
  178.0 2.7 %shard_map.149 = f32[2,96,1024]{2,1,0:T(8,128)} custom-call(bf16[96,256]{1,0:T(8,128)(2,1)} %get-tuple-element.12.member_p, bf16[3,96,256]{2,1,0:T(8,128)(2,1)} %get-tuple-element.13.gates_f, bf16[32,16,1024]{2,1,0:T(8,128)(2,1)} %copy-done.1), custom_call_target="tpu_custom_call" | custom-call | flops 100000000 | bytes 2031616 | tf_op jit(solution)/shard_map/pallas_call | solution.py:35
  180.7 1.4 slice_select_fusion.2
  182.1 3.1 %collective-permute-start.8 = (f32[2,48,512]{2,1,0:T(8,128)S(1)}, f32[2,48,512]{2,1,0:T(8,128)S(1)}, u32[]{:S(2)}, u32[]{:S(2)}) collective-permute-start(f32[2,48,512]{2,1,0:T(8,128)S(1)} %get-tuple-element.30), channel_id=1, source_target_pairs={{0,2},{2,0},{1,3},{3,1},{4,6},{6,4},{5,7},{7,5},{8,10},{10,8},{9,1... | collective-permute-start | bytes 589832 | tf_op jit(solution)/shard_map/ppermute | solution.py:157
  186.4 1.0 pad_maximum_fusion.1
  187.4 4.1 %collective-permute-done.8 = f32[2,48,512]{2,1,0:T(8,128)S(1)} collective-permute-done((f32[2,48,512]{2,1,0:T(8,128)S(1)}, f32[2,48,512]{2,1,0:T(8,128)S(1)}, u32[]{:S(2)}, u32[]{:S(2)}) %collective-permute-start.8) | collective-permute-done | bytes 196640 | tf_op jit(solution)/shard_map/ppermute | solution.py:157
  191.5 2.1 %collective-permute-done.9 = f32[2,48,512]{2,1,0:T(8,128)S(1)} collective-permute-done((f32[2,48,512]{2,1,0:T(8,128)S(1)}, f32[2,48,512]{2,1,0:T(8,128)S(1)}, u32[]{:S(2)}, u32[]{:S(2)}) %collective-permute-start.9) | collective-permute-done | bytes 196640 | tf_op jit(solution)/shard_map/ppermute | solution.py:157
  (75 shorter events, 8.1 us)
Async XLA Ops:
  0.6 4.4 %copy-start.11 = (s32[48,8]{0,1:T(8,128)S(1)}, s32[48,8]{0,1:T(8,128)}, u32[]{:S(2)}) copy-start(s32[48,8]{0,1:T(8,128)} %param.15) | copy-start | bytes 4612
  0.6 4.4 %copy-start.12 = (s32[48,8]{0,1:T(8,128)S(1)}, s32[48,8]{0,1:T(8,128)}, u32[]{:S(2)}) copy-start(s32[48,8]{0,1:T(8,128)} %param.17) | copy-start | bytes 4612
  0.7 4.6 %copy-start.9 = (f32[48,8]{0,1:T(8,128)S(1)}, f32[48,8]{0,1:T(8,128)}, u32[]{:S(2)}) copy-start(f32[48,8]{0,1:T(8,128)} %param.16) | copy-start | bytes 4612
  0.7 4.6 %copy-start.10 = (f32[48,8]{0,1:T(8,128)S(1)}, f32[48,8]{0,1:T(8,128)}, u32[]{:S(2)}) copy-start(f32[48,8]{0,1:T(8,128)} %param.18) | copy-start | bytes 4612
  3.5 9.4 %copy-start.4 = (bf16[3,48,1024]{2,1,0:T(8,128)(2,1)}, bf16[3,48,1024]{2,1,0:T(8,128)(2,1)S(1)}, u32[]{:S(2)}) copy-start(bf16[3,48,1024]{2,1,0:T(8,128)(2,1)S(1)} %pad_maximum_fusion.3.own) | copy-start | bytes 884740
  3.5 9.4 %collective-permute-start.1 = (bf16[3,48,1024]{2,1,0:T(8,128)(2,1)S(1)}, bf16[3,48,1024]{2,1,0:T(8,128)(2,1)S(1)}, u32[]{:S(2)}, u32[]{:S(2)}) collective-permute-start(bf16[3,48,1024]{2,1,0:T(8,128)(2,1)S(1)} %pad_maximum_fusion.3.own), channel_id=1, source_target_pairs={{0,4},{4,0},{1,5},{5,1},{2,6},{6,2},{3,7},{7,3},{8,12},{12,8},{9,1... | collective-permute-start | bytes 884744 | tf_op jit(solution)/shard_map/ppermute | solution.py:157
  5.5 7.4 %copy-start.7 = (f32[48,32]{1,0:T(8,128)}, f32[48,32]{1,0:T(8,128)S(1)}, u32[]{:S(2)}) copy-start(f32[48,32]{1,0:T(8,128)S(1)} %pad_maximum_fusion.4.meta_a) | copy-start | bytes 18436
  5.5 7.3 %collective-permute-start = (f32[48,32]{1,0:T(8,128)S(1)}, f32[48,32]{1,0:T(8,128)S(1)}, u32[]{:S(2)}, u32[]{:S(2)}) collective-permute-start(f32[48,32]{1,0:T(8,128)S(1)} %pad_maximum_fusion.4.meta_a), channel_id=1, source_target_pairs={{0,4},{4,0},{1,5},{5,1},{2,6},{6,2},{3,7},{7,3},{8,12},{12,8},{9,1... | collective-permute-start | bytes 18440 | tf_op jit(solution)/shard_map/ppermute | solution.py:157
  13.4 0.7 copy-start.13
  68.5 6.1 %copy-start.2 = (bf16[32,24,1024]{2,1,0:T(8,128)(2,1)}, bf16[32,24,1024]{2,1,0:T(8,128)(2,1)S(1)}, u32[]{:S(2)}) copy-start(bf16[32,24,1024]{2,1,0:T(8,128)(2,1)S(1)} %all_to_all.10.mine) | copy-start | bytes 4718596
  68.5 57.3 %collective-permute-start.2 = (bf16[32,24,1024]{2,1,0:T(8,128)(2,1)S(1)}, bf16[32,24,1024]{2,1,0:T(8,128)(2,1)}, u32[]{:S(2)}, u32[]{:S(2)}) collective-permute-start(bf16[32,24,1024]{2,1,0:T(8,128)(2,1)S(1)} %all_to_all.10.mine), channel_id=1, source_target_pairs={{0,1},{1,0},{2,3},{3,2},{4,5},{5,4},{6,7},{7,6},{8,9},{9,8},{10,11... | collective-permute-start | bytes 4718600 | tf_op jit(solution)/shard_map/ppermute | solution.py:157
  68.5 6.7 %copy-start.3 = (bf16[2,2048,192]{1,2,0:T(8,128)(2,1)S(1)}, bf16[2,2048,192]{1,2,0:T(8,128)(2,1)}, u32[]{:S(2)}) copy-start(bf16[2,2048,192]{1,2,0:T(8,128)(2,1)} %param.19) | copy-start | bytes 4718596
  70.3 8.9 %copy-start.8 = (bf16[2,192,64]{1,2,0:T(8,128)(2,1)S(1)}, bf16[2,192,64]{1,2,0:T(8,128)(2,1)}, u32[]{:S(2)}) copy-start(bf16[2,192,64]{1,2,0:T(8,128)(2,1)} %param.22) | copy-start | bytes 147460
  70.3 55.5 %collective-permute-start.5 = (bf16[192,2048]{1,0:T(8,128)(2,1)S(1)}, bf16[192,2048]{1,0:T(8,128)(2,1)}, u32[]{:S(2)}, u32[]{:S(2)}) collective-permute-start(bf16[192,2048]{1,0:T(8,128)(2,1)S(1)} %dynamic-slice_bitcast_fusion), channel_id=1, source_target_pairs={{0,2},{2,0},{1,3},{3,1},{4,6},{6,4},{5,7},{7,5},{8,10},{10,8},{9,1... | collective-permute-start | bytes 2359304 | tf_op jit(solution)/shard_map/ppermute | solution.py:157
  74.6 51.2 %collective-permute-start.4 = (bf16[192,2048]{1,0:T(8,128)(2,1)S(1)}, bf16[192,2048]{1,0:T(8,128)(2,1)}, u32[]{:S(2)}, u32[]{:S(2)}) collective-permute-start(bf16[192,2048]{1,0:T(8,128)(2,1)S(1)} %dynamic-slice_bitcast_fusion.1), channel_id=1, source_target_pairs={{0,2},{2,0},{1,3},{3,1},{4,6},{6,4},{5,7},{7,5},{8,10},{10,8},{9,1... | collective-permute-start | bytes 2359304 | tf_op jit(solution)/shard_map/ppermute | solution.py:157
  76.2 49.6 %collective-permute-start.3 = (bf16[192,2048]{1,0:T(8,128)(2,1)}, bf16[192,2048]{1,0:T(8,128)(2,1)}, u32[]{:S(2)}, u32[]{:S(2)}) collective-permute-start(bf16[192,2048]{1,0:T(8,128)(2,1)} %dynamic-slice_bitcast_fusion.2), channel_id=1, source_target_pairs={{0,2},{2,0},{1,3},{3,1},{4,6},{6,4},{5,7},{7,5},{8,10},{10,8},{9,1... | collective-permute-start | bytes 2359304 | tf_op jit(solution)/shard_map/ppermute | solution.py:157
  79.2 46.6 %collective-permute-start.6 = (bf16[64,192]{1,0:T(8,128)(2,1)S(1)}, bf16[64,192]{1,0:T(8,128)(2,1)S(1)}, u32[]{:S(2)}, u32[]{:S(2)}) collective-permute-start(bf16[64,192]{1,0:T(8,128)(2,1)S(1)} %dynamic-slice_bitcast_fusion.3), channel_id=1, source_target_pairs={{0,2},{2,0},{1,3},{3,1},{4,6},{6,4},{5,7},{7,5},{8,10},{10,8},{9,1... | collective-permute-start | bytes 73736 | tf_op jit(solution)/shard_map/ppermute | solution.py:157
  125.8 0.6 copy-start.15
  139.1 0.9 copy-start.5
  139.3 2.7 %collective-permute-start.7 = (bf16[32,16,1024]{2,1,0:T(8,128)(2,1)S(1)}, bf16[32,16,1024]{2,1,0:T(8,128)(2,1)S(1)}, u32[]{:S(2)}, u32[]{:S(2)}) collective-permute-start(bf16[32,16,1024]{2,1,0:T(8,128)(2,1)S(1)} %pad_maximum_fusion), channel_id=1, source_target_pairs={{0,1},{1,0},{2,3},{3,2},{4,5},{5,4},{6,7},{7,6},{8,9},{9,8},{10,11... | collective-permute-start | bytes 3145736 | tf_op jit(solution)/shard_map/ppermute | solution.py:157
  140.0 8.3 %collective-permute-start.12 = (f32[256,64]{1,0:T(8,128)S(1)}, f32[256,64]{1,0:T(8,128)S(1)}, u32[]{:S(2)}, u32[]{:S(2)}) collective-permute-start(f32[256,64]{1,0:T(8,128)S(1)} %copy-done.5), channel_id=1, source_target_pairs={{0,1},{1,0},{2,3},{3,2},{4,5},{5,4},{6,7},{7,6},{8,9},{9,8},{10,11... | collective-permute-start | bytes 196616 | tf_op jit(solution)/shard_map/ppermute | solution.py:157
  143.4 33.6 %all-to-all-start.1 = ((bf16[32,16,1024]{2,1,0:T(8,128)(2,1)}), bf16[32,16,1024]{2,1,0:T(8,128)(2,1)S(1)}, u32[]{:S(2)}, u32[]{:S(2)}) async-start(bf16[32,16,1024]{2,1,0:T(8,128)(2,1)} %add_convert_fusion), calls=%async_computation.1 | async-start | bytes 2097152 | tf_op jit(solution)/shard_map/all_to_all | solution.py:165
  149.6 4.9 %copy-start.14 = (f32[64,192]{1,0:T(8,128)S(1)}, f32[64,192]{1,0:T(8,128)}, u32[]{:S(2)}) copy-start(f32[64,192]{1,0:T(8,128)} %get-tuple-element.18) | copy-start | bytes 147460
  149.6 18.7 %copy-start.6 = (f32[64,192]{1,0:T(8,128)S(1)}, f32[64,192]{1,0:T(8,128)}, u32[]{:S(2)}) copy-start(f32[64,192]{1,0:T(8,128)} %get-tuple-element.17) | copy-start | bytes 147460
  149.6 1.6 collective-permute-start.13
  151.4 17.6 %collective-permute-start.14 = (f32[64,2048]{1,0:T(8,128)S(1)}, f32[64,2048]{1,0:T(8,128)S(1)}, u32[]{:S(2)}, u32[]{:S(2)}) collective-permute-start(f32[64,2048]{1,0:T(8,128)S(1)} %pad_maximum_fusion.2), channel_id=1, source_target_pairs={{0,2},{2,0},{1,3},{3,1},{4,6},{6,4},{5,7},{7,5},{8,10},{10,8},{9,1... | collective-permute-start | bytes 1572872 | tf_op jit(solution)/shard_map/ppermute | solution.py:157
  154.5 13.8 %collective-permute-start.11 = (f32[64,192]{1,0:T(8,128)S(1)}, f32[64,192]{1,0:T(8,128)S(1)}, u32[]{:S(2)}, u32[]{:S(2)}) collective-permute-start(f32[64,192]{1,0:T(8,128)S(1)} %copy-done.14), channel_id=1, source_target_pairs={{0,2},{2,0},{1,3},{3,1},{4,6},{6,4},{5,7},{7,5},{8,10},{10,8},{9,1... | collective-permute-start | bytes 147464 | tf_op jit(solution)/shard_map/ppermute | solution.py:157
  177.1 1.0 copy-start.1
  180.7 13.2 %copy-start = (f32[2,96,1024]{2,1,0:T(8,128)S(1)}, f32[2,96,1024]{2,1,0:T(8,128)}, u32[]{:S(2)}) copy-start(f32[2,96,1024]{2,1,0:T(8,128)} %shard_map.149) | copy-start | bytes 2359300
  182.1 9.4 %collective-permute-start.8 = (f32[2,48,512]{2,1,0:T(8,128)S(1)}, f32[2,48,512]{2,1,0:T(8,128)S(1)}, u32[]{:S(2)}, u32[]{:S(2)}) collective-permute-start(f32[2,48,512]{2,1,0:T(8,128)S(1)} %get-tuple-element.30), channel_id=1, source_target_pairs={{0,2},{2,0},{1,3},{3,1},{4,6},{6,4},{5,7},{7,5},{8,10},{10,8},{9,1... | collective-permute-start | bytes 589832 | tf_op jit(solution)/shard_map/ppermute | solution.py:157
  185.2 8.4 %collective-permute-start.9 = (f32[2,48,512]{2,1,0:T(8,128)S(1)}, f32[2,48,512]{2,1,0:T(8,128)S(1)}, u32[]{:S(2)}, u32[]{:S(2)}) collective-permute-start(f32[2,48,512]{2,1,0:T(8,128)S(1)} %get-tuple-element.31), channel_id=1, source_target_pairs={{0,4},{4,0},{1,5},{5,1},{2,6},{6,2},{3,7},{7,3},{8,12},{12,8},{9,1... | collective-permute-start | bytes 589832 | tf_op jit(solution)/shard_map/ppermute | solution.py:157
  185.8 8.1 %collective-permute-start.10 = (f32[2,48,512]{2,1,0:T(8,128)S(1)}, f32[2,48,512]{2,1,0:T(8,128)S(1)}, u32[]{:S(2)}, u32[]{:S(2)}) collective-permute-start(f32[2,48,512]{2,1,0:T(8,128)S(1)} %get-tuple-element.32), channel_id=1, source_target_pairs={{0,6},{2,4},{4,2},{6,0},{1,7},{3,5},{5,3},{7,1},{8,14},{10,12},{12... | collective-permute-start | bytes 589832 | tf_op jit(solution)/shard_map/ppermute | solution.py:161
  (1 other events, 0.6 us)

commit v2 on v1

v2 whole, which is shorter than its diff:
```python
import jax
import jax.numpy as jnp
from jax import lax
from jax.experimental import pallas as pl
from jax.experimental.pallas import tpu as pltpu
from jax.sharding import Mesh, PartitionSpec as P

BF = jnp.bfloat16
F32 = jnp.float32
SCALE = 2.0
SLOT = 4
PEERS = 32
TOK = 48
Q = 512
ROWS = 256
FULL = 67043328


def nt(a, b):
    return lax.dot_general(a, b, (((1,), (1,)), ((), ())), preferred_element_type=F32)


def nn(a, b):
    return lax.dot_general(a, b, (((1,), (0,)), ((), ())), preferred_element_type=F32)


def tn(a, b):
    return lax.dot_general(a, b, (((0,), (0,)), ((), ())), preferred_element_type=F32)


def vmem_call(body, outs, args, flops=0, mib=16):
    specs = [pl.BlockSpec(memory_space=pltpu.SMEM)]
    specs += [pl.BlockSpec(memory_space=pltpu.VMEM)] * (len(args) - 1)
    moved = sum(a.size * a.dtype.itemsize for a in args)
    moved += sum(o.size * o.dtype.itemsize for o in outs)
    return pl.pallas_call(
        body,
        out_shape=outs,
        in_specs=specs,
        out_specs=[pl.BlockSpec(memory_space=pltpu.VMEM)] * len(outs),
        compiler_params=pltpu.CompilerParams(vmem_limit_bytes=mib << 20),
        cost_estimate=pl.CostEstimate(flops=flops, bytes_accessed=moved, transcendentals=0),
    )(*args)


def sds(shape, dtype):
    return jax.ShapeDtypeStruct(shape, dtype)


def quarter(h, core):
    return pl.ds(pl.multiple_of((2 * h + core) * Q, Q), Q)


def halves_body(where_ref, policy, frozen, cotangent, own, sems):
    copies = []
    for n, ref in enumerate((policy, frozen, cotangent)):
        for h in range(2):
            copies.append(pltpu.make_async_copy(
                ref.at[:, quarter(h, where_ref[1])], own.at[n, :, h * Q : (h + 1) * Q], sems.at[n, h]
            ))
    for copy in copies:
        copy.start()
    for copy in copies:
        copy.wait()


def bundle_body(where_ref, wg, wu, wd, out, sems):
    away = 1 - where_ref[2]
    copies = [
        pltpu.make_async_copy(ref.at[away], out.at[n], sems.at[n]) for n, ref in enumerate((wg, wu, wd))
    ]
    for copy in copies:
        copy.start()
    for copy in copies:
        copy.wait()


def tables(where_ref, meta_a, meta_b, at):
    cols = 2 * TOK
    meta = jnp.concatenate([meta_a[at : at + 16], meta_b[at : at + 16]], axis=1)
    col = lax.broadcasted_iota(jnp.int32, (ROWS, cols), 1)
    row = lax.broadcasted_iota(jnp.int32, (ROWS, cols), 0)
    expert = (4 * (row // 8) + where_ref[0]).astype(F32)
    named = jnp.zeros((ROWS, cols), F32)
    gate = jnp.zeros((ROWS, cols), F32)
    for k in range(8):
        match = meta[k : k + 1] == expert
        named = named + jnp.where(match, 1.0, 0.0)
        gate = gate + jnp.where(match, meta[8 + k : 9 + k], 0.0)
    r0 = lax.broadcasted_iota(jnp.int32, (cols, cols), 0)
    r1 = lax.broadcasted_iota(jnp.int32, (cols, cols), 1)
    earlier = jnp.where((r0 < r1) & ((r0 < TOK) == (r1 < TOK)), 1.0, 0.0)
    position = nn(named.astype(BF), earlier.astype(BF))
    here = (position == (row % SLOT).astype(F32)) & (((row // SLOT) % 2 == 1) == (col >= TOK))
    return jnp.where(here, named, 0.0), jnp.where(here, gate, 0.0)


def pieces(x):
    hi = x.astype(BF)
    rest = x - hi.astype(F32)
    mid = rest.astype(BF)
    return hi, mid, (rest - mid.astype(F32)).astype(BF)


def select_body(where_ref, meta_a, meta_b, own, other, sent, both, sems):
    copies = [
        pltpu.make_async_copy(ref, both.at[:, TOK * n : TOK * n + TOK, :], sems.at[n])
        for n, ref in enumerate((own, other))
    ]
    for copy in copies:
        copy.start()
    member_p, gate_p = tables(where_ref, meta_a, meta_b, 0)
    member_f, _ = tables(where_ref, meta_a, meta_b, 16)
    for copy in copies:
        copy.wait()
    for i, member in enumerate((member_p, member_f, member_p)):
        picked = nn(member.astype(BF), both[i])
        if i == 2:
            picked = picked * jnp.sum(gate_p, axis=1, keepdims=True)
        sent[:, 8 * i : 8 * i + 8, :] = picked.astype(BF).reshape(PEERS, 8, 2 * Q)


def home_body(where_ref, meta_a, meta_b, member_p, gates_f):
    member, _ = tables(where_ref, meta_a, meta_b, 0)
    member_p[...] = member.T.astype(BF)
    _, gate = tables(where_ref, meta_a, meta_b, 16)
    hi, mid, low = pieces(gate.T)
    gates_f[0] = hi
    gates_f[1] = mid
    gates_f[2] = low


def contract(where_ref, mine, theirs, i, weight, index):
    total = None
    for ref, core in ((mine, where_ref[1]), (theirs, 1 - where_ref[1])):
        for h in range(2):
            x = ref[:, 8 * i : 8 * i + 8, h * Q : (h + 1) * Q].reshape(ROWS, Q)
            at = quarter(h, core)
            part = nt(x, weight[:, at] if index is None else weight[index, :, at])
            total = part if total is None else total + part
    return total


def main_body(
    where_ref, mine, theirs, wg, wu, wd, ad, au, w2, ad2, give, keep, inner, down_grad, down_grad2
):
    e = where_ref[2]
    weights = ((wg.at[e], wu.at[e], wd.at[e]), (w2.at[0], w2.at[1], w2.at[2]))
    adapters = (ad[e], ad2[...])

    def dot(i, weight):
        return contract(where_ref, mine, theirs, i, weight, None)

    def expand(pairs, i):
        for out, core in ((give, 1 - where_ref[1]), (keep, where_ref[1])):
            for h in range(2):
                at = quarter(h, core)
                total = None
                for x, w in pairs:
                    part = nn(x, w[:, at])
                    total = part if total is None else total + part
                out[:, 8 * i : 8 * i + 8, h * Q : (h + 1) * Q] = total.astype(BF).reshape(PEERS, 8, Q)

    pairs = []
    for g, u, d in weights:
        gate_pre = dot(1, g)
        pairs.append(((gate_pre * jax.nn.sigmoid(gate_pre) * dot(1, u)).astype(BF), d))
    expand(pairs, 1)
    inner_grad = (SCALE * dot(2, au.at[e])).astype(BF)
    pairs = []
    total = None
    for n, (g, u, d) in enumerate(weights):
        gate_pre = dot(0, g)
        up_pre = dot(0, u)
        sigmoid = jax.nn.sigmoid(gate_pre)
        activated = gate_pre * sigmoid
        hidden = (activated * up_pre).astype(BF)
        part = nt(hidden, adapters[n])
        total = part if total is None else total + part
        (down_grad, down_grad2)[n][...] = tn(inner_grad, hidden)
        hidden_grad = dot(2, d) + nn(inner_grad, adapters[n])
        slope = up_pre * sigmoid * (1.0 + gate_pre * (1.0 - sigmoid))
        pairs.append(((hidden_grad * slope).astype(BF), g))
        pairs.append(((hidden_grad * activated).astype(BF), u))
    inner[...] = total
    expand(pairs, 0)


def up_body(where_ref, inner_a, inner_b, cot, out):
    inner = (inner_a[...] + inner_b[...]).astype(BF)
    out[...] = SCALE * tn(inner, cot[:, 16:24, :].reshape(ROWS, 2 * Q))


def combine_body(where_ref, member, gates, back, own, to_xh, to_xl, to_both):
    for at, near, far in ((where_ref[2], own, to_xl), (1 - where_ref[2], to_xh, to_both)):
        lanes = pl.ds(pl.multiple_of(at * Q, Q), Q)
        grads = back[:, 0:8, lanes].reshape(ROWS, Q)
        frozen = back[:, 8:16, lanes].reshape(ROWS, Q)
        frozen = nn(gates[2], frozen) + nn(gates[1], frozen) + nn(gates[0], frozen)
        grads = nn(member[...], grads)
        for n, total in enumerate((frozen, grads)):
            near[n] = total[:TOK].astype(near.dtype)
            far[n] = total[TOK:].astype(far.dtype)


def swap(x, axis):
    return lax.ppermute(x, axis, [(0, 1), (1, 0)])


def swap_both(x):
    return lax.ppermute(x, ("xl", "xh"), [(i, 3 - i) for i in range(4)])


def exchange(x):
    return lax.all_to_all(x, ("y", "z"), split_axis=0, concat_axis=0, tiled=True)


def pick(c, a, b):
    return jnp.where(c == 0, a, b)


def step(
    policy_tokens, policy_cotangent, frozen_tokens, policy_route, policy_gates,
    frozen_route, frozen_gates, w_gate, w_up, w_down, adapter_down, adapter_up,
):
    c, xh, xl = lax.axis_index("core"), lax.axis_index("xh"), lax.axis_index("xl")
    where = jnp.stack([2 * xl + xh, c, xh]).astype(jnp.int32)
    wg, wu = w_gate.swapaxes(1, 2), w_up.swapaxes(1, 2)
    ad = adapter_down.swapaxes(1, 2)

    def away(w):
        return lax.dynamic_index_in_dim(w, 1 - xh, 0, keepdims=False)

    meta = jnp.concatenate(
        [policy_route.T.astype(F32), policy_gates.T, frozen_route.T.astype(F32), frozen_gates.T]
    )
    hbm = pl.BlockSpec(memory_space=pltpu.HBM)
    own = pl.pallas_call(
        halves_body,
        name="halves",
        out_shape=sds((3, TOK, 2 * Q), BF),
        in_specs=[pl.BlockSpec(memory_space=pltpu.SMEM), hbm, hbm, hbm],
        out_specs=pl.BlockSpec(memory_space=pltpu.VMEM),
        scratch_shapes=[pltpu.SemaphoreType.DMA((3, 2))],
        compiler_params=pltpu.CompilerParams(vmem_limit_bytes=FULL),
    )(where, policy_tokens, frozen_tokens, policy_cotangent)
    other = swap(own, "xl")
    meta_b = swap(meta, "xl")
    mine_w = pl.pallas_call(
        bundle_body,
        name="bundle",
        out_shape=sds((3, 192, 4 * Q), BF),
        in_specs=[pl.BlockSpec(memory_space=pltpu.SMEM), hbm, hbm, hbm],
        out_specs=pl.BlockSpec(memory_space=pltpu.VMEM),
        scratch_shapes=[pltpu.SemaphoreType.DMA((3,))],
        compiler_params=pltpu.CompilerParams(vmem_limit_bytes=FULL),
    )(where, wg, wu, w_down)
    w2 = swap(mine_w, "xh")
    ad2 = swap(away(ad), "xh")

    vmem = pl.BlockSpec(memory_space=pltpu.VMEM)
    sent = pl.pallas_call(
        select_body,
        name="select",
        out_shape=sds((PEERS, 24, 2 * Q), BF),
        in_specs=[pl.BlockSpec(memory_space=pltpu.SMEM), vmem, vmem, hbm, hbm],
        out_specs=vmem,
        scratch_shapes=[pltpu.VMEM((3, 2 * TOK, 2 * Q), BF), pltpu.SemaphoreType.DMA((2,))],
        compiler_params=pltpu.CompilerParams(vmem_limit_bytes=FULL),
    )(where, meta, meta_b, own, other)
    member_p, gates_f = vmem_call(
        home_body, [sds((2 * TOK, ROWS), BF), sds((3, 2 * TOK, ROWS), BF)],
        [where, meta, meta_b], flops=10**8, mib=8,
    )
    mine = exchange(sent)
    theirs = swap(mine, "core")
    wide = sds((PEERS, 16, 2 * Q), BF)
    give, keep, inner, down_grad, down_grad2 = vmem_call(
        main_body,
        [wide, wide, sds((ROWS, 64), F32), sds((64, 192), F32), sds((64, 192), F32)],
        [where, mine, theirs, wg, wu, w_down, ad, adapter_up, w2, ad2], flops=4 * 10**9, mib=28,
    )
    total = (keep.astype(F32) + swap(give, "core").astype(F32)).astype(BF)
    back = exchange(total)
    own, to_xh, to_xl, to_both = vmem_call(
        combine_body, [sds((2, TOK, Q), F32)] + [sds((2, TOK, Q), BF)] * 3,
        [where, member_p, gates_f, back], flops=10**8, mib=8,
    )
    from_xh = swap(to_xh, "xh")
    from_xl = swap(to_xl, "xl")
    from_both = swap_both(to_both)
    outs = own + from_xh.astype(F32) + from_xl.astype(F32) + from_both.astype(F32)
    frozen_out, input_grad = outs[0].astype(BF), outs[1].astype(BF)

    (up_half,) = vmem_call(
        up_body, [sds((64, 2 * Q), F32)], [where, inner, swap(inner, "core"), mine],
        flops=10**8, mib=6,
    )
    up_other = swap(up_half, "core")
    lo, hi = pick(c, up_half, up_other), pick(c, up_other, up_half)
    up_own = jnp.concatenate([lo[:, :Q], hi[:, :Q], lo[:, Q:], hi[:, Q:]], axis=1)
    up_away = swap(up_own, "xh")
    up_grad = jnp.stack([pick(xh, up_own, up_away), pick(xh, up_away, up_own)])
    down_away = swap(down_grad2, "xh")
    down = jnp.stack([pick(xh, down_grad, down_away), pick(xh, down_away, down_grad)]).swapaxes(1, 2)
    return frozen_out, input_grad, down, up_grad


def solution(mesh):
    fine = Mesh(mesh.devices.reshape(4, 8, 2, 2, 2), ("y", "z", "xl", "xh", "core"))
    ex, pr = ("y", "z", "xl"), ("xh", "core")
    in_specs = (P(ex, None),) * 7 + (
        P(ex, None, pr), P(ex, None, pr), P(ex, pr, None), P(ex, pr, None), P(ex, None, None),
    )
    out_specs = (P(ex, pr), P(ex, pr), P(ex, pr, None), P(ex, None, None))
    return jax.shard_map(step, mesh=fine, in_specs=in_specs, out_specs=out_specs, check_vma=False)
```

time: 195 us -> 158 us (0.81)
  blocking collectives: 50.6 us -> 0 us
  starting transfers between devices: 22.3 us -> 38.3 us
  other arithmetic: 10.2 us -> 5.32 us
  Pallas kernels: 17.4 us -> 21.6 us
    all_to_all x1 -> x0, blocking collectives: 50.6 us -> none  [exchange(): lax.all_to_all(x, ('y', 'z'), split_axis=0, concat_axis=0, tiled=True)]
    ppermute x14 -> x12, waiting for transfers between devices: 75.1 us -> 37.8 us  [swap(): return lax.ppermute(x, axis, [(0, 1), (1, 0)])]
    all_to_all x1 -> x2, waiting for transfers between devices: 7.96 us -> 42.7 us  [exchange(): lax.all_to_all(x, ('y', 'z'), split_axis=0, concat_axis=0, tiled=True)]
    all_to_all x1 -> x2, starting transfers between devices: 4.84 us -> 21.2 us  [exchange(): lax.all_to_all(x, ('y', 'z'), split_axis=0, concat_axis=0, tiled=True)]
    pallas_call x0 -> x3, Pallas kernels: none -> 9.62 us  [the longest x1 3.71 us: step(): pl.pallas_call(bundle_body, name='bundle', out_shape=sds((3, 192, 4 * Q),...]
    select_n x6 -> x1, other arithmetic: 5.76 us -> 0.05 us  [pick(): return jnp.where(c == 0, a, b)]
    pallas_call x3 -> x4, Pallas kernels: 17.4 us -> 11.9 us  [vmem_call(): pl.pallas_call(body, out_shape=outs, in_specs=specs, out_specs=[pl.BlockS...]
    unnamed x36 -> x22, local copies, waits for them, and re-layouts: 3.71 us -> 7.93 us
  transfers between devices with their start and end apart: 16 -> 15, of which waited for: 9 -> 9; matrix products, arithmetic and copies ran while one was open for 5% -> 3% of each run, Pallas kernels for 0% -> 4%
where the time goes in v2:
time: 158 us; the launch traced here: 157 us
  waiting for transfers between devices  81.9 us (52%)
  starting transfers between devices  38.3 us (24%)
  Pallas kernels  21.6 us (14%)
  local copies, waits for them, and re-layouts  9.37 us (6%)
  other arithmetic  5.32 us (3%)
    all_to_all x2, waiting for transfers between devices, exchange(): lax.all_to_all(x, ('y', 'z'), split_axis=0, concat_axis=0, tiled=True)  42.7 us
    ppermute x12, waiting for transfers between devices, swap(): return lax.ppermute(x, axis, [(0, 1), (1, 0)])  37.8 us
    all_to_all x2, starting transfers between devices, exchange(): lax.all_to_all(x, ('y', 'z'), split_axis=0, concat_axis=0, tiled=True)  21.2 us
    ppermute x12, starting transfers between devices, swap(): return lax.ppermute(x, axis, [(0, 1), (1, 0)])  16.6 us
    pallas_call x4, Pallas kernels, vmem_call(): pl.pallas_call(body, out_shape=outs, in_specs=specs, out_specs=[pl.BlockS...  11.9 us
    unnamed x22, local copies, waits for them, and re-layouts  7.93 us
    pallas_call x1, Pallas kernels, step(): pl.pallas_call(bundle_body, name='bundle', out_shape=sds((3, 192, 4 * Q),...  3.71 us
    pallas_call x1, Pallas kernels, step(): pl.pallas_call(select_body, name='select', out_shape=sds((PEERS, 24, 2 *...  3.56 us
  transfers between devices with their start and end apart: 15, of which 9 were waited for; matrix products, arithmetic and copies ran while one was open for 3% of the time, Pallas kernels for 4%

profile of v2, /device:TPU:32, one launch (start us, length us, event | category | flops | bytes accessed | tf_op | source)
XLA Modules:
  0.0 157.3 jit_solution(869006637841126090)
XLA Ops:
  1.2 2.3 %halves.1.own = bf16[3,48,1024]{2,1,0:T(8,128)(2,1)} custom-call(s32[3]{0:T(128)} %pad_add_fusion.where_ref, bf16[48,2048]{1,0:T(8,128)(2,1)} %policy.1, bf16[48,2048]{1,0:T(8,128)(2,1)} %frozen.1, bf16[48,2048]{1,0:T(8,128)(2,1)} %cotangent.1), custom_call_target="tpu_custom_call" | custom-call | tf_op jit(solution)/shard_map/halves/pallas_call | solution.py:238
  3.6 1.6 %collective-permute-start.1 = (bf16[3,48,1024]{2,1,0:T(8,128)(2,1)}, bf16[3,48,1024]{2,1,0:T(8,128)(2,1)}, u32[]{:S(2)}, u32[]{:S(2)}) collective-permute-start(bf16[3,48,1024]{2,1,0:T(8,128)(2,1)} %halves.1.own), channel_id=1, source_target_pairs={{0,4},{4,0},{1,5},{5,1},{2,6},{6,2},{3,7},{7,3},{8,12},{12,8},{9,1... | collective-permute-start | bytes 884744 | tf_op jit(solution)/shard_map/ppermute | solution.py:207
  5.9 0.7 pad_maximum_fusion.2.meta_a
  7.7 5.3 %collective-permute-done.meta_b = f32[32,48]{1,0:T(8,128)S(1)} collective-permute-done((f32[32,48]{1,0:T(8,128)S(1)}, f32[32,48]{1,0:T(8,128)S(1)}, u32[]{:S(2)}, u32[]{:S(2)}) %collective-permute-start) | collective-permute-done | bytes 6176 | tf_op jit(solution)/shard_map/ppermute | solution.py:207
  13.6 3.6 %select.1 = bf16[32,24,1024]{2,1,0:T(8,128)(2,1)} custom-call(s32[3]{0:T(128)} %pad_add_fusion.where_ref, f32[32,48]{1,0:T(8,128)} %copy-done.3, f32[32,48]{1,0:T(8,128)} %copy-done.7, bf16[3,48,1024]{2,1,0:T(8,128)(2,1)} %halves.1.own, bf16[3,48,1024]{2,1,0:T(8,128)(2,1)} %collective-permute-done.1.other), custom_call_target="tpu_custom_call" | custom-call | tf_op jit(solution)/shard_map/select/pallas_call | solution.py:262
  17.2 11.4 %all-to-all-start = ((bf16[32,24,1024]{2,1,0:T(8,128)(2,1)}), bf16[32,24,1024]{2,1,0:T(8,128)(2,1)}, u32[]{:S(2)}, u32[]{:S(2)}) async-start(bf16[32,24,1024]{2,1,0:T(8,128)(2,1)} %select.1), calls=%async_computation | async-start | bytes 3145728 | tf_op jit(solution)/shard_map/all_to_all | solution.py:215
  28.6 3.7 %bundle.1 = bf16[3,192,2048]{2,1,0:T(8,128)(2,1)} custom-call(s32[3]{0:T(128)} %pad_add_fusion.where_ref, bf16[2,192,2048]{2,1,0:T(8,128)(2,1)} %bitcast.30, bf16[2,192,2048]{2,1,0:T(8,128)(2,1)} %bitcast.32, bf16[2,192,2048]{2,1,0:T(8,128)(2,1)} %wd.3), custom_call_target="tpu_custom_call" | custom-call | tf_op jit(solution)/shard_map/bundle/pallas_call | solution.py:249
  32.3 3.1 %collective-permute-start.3 = (bf16[3,192,2048]{2,1,0:T(8,128)(2,1)}, bf16[3,192,2048]{2,1,0:T(8,128)(2,1)S(1)}, u32[]{:S(2)}, u32[]{:S(2)}) collective-permute-start(bf16[3,192,2048]{2,1,0:T(8,128)(2,1)} %bundle.1), channel_id=1, source_target_pairs={{0,2},{2,0},{1,3},{3,1},{4,6},{6,4},{5,7},{7,5},{8,10},{10,8},{9,1... | collective-permute-start | bytes 7077896 | tf_op jit(solution)/shard_map/ppermute | solution.py:207
  35.4 31.9 %all-to-all-done.mine.cot = bf16[32,24,1024]{2,1,0:T(8,128)(2,1)} async-done(((bf16[32,24,1024]{2,1,0:T(8,128)(2,1)}), bf16[32,24,1024]{2,1,0:T(8,128)(2,1)}, u32[]{:S(2)}, u32[]{:S(2)}) %all-to-all-start) | async-done | bytes 1572896 | tf_op jit(solution)/shard_map/all_to_all | solution.py:215
  67.3 0.8 dynamic-slice_bitcast_fusion
  68.1 3.0 %collective-permute-start.4 = (bf16[64,192]{1,0:T(8,128)(2,1)S(1)}, bf16[64,192]{1,0:T(8,128)(2,1)S(1)}, u32[]{:S(2)}, u32[]{:S(2)}) collective-permute-start(bf16[64,192]{1,0:T(8,128)(2,1)S(1)} %dynamic-slice_bitcast_fusion), channel_id=1, source_target_pairs={{0,2},{2,0},{1,3},{3,1},{4,6},{6,4},{5,7},{7,5},{8,10},{10,8},{9,1... | collective-permute-start | bytes 73736 | tf_op jit(solution)/shard_map/ppermute | solution.py:207
  71.1 15.4 %collective-permute-done.4.ad2 = bf16[64,192]{1,0:T(8,128)(2,1)S(1)} collective-permute-done((bf16[64,192]{1,0:T(8,128)(2,1)S(1)}, bf16[64,192]{1,0:T(8,128)(2,1)S(1)}, u32[]{:S(2)}, u32[]{:S(2)}) %collective-permute-start.4) | collective-permute-done | bytes 24608 | tf_op jit(solution)/shard_map/ppermute | solution.py:207
  86.5 1.4 copy-done
  87.9 1.4 copy-done.1
  89.3 1.4 copy-done.2
  91.3 0.8 copy-done.9
  92.2 1.0 copy-done.10
  93.2 8.2 %shard_map.148 = (bf16[32,16,1024]{2,1,0:T(8,128)(2,1)S(1)}, bf16[32,16,1024]{2,1,0:T(8,128)(2,1)S(1)}, f32[256,64]{1,0:T(8,128)S(1)}, f32[64,192]{1,0:T(8,128)S(1)}, f32[64,192]{1,0:T(8,128)S(1)}) custom-call(s32[3]{0:T(128)S(1)} %copy-done.5, bf16[32,24,1024]{2,1,0:T(8,128)(2,1)} %all-to-all-done.mine.cot, ...), custom_call_target="tpu_custom_call" | custom-call | flops 4000000000 | bytes 13082636 | tf_op jit(solution)/shard_map/pallas_call | solution.py:36
  102.0 2.3 %collective-permute-done.10.inner_b = f32[256,64]{1,0:T(8,128)S(1)} collective-permute-done((f32[256,64]{1,0:T(8,128)S(1)}, f32[256,64]{1,0:T(8,128)S(1)}, u32[]{:S(2)}, u32[]{:S(2)}) %collective-permute-start.10) | collective-permute-done | bytes 65568 | tf_op jit(solution)/shard_map/ppermute | solution.py:207
  104.4 1.6 %shard_map.150 = f32[64,1024]{1,0:T(8,128)S(1)} custom-call(s32[3]{0:T(128)S(1)} %copy-done.5, f32[256,64]{1,0:T(8,128)S(1)} %get-tuple-element.25.inner_a, f32[256,64]{1,0:T(8,128)S(1)} %collective-permute-done.10.inner_b, bf16[32,24,1024]{2,1,0:T(8,128)(2,1)} %all-to-all-done.mine.cot), custom_call_target="tpu_custom_call" | custom-call | flops 100000000 | bytes 1966092 | tf_op jit(solution)/shard_map/pallas_call | solution.py:36
  106.3 1.4 add_convert_fusion
  107.6 9.8 %all-to-all-start.1 = ((bf16[32,16,1024]{2,1,0:T(8,128)(2,1)}), bf16[32,16,1024]{2,1,0:T(8,128)(2,1)S(1)}, u32[]{:S(2)}, u32[]{:S(2)}) async-start(bf16[32,16,1024]{2,1,0:T(8,128)(2,1)} %add_convert_fusion), calls=%async_computation.1 | async-start | bytes 2097152 | tf_op jit(solution)/shard_map/all_to_all | solution.py:215
  117.6 3.3 %collective-permute-start.12 = (f32[64,2048]{1,0:T(8,128)S(1)}, f32[64,2048]{1,0:T(8,128)S(1)}, u32[]{:S(2)}, u32[]{:S(2)}) collective-permute-start(f32[64,2048]{1,0:T(8,128)S(1)} %pad_maximum_fusion.1), channel_id=1, source_target_pairs={{0,2},{2,0},{1,3},{3,1},{4,6},{6,4},{5,7},{7,5},{8,10},{10,8},{9,1... | collective-permute-start | bytes 1572872 | tf_op jit(solution)/shard_map/ppermute | solution.py:207
  121.4 1.1 shard_map.147
  122.5 11.9 %collective-permute-done.9 = f32[64,192]{1,0:T(8,128)S(1)} collective-permute-done((f32[64,192]{1,0:T(8,128)S(1)}, f32[64,192]{1,0:T(8,128)S(1)}, u32[]{:S(2)}, u32[]{:S(2)}) %collective-permute-start.9) | collective-permute-done | bytes 49184 | tf_op jit(solution)/shard_map/ppermute | solution.py:207
  135.2 10.8 %all-to-all-done.1.back = bf16[32,16,1024]{2,1,0:T(8,128)(2,1)S(1)} async-done(((bf16[32,16,1024]{2,1,0:T(8,128)(2,1)}), bf16[32,16,1024]{2,1,0:T(8,128)(2,1)S(1)}, u32[]{:S(2)}, u32[]{:S(2)}) %all-to-all-start.1) | async-done | bytes 1048608 | tf_op jit(solution)/shard_map/all_to_all | solution.py:215
  146.0 1.0 shard_map.149
  147.0 3.1 %collective-permute-start.6 = (bf16[2,48,512]{2,1,0:T(8,128)(2,1)S(1)}, bf16[2,48,512]{2,1,0:T(8,128)(2,1)S(1)}, u32[]{:S(2)}, u32[]{:S(2)}) collective-permute-start(bf16[2,48,512]{2,1,0:T(8,128)(2,1)S(1)} %get-tuple-element.20), channel_id=1, source_target_pairs={{0,2},{2,0},{1,3},{3,1},{4,6},{6,4},{5,7},{7,5},{8,10},{10,8},{9,1... | collective-permute-start | bytes 294920 | tf_op jit(solution)/shard_map/ppermute | solution.py:207
  151.3 1.0 pad_maximum_fusion
  152.3 1.5 collective-permute-done.6
  153.9 1.4 collective-permute-done.7
  155.2 1.4 collective-permute-done.8
  (42 shorter events, 7.7 us)
Async XLA Ops:
  3.6 10.0 %collective-permute-start.1 = (bf16[3,48,1024]{2,1,0:T(8,128)(2,1)}, bf16[3,48,1024]{2,1,0:T(8,128)(2,1)}, u32[]{:S(2)}, u32[]{:S(2)}) collective-permute-start(bf16[3,48,1024]{2,1,0:T(8,128)(2,1)} %halves.1.own), channel_id=1, source_target_pairs={{0,4},{4,0},{1,5},{5,1},{2,6},{6,2},{3,7},{7,3},{8,12},{12,8},{9,1... | collective-permute-start | bytes 884744 | tf_op jit(solution)/shard_map/ppermute | solution.py:207
  6.6 0.6 copy-start.3
  7.2 5.8 %collective-permute-start = (f32[32,48]{1,0:T(8,128)S(1)}, f32[32,48]{1,0:T(8,128)S(1)}, u32[]{:S(2)}, u32[]{:S(2)}) collective-permute-start(f32[32,48]{1,0:T(8,128)S(1)} %pad_maximum_fusion.2.meta_a), channel_id=1, source_target_pairs={{0,4},{4,0},{1,5},{5,1},{2,6},{6,2},{3,7},{7,3},{8,12},{12,8},{9,1... | collective-permute-start | bytes 18440 | tf_op jit(solution)/shard_map/ppermute | solution.py:207
  13.0 0.6 copy-start.7
  17.2 50.1 %all-to-all-start = ((bf16[32,24,1024]{2,1,0:T(8,128)(2,1)}), bf16[32,24,1024]{2,1,0:T(8,128)(2,1)}, u32[]{:S(2)}, u32[]{:S(2)}) async-start(bf16[32,24,1024]{2,1,0:T(8,128)(2,1)} %select.1), calls=%async_computation | async-start | bytes 3145728 | tf_op jit(solution)/shard_map/all_to_all | solution.py:215
  32.3 54.2 %collective-permute-start.3 = (bf16[3,192,2048]{2,1,0:T(8,128)(2,1)}, bf16[3,192,2048]{2,1,0:T(8,128)(2,1)S(1)}, u32[]{:S(2)}, u32[]{:S(2)}) collective-permute-start(bf16[3,192,2048]{2,1,0:T(8,128)(2,1)} %bundle.1), channel_id=1, source_target_pairs={{0,2},{2,0},{1,3},{3,1},{4,6},{6,4},{5,7},{7,5},{8,10},{10,8},{9,1... | collective-permute-start | bytes 7077896 | tf_op jit(solution)/shard_map/ppermute | solution.py:207
  67.3 19.2 %collective-permute-start.2 = (bf16[32,24,1024]{2,1,0:T(8,128)(2,1)}, bf16[32,24,1024]{2,1,0:T(8,128)(2,1)}, u32[]{:S(2)}, u32[]{:S(2)}) collective-permute-start(bf16[32,24,1024]{2,1,0:T(8,128)(2,1)} %all-to-all-done.mine.cot), channel_id=1, source_target_pairs={{0,1},{1,0},{2,3},{3,2},{4,5},{5,4},{6,7},{7,6},{8,9},{9,8},{10,11... | collective-permute-start | bytes 4718600 | tf_op jit(solution)/shard_map/ppermute | solution.py:207
  68.1 18.4 %collective-permute-start.4 = (bf16[64,192]{1,0:T(8,128)(2,1)S(1)}, bf16[64,192]{1,0:T(8,128)(2,1)S(1)}, u32[]{:S(2)}, u32[]{:S(2)}) collective-permute-start(bf16[64,192]{1,0:T(8,128)(2,1)S(1)} %dynamic-slice_bitcast_fusion), channel_id=1, source_target_pairs={{0,2},{2,0},{1,3},{3,1},{4,6},{6,4},{5,7},{7,5},{8,10},{10,8},{9,1... | collective-permute-start | bytes 73736 | tf_op jit(solution)/shard_map/ppermute | solution.py:207
  86.5 1.4 copy-start
  87.9 1.4 copy-start.1
  89.3 1.4 copy-start.2
  90.7 0.6 copy-start.5
  91.3 0.8 copy-start.9
  92.2 1.0 copy-start.10
  101.4 4.8 %collective-permute-start.5 = (bf16[32,16,1024]{2,1,0:T(8,128)(2,1)S(1)}, bf16[32,16,1024]{2,1,0:T(8,128)(2,1)S(1)}, u32[]{:S(2)}, u32[]{:S(2)}) collective-permute-start(bf16[32,16,1024]{2,1,0:T(8,128)(2,1)S(1)} %get-tuple-element.18), channel_id=1, source_target_pairs={{0,1},{1,0},{2,3},{3,2},{4,5},{5,4},{6,7},{7,6},{8,9},{9,8},{10,11... | collective-permute-start | bytes 3145736 | tf_op jit(solution)/shard_map/ppermute | solution.py:207
  101.5 2.8 %collective-permute-start.10 = (f32[256,64]{1,0:T(8,128)S(1)}, f32[256,64]{1,0:T(8,128)S(1)}, u32[]{:S(2)}, u32[]{:S(2)}) collective-permute-start(f32[256,64]{1,0:T(8,128)S(1)} %get-tuple-element.25.inner_a), channel_id=1, source_target_pairs={{0,1},{1,0},{2,3},{3,2},{4,5},{5,4},{6,7},{7,6},{8,9},{9,8},{10,11... | collective-permute-start | bytes 196616 | tf_op jit(solution)/shard_map/ppermute | solution.py:207
  106.0 11.4 %collective-permute-start.11 = (f32[64,1024]{1,0:T(8,128)S(1)}, f32[64,1024]{1,0:T(8,128)S(1)}, u32[]{:S(2)}, u32[]{:S(2)}) collective-permute-start(f32[64,1024]{1,0:T(8,128)S(1)} %shard_map.150), channel_id=1, source_target_pairs={{0,1},{1,0},{2,3},{3,2},{4,5},{5,4},{6,7},{7,6},{8,9},{9,8},{10,11... | collective-permute-start | bytes 786440 | tf_op jit(solution)/shard_map/ppermute | solution.py:207
  107.6 38.4 %all-to-all-start.1 = ((bf16[32,16,1024]{2,1,0:T(8,128)(2,1)}), bf16[32,16,1024]{2,1,0:T(8,128)(2,1)S(1)}, u32[]{:S(2)}, u32[]{:S(2)}) async-start(bf16[32,16,1024]{2,1,0:T(8,128)(2,1)} %add_convert_fusion), calls=%async_computation.1 | async-start | bytes 2097152 | tf_op jit(solution)/shard_map/all_to_all | solution.py:215
  117.4 4.0 %copy-start.4 = (f32[32,48]{1,0:T(8,128)S(1)}, f32[32,48]{1,0:T(8,128)}, u32[]{:S(2)}) copy-start(f32[32,48]{1,0:T(8,128)} %copy-done.3) | copy-start | bytes 18436
  117.4 4.0 %copy-start.6 = (s32[3]{0:T(128)S(1)}, s32[3]{0:T(128)}, u32[]{:S(2)}) copy-start(s32[3]{0:T(128)} %pad_add_fusion.where_ref) | copy-start | bytes 40
  117.4 4.0 %copy-start.8 = (f32[32,48]{1,0:T(8,128)S(1)}, f32[32,48]{1,0:T(8,128)}, u32[]{:S(2)}) copy-start(f32[32,48]{1,0:T(8,128)} %copy-done.7) | copy-start | bytes 18436
  117.6 17.5 %collective-permute-start.12 = (f32[64,2048]{1,0:T(8,128)S(1)}, f32[64,2048]{1,0:T(8,128)S(1)}, u32[]{:S(2)}, u32[]{:S(2)}) collective-permute-start(f32[64,2048]{1,0:T(8,128)S(1)} %pad_maximum_fusion.1), channel_id=1, source_target_pairs={{0,2},{2,0},{1,3},{3,1},{4,6},{6,4},{5,7},{7,5},{8,10},{10,8},{9,1... | collective-permute-start | bytes 1572872 | tf_op jit(solution)/shard_map/ppermute | solution.py:207
  120.9 13.5 %collective-permute-start.9 = (f32[64,192]{1,0:T(8,128)S(1)}, f32[64,192]{1,0:T(8,128)S(1)}, u32[]{:S(2)}, u32[]{:S(2)}) collective-permute-start(f32[64,192]{1,0:T(8,128)S(1)} %get-tuple-element.24), channel_id=1, source_target_pairs={{0,2},{2,0},{1,3},{3,1},{4,6},{6,4},{5,7},{7,5},{8,10},{10,8},{9,1... | collective-permute-start | bytes 147464 | tf_op jit(solution)/shard_map/ppermute | solution.py:207
  147.0 6.8 %collective-permute-start.6 = (bf16[2,48,512]{2,1,0:T(8,128)(2,1)S(1)}, bf16[2,48,512]{2,1,0:T(8,128)(2,1)S(1)}, u32[]{:S(2)}, u32[]{:S(2)}) collective-permute-start(bf16[2,48,512]{2,1,0:T(8,128)(2,1)S(1)} %get-tuple-element.20), channel_id=1, source_target_pairs={{0,2},{2,0},{1,3},{3,1},{4,6},{6,4},{5,7},{7,5},{8,10},{10,8},{9,1... | collective-permute-start | bytes 294920 | tf_op jit(solution)/shard_map/ppermute | solution.py:207
  150.1 5.1 %collective-permute-start.7 = (bf16[2,48,512]{2,1,0:T(8,128)(2,1)S(1)}, bf16[2,48,512]{2,1,0:T(8,128)(2,1)S(1)}, u32[]{:S(2)}, u32[]{:S(2)}) collective-permute-start(bf16[2,48,512]{2,1,0:T(8,128)(2,1)S(1)} %get-tuple-element.21), channel_id=1, source_target_pairs={{0,4},{4,0},{1,5},{5,1},{2,6},{6,2},{3,7},{7,3},{8,12},{12,8},{9,1... | collective-permute-start | bytes 294920 | tf_op jit(solution)/shard_map/ppermute | solution.py:207
  150.7 5.8 %collective-permute-start.8 = (bf16[2,48,512]{2,1,0:T(8,128)(2,1)S(1)}, bf16[2,48,512]{2,1,0:T(8,128)(2,1)S(1)}, u32[]{:S(2)}, u32[]{:S(2)}) collective-permute-start(bf16[2,48,512]{2,1,0:T(8,128)(2,1)S(1)} %get-tuple-element.22), channel_id=1, source_target_pairs={{0,6},{2,4},{4,2},{6,0},{1,7},{3,5},{5,3},{7,1},{8,14},{10,12},{12... | collective-permute-start | bytes 294920 | tf_op jit(solution)/shard_map/ppermute | solution.py:211

commit v3 on v2

v3 whole, which is shorter than its diff:
```python
import jax
import jax.numpy as jnp
from jax import lax
from jax.experimental import pallas as pl
from jax.experimental.pallas import tpu as pltpu
from jax.sharding import Mesh, PartitionSpec as P

BF = jnp.bfloat16
F32 = jnp.float32
SCALE = 2.0
SLOT = 4
PEERS = 32
TOK = 48
Q = 512
ROWS = 256
META = 3 * TOK
FULL = 67043328


def nt(a, b):
    return lax.dot_general(a, b, (((1,), (1,)), ((), ())), preferred_element_type=F32)


def nn(a, b):
    return lax.dot_general(a, b, (((1,), (0,)), ((), ())), preferred_element_type=F32)


def tn(a, b):
    return lax.dot_general(a, b, (((0,), (0,)), ((), ())), preferred_element_type=F32)


def vmem_call(body, outs, args, flops=10**8, mib=16):
    return kernel(body, outs, args, [], "v" * len(args), "v" * len(outs), flops, mib << 20)


SPACES = {
    "h": pl.BlockSpec(memory_space=pltpu.HBM),
    "v": pl.BlockSpec(memory_space=pltpu.VMEM),
}


def kernel(body, outs, args, scratch, ins, places, flops=10**8, limit=FULL):
    moved = sum(a.size * a.dtype.itemsize for a in [*args, *outs])

    def run(*refs):
        xl, xh = lax.axis_index("xl"), lax.axis_index("xh")
        body((2 * xl + xh, lax.axis_index("core"), xh), *refs)

    return pl.pallas_call(
        run,
        out_shape=outs,
        in_specs=[SPACES[x] for x in ins],
        out_specs=[SPACES[x] for x in places],
        scratch_shapes=scratch,
        compiler_params=pltpu.CompilerParams(vmem_limit_bytes=limit),
        cost_estimate=pl.CostEstimate(flops=flops, bytes_accessed=moved, transcendentals=0),
    )(*args)


def sds(shape, dtype):
    return jax.ShapeDtypeStruct(shape, dtype)


def quarter(h, core):
    return pl.ds(pl.multiple_of((2 * h + core) * Q, Q), Q)


def pieces(x):
    hi = x.astype(BF)
    rest = x - hi.astype(F32)
    mid = rest.astype(BF)
    return hi, mid, (rest - mid.astype(F32)).astype(BF)


def run_all(copies):
    for copy in copies:
        copy.start()
    for copy in copies:
        copy.wait()


def halves_body(where, policy, frozen, cotangent, route_p, gates_p, route_f, gates_f, own, sems):
    copies = []
    for n, ref in enumerate((policy, frozen, cotangent)):
        for h in range(2):
            copies.append(pltpu.make_async_copy(
                ref.at[:, quarter(h, where[1])],
                own.at[TOK * n : TOK * n + TOK, h * Q : (h + 1) * Q],
                sems.at[n, h],
            ))
    for copy in copies:
        copy.start()
    pad = jnp.zeros((8, 128 - TOK), BF)
    for n, (route, gates) in enumerate(((route_p, gates_p), (route_f, gates_f))):
        for p, x in enumerate((route[...].astype(F32).astype(BF), *pieces(gates[...]))):
            at = 128 * (4 * n + p)
            own[META:, at : at + 128] = jnp.concatenate([x, pad], axis=1)
    for copy in copies:
        copy.wait()


def bundle_body(where, wg, wu, wd, ad, out, stage, small, sems):
    away = 1 - where[2]
    last = pltpu.make_async_copy(ad.at[away], small, sems.at[0, 12])
    into, back = [], []
    for n, ref in enumerate((wg, wu, wd)):
        for k in range(4):
            at = 192 * n + 48 * k
            piece = stage.at[at : at + 48, :]
            src = ref.at[away, 48 * k : 48 * k + 48, :]
            into.append(pltpu.make_async_copy(src, piece, sems.at[0, 4 * n + k]))
            back.append(pltpu.make_async_copy(piece, out.at[at : at + 48, :], sems.at[1, 4 * n + k]))
    for copy in (*into, last):
        copy.start()
    for a, b in zip(into, back):
        a.wait()
        b.start()
    last.wait()
    pad = jnp.zeros((8, 64), BF)
    rest = [jnp.concatenate([small[8 * k : 8 * k + 8, :], pad], axis=1) for k in range(8)]
    stage[576:584, :] = jnp.concatenate(rest, axis=1)
    tail = pltpu.make_async_copy(stage.at[576:584, :], out.at[576:584, :], sems.at[1, 12])
    tail.start()
    for copy in (*back, tail):
        copy.wait()


def blocks(meta_a, meta_b, n):
    out = []
    for meta in (meta_a, meta_b):
        part = [meta[:, 128 * (4 * n + p) : 128 * (4 * n + p) + TOK].astype(F32) for p in range(4)]
        out.append((part[0], part[1] + part[2] + part[3]))
    return [jnp.concatenate([a, b], axis=1) for a, b in zip(*out)]


def tables(where, meta_a, meta_b, n):
    cols = 2 * TOK
    route, gates = blocks(meta_a, meta_b, n)
    col = lax.broadcasted_iota(jnp.int32, (ROWS, cols), 1)
    row = lax.broadcasted_iota(jnp.int32, (ROWS, cols), 0)
    expert = (4 * (row // 8) + where[0]).astype(F32)
    named = jnp.zeros((ROWS, cols), F32)
    gate = jnp.zeros((ROWS, cols), F32)
    for k in range(8):
        match = route[k : k + 1] == expert
        named = named + jnp.where(match, 1.0, 0.0)
        gate = gate + jnp.where(match, gates[k : k + 1], 0.0)
    r0 = lax.broadcasted_iota(jnp.int32, (cols, cols), 0)
    r1 = lax.broadcasted_iota(jnp.int32, (cols, cols), 1)
    earlier = jnp.where((r0 < r1) & ((r0 < TOK) == (r1 < TOK)), 1.0, 0.0)
    position = nn(named.astype(BF), earlier.astype(BF))
    here = (position == (row % SLOT).astype(F32)) & (((row // SLOT) % 2 == 1) == (col >= TOK))
    return jnp.where(here, named, 0.0), jnp.where(here, gate, 0.0)


def select_body(where, own, other, sent, stage, sems):
    member_p, gate_p = tables(where, own[META:, :], other[META:, :], 0)
    copies = []
    for i in (0, 2, 1):
        member = member_p
        if i == 1:
            member, _ = tables(where, own[META:, :], other[META:, :], 1)
        at = slice(TOK * i, TOK * i + TOK)
        picked = nn(member.astype(BF), jnp.concatenate([own[at, :], other[at, :]], axis=0))
        if i == 2:
            picked = picked * jnp.sum(gate_p, axis=1, keepdims=True)
        at = slice(8 * i, 8 * i + 8)
        stage[:, at, :] = picked.astype(BF).reshape(PEERS, 8, 2 * Q)
        copies.append(pltpu.make_async_copy(stage.at[:, at, :], sent.at[:, at, :], sems.at[i]))
        copies[-1].start()
    for copy in copies:
        copy.wait()


def home_body(where, own, other, member_p, gates_f):
    meta_a, meta_b = own[META:, :], other[META:, :]
    member, _ = tables(where, meta_a, meta_b, 0)
    member_p[...] = member.T.astype(BF)
    _, gate = tables(where, meta_a, meta_b, 1)
    for n, piece in enumerate(pieces(gate.T)):
        gates_f[n] = piece


def preload_body(where, wg, wu, wd, ad, au, w, small, up, sems):
    e = where[2]
    moves = [(r.at[e], w.at[n]) for n, r in enumerate((wg, wu, wd))]
    moves += [(ad.at[e], small), (au.at[e], up)]
    run_all([pltpu.make_async_copy(a, b, sems.at[n]) for n, (a, b) in enumerate(moves)])


def arrive_body(where, w2, out, sems):
    run_all([pltpu.make_async_copy(w2, out, sems.at[0])])


def main_body(
    where, mine, theirs, own, small, up, w2, give, keep, inner, down_grad, down_grad2
):
    c = where[1]

    def weight(*kinds):
        def at(lanes):
            out = []
            for k in kinds:
                out += [up[:, lanes]] if k == 3 else [own[k, :, lanes], w2[192 * k : 192 * k + 192, lanes]]
            return jnp.concatenate(out, axis=0)

        return at

    def dot(i, w):
        total = None
        for ref, core in ((mine, c), (theirs, 1 - c)):
            for h in range(2):
                x = ref[:, 8 * i : 8 * i + 8, h * Q : (h + 1) * Q].reshape(ROWS, Q)
                part = nt(x, w(quarter(h, core)))
                total = part if total is None else total + part
        return total

    def expand(x, w, i):
        for out, core in ((give, 1 - c), (keep, c)):
            for h in range(2):
                total = nn(x, w(quarter(h, core))).astype(BF).reshape(PEERS, 8, Q)
                out[:, 8 * i : 8 * i + 8, h * Q : (h + 1) * Q] = total

    both, down, down_up = weight(0, 1), weight(2), weight(2, 3)
    pre = dot(1, both)
    gate_pre, up_pre = pre[:, :384], pre[:, 384:]
    expand((gate_pre * jax.nn.sigmoid(gate_pre) * up_pre).astype(BF), down, 1)
    tail = [w2[576:584, 256 * k : 256 * k + 192] for k in range(8)]
    adapters = jnp.concatenate([small[...], jnp.concatenate(tail, axis=0)], axis=1)
    pre = dot(0, both)
    gate_pre, up_pre = pre[:, :384], pre[:, 384:]
    sigmoid = jax.nn.sigmoid(gate_pre)
    activated = gate_pre * sigmoid
    hidden = (activated * up_pre).astype(BF)
    slope = up_pre * sigmoid * (1.0 + gate_pre * (1.0 - sigmoid))
    inner[...] = nt(hidden, adapters)
    pre = dot(2, down_up)
    inner_grad = (SCALE * pre[:, 384:]).astype(BF)
    grads = tn(inner_grad, hidden)
    down_grad[...] = grads[:, :192]
    down_grad2[...] = grads[:, 192:]
    hidden_grad = pre[:, :384] + nn(inner_grad, adapters)
    gate_grad = (hidden_grad * slope).astype(BF)
    up_grad = (hidden_grad * activated).astype(BF)
    expand(jnp.concatenate([gate_grad, up_grad], axis=1), both, 0)


def up_body(where, inner_a, inner_b, cot, out):
    inner = (inner_a[...] + inner_b[...]).astype(BF)
    out[...] = SCALE * tn(inner, cot[:, 16:24, :].reshape(ROWS, 2 * Q))


def combine_body(where, member, gates, back, own, to_xh, to_xl, to_both):
    for at, near, far in ((where[2], own, to_xl), (1 - where[2], to_xh, to_both)):
        lanes = pl.ds(pl.multiple_of(at * Q, Q), Q)
        grads = back[:, 0:8, lanes].reshape(ROWS, Q)
        frozen = back[:, 8:16, lanes].reshape(ROWS, Q)
        frozen = nn(gates[2], frozen) + nn(gates[1], frozen) + nn(gates[0], frozen)
        grads = nn(member[...], grads)
        for n, total in enumerate((frozen, grads)):
            near[n] = total[:TOK].astype(near.dtype)
            far[n] = total[TOK:].astype(far.dtype)


def swap(x, axis):
    return lax.ppermute(x, axis, [(0, 1), (1, 0)])


def swap_both(x):
    return lax.ppermute(x, ("xl", "xh"), [(i, 3 - i) for i in range(4)])


def exchange(x):
    return lax.all_to_all(x, ("y", "z"), split_axis=0, concat_axis=0, tiled=True)


def pick(c, a, b):
    return jnp.where(c == 0, a, b)


def step(
    policy_tokens, policy_cotangent, frozen_tokens, policy_route, policy_gates,
    frozen_route, frozen_gates, w_gate, w_up, w_down, adapter_down, adapter_up,
):
    c, xh = lax.axis_index("core"), lax.axis_index("xh")
    wg, wu = w_gate.swapaxes(1, 2), w_up.swapaxes(1, 2)
    ad = adapter_down.swapaxes(1, 2)
    own = kernel(
        halves_body, [sds((META + 8, 2 * Q), BF)],
        [policy_tokens, frozen_tokens, policy_cotangent,
         policy_route.T, policy_gates.T, frozen_route.T, frozen_gates.T],
        [pltpu.SemaphoreType.DMA((3, 2))], "hhhvvvv", "v", limit=FULL - 400000,
    )[0]
    other = swap(own, "xl")
    bundle = kernel(
        bundle_body, [sds((584, 4 * Q), BF)], [wg, wu, w_down, ad],
        [pltpu.VMEM((584, 4 * Q), BF), pltpu.VMEM((64, 192), BF), pltpu.SemaphoreType.DMA((2, 13))],
        "hhhh", "h", limit=FULL - 800000,
    )[0]
    w2 = swap(bundle, "xh")
    (sent,) = kernel(
        select_body, [sds((PEERS, 24, 2 * Q), BF)], [own, other],
        [pltpu.VMEM((PEERS, 24, 2 * Q), BF), pltpu.SemaphoreType.DMA((3,))], "vv", "h",
        limit=12 << 20,
    )
    member_p, gates_f = vmem_call(
        home_body, [sds((2 * TOK, ROWS), BF), sds((3, 2 * TOK, ROWS), BF)],
        [own, other], flops=10**8, mib=8,
    )
    mine = exchange(sent)
    theirs = swap(mine, "core")
    own_w, small, up = kernel(
        preload_body, [sds((3, 192, 4 * Q), BF), sds((64, 192), BF), sds((64, 4 * Q), BF)],
        [wg, wu, w_down, ad, adapter_up], [pltpu.SemaphoreType.DMA((5,))], "hhhhh", "vvv", limit=8 << 20,
    )
    (w2,) = kernel(
        arrive_body, [sds((584, 4 * Q), BF)], [w2], [pltpu.SemaphoreType.DMA((1,))],
        "h", "v", limit=8 << 20,
    )
    wide = sds((PEERS, 16, 2 * Q), BF)
    give, keep, inner, down_grad, down_grad2 = kernel(
        main_body,
        [wide, wide, sds((ROWS, 64), F32), sds((64, 192), F32), sds((64, 192), F32)],
        [mine, theirs, own_w, small, up, w2], [], "vvvvvv", "vvvvv", flops=4 * 10**9, limit=28 << 20,
    )
    total = (keep.astype(F32) + swap(give, "core").astype(F32)).astype(BF)
    back = exchange(total)
    own, to_xh, to_xl, to_both = vmem_call(
        combine_body, [sds((2, TOK, Q), F32)] + [sds((2, TOK, Q), BF)] * 3,
        [member_p, gates_f, back], flops=10**8, mib=8,
    )
    from_xh = swap(to_xh, "xh")
    from_xl = swap(to_xl, "xl")
    from_both = swap_both(to_both)
    outs = own + from_xh.astype(F32) + from_xl.astype(F32) + from_both.astype(F32)
    frozen_out, input_grad = outs[0].astype(BF), outs[1].astype(BF)

    (up_half,) = vmem_call(
        up_body, [sds((64, 2 * Q), F32)], [inner, swap(inner, "core"), mine],
        flops=10**8, mib=6,
    )
    up_other = swap(up_half, "core")
    lo, hi = pick(c, up_half, up_other), pick(c, up_other, up_half)
    up_own = jnp.concatenate([lo[:, :Q], hi[:, :Q], lo[:, Q:], hi[:, Q:]], axis=1)
    up_away = swap(up_own, "xh")
    up_grad = jnp.stack([pick(xh, up_own, up_away), pick(xh, up_away, up_own)])
    down_away = swap(down_grad2, "xh")
    down = jnp.stack([pick(xh, down_grad, down_away), pick(xh, down_away, down_grad)]).swapaxes(1, 2)
    return frozen_out, input_grad, down, up_grad


def solution(mesh):
    fine = Mesh(mesh.devices.reshape(4, 8, 2, 2, 2), ("y", "z", "xl", "xh", "core"))
    ex, pr = ("y", "z", "xl"), ("xh", "core")
    in_specs = (P(ex, None),) * 7 + (
        P(ex, None, pr), P(ex, None, pr), P(ex, pr, None), P(ex, pr, None), P(ex, None, None),
    )
    out_specs = (P(ex, pr), P(ex, pr), P(ex, pr, None), P(ex, None, None))
    return jax.shard_map(step, mesh=fine, in_specs=in_specs, out_specs=out_specs, check_vma=False)
```

time: 158 us -> 145 us (0.918)
  Pallas kernels: 21.6 us -> 17 us
  starting transfers between devices: 38.3 us -> 34.5 us
  local copies, waits for them, and re-layouts: 9.37 us -> 6.92 us
    pallas_call x7 -> x9, Pallas kernels: 21.6 us -> 17 us  [kernel(): pl.pallas_call(run, out_shape=outs, in_specs=[SPACES[x] for x in ins], ou...]
    ppermute x12 -> x10, starting transfers between devices: 16.6 us -> 12.7 us  [swap(): return lax.ppermute(x, axis, [(0, 1), (1, 0)])]
    all_to_all x2, waiting for transfers between devices: 42.7 us -> 39.1 us  [exchange(): lax.all_to_all(x, ('y', 'z'), split_axis=0, concat_axis=0, tiled=True)]
    unnamed x22 -> x16, local copies, waits for them, and re-layouts: 7.93 us -> 6.24 us
    ppermute x12 -> x10, waiting for transfers between devices: 37.8 us -> 39.5 us  [swap(): return lax.ppermute(x, axis, [(0, 1), (1, 0)])]
  transfers between devices with their start and end apart: 15 -> 13, of which waited for: 9 -> 10; matrix products, arithmetic and copies ran while one was open for 3% -> 3% of each run, Pallas kernels for 4% -> 4%
where the time goes in v3:
time: 145 us; the launch traced here: 144 us
  waiting for transfers between devices  80.4 us (55%)
  starting transfers between devices  34.5 us (24%)
  Pallas kernels  17 us (12%)
  local copies, waits for them, and re-layouts  6.92 us (5%)
  other arithmetic  4.4 us (3%)
    ppermute x10, waiting for transfers between devices, swap(): return lax.ppermute(x, axis, [(0, 1), (1, 0)])  39.5 us
    all_to_all x2, waiting for transfers between devices, exchange(): lax.all_to_all(x, ('y', 'z'), split_axis=0, concat_axis=0, tiled=True)  39.1 us
    all_to_all x2, starting transfers between devices, exchange(): lax.all_to_all(x, ('y', 'z'), split_axis=0, concat_axis=0, tiled=True)  21.2 us
    pallas_call x9, Pallas kernels, kernel(): pl.pallas_call(run, out_shape=outs, in_specs=[SPACES[x] for x in ins], ou...  17 us
    ppermute x10, starting transfers between devices, swap(): return lax.ppermute(x, axis, [(0, 1), (1, 0)])  12.7 us
    unnamed x16, local copies, waits for them, and re-layouts  6.24 us
  transfers between devices with their start and end apart: 13, of which 10 were waited for; matrix products, arithmetic and copies ran while one was open for 3% of the time, Pallas kernels for 4%

profile of v3, /device:TPU:32, one launch (start us, length us, event | category | flops | bytes accessed | tf_op | source)
XLA Modules:
  0.0 144.0 jit_solution(11018114263423858340)
XLA Ops:
  0.6 2.4 %shard_map.147.refs_0_ = bf16[152,1024]{1,0:T(8,128)(2,1)} custom-call(bf16[48,2048]{1,0:T(8,128)(2,1)} %refs_0_.1, bf16[48,2048]{1,0:T(8,128)(2,1)} %refs_1_.1, bf16[48,2048]{1,0:T(8,128)(2,1)} %refs_2_.3, s32[8,48]{1,0:T(8,128)} %bitcast.27, f32[8,48]{1,0:T(8,128)} %bitcast.28, s32[8,48]{1,0:T(8,128)} %bitcast.29, f32[8,48]{1,0:T(8,128)} %bitcast.30), custom_call_target="tpu_custom_call" | custom-call | flops 100000000 | bytes 907264 | tf_op jit(solution)/shard_map/pallas_call | solution.py:49
  3.1 1.6 %collective-permute-start = (bf16[152,1024]{1,0:T(8,128)(2,1)}, bf16[152,1024]{1,0:T(8,128)(2,1)S(1)}, u32[]{:S(2)}, u32[]{:S(2)}) collective-permute-start(bf16[152,1024]{1,0:T(8,128)(2,1)} %shard_map.147.refs_0_), channel_id=1, source_target_pairs={{0,4},{4,0},{1,5},{5,1},{2,6},{6,2},{3,7},{7,3},{8,12},{12,8},{9,1... | collective-permute-start | bytes 933896 | tf_op jit(solution)/shard_map/ppermute | solution.py:266
  4.7 7.8 %collective-permute-done.refs_1_ = bf16[152,1024]{1,0:T(8,128)(2,1)S(1)} collective-permute-done((bf16[152,1024]{1,0:T(8,128)(2,1)}, bf16[152,1024]{1,0:T(8,128)(2,1)S(1)}, u32[]{:S(2)}, u32[]{:S(2)}) %collective-permute-start) | collective-permute-done | bytes 311328 | tf_op jit(solution)/shard_map/ppermute | solution.py:266
  12.5 1.0 copy-done.3
  13.4 1.8 %shard_map.149 = bf16[32,24,1024]{2,1,0:T(8,128)(2,1)} custom-call(bf16[152,1024]{1,0:T(8,128)(2,1)S(1)} %copy-done.3, bf16[152,1024]{1,0:T(8,128)(2,1)S(1)} %collective-permute-done.refs_1_), custom_call_target="tpu_custom_call" | custom-call | flops 100000000 | bytes 2195456 | tf_op jit(solution)/shard_map/pallas_call | solution.py:49
  15.3 11.4 %all-to-all-start = ((bf16[32,24,1024]{2,1,0:T(8,128)(2,1)}), bf16[32,24,1024]{2,1,0:T(8,128)(2,1)}, u32[]{:S(2)}, u32[]{:S(2)}) async-start(bf16[32,24,1024]{2,1,0:T(8,128)(2,1)} %shard_map.149), calls=%async_computation | async-start | bytes 3145728 | tf_op jit(solution)/shard_map/all_to_all | solution.py:274
  26.7 2.7 %shard_map.151 = bf16[584,2048]{1,0:T(8,128)(2,1)} custom-call(bf16[2,192,2048]{2,1,0:T(8,128)(2,1)} %bitcast.21, bf16[2,192,2048]{2,1,0:T(8,128)(2,1)} %bitcast.23, bf16[2,192,2048]{2,1,0:T(8,128)(2,1)} %refs_2_.5, bf16[2,64,192]{2,1,0:T(8,128)(2,1)} %bitcast.25), custom_call_target="tpu_custom_call" | custom-call | flops 100000000 | bytes 7159808 | tf_op jit(solution)/shard_map/pallas_call | solution.py:49
  29.4 3.1 %collective-permute-start.2 = (bf16[584,2048]{1,0:T(8,128)(2,1)}, bf16[584,2048]{1,0:T(8,128)(2,1)S(1)}, u32[]{:S(2)}, u32[]{:S(2)}) collective-permute-start(bf16[584,2048]{1,0:T(8,128)(2,1)} %shard_map.151), channel_id=1, source_target_pairs={{0,2},{2,0},{1,3},{3,1},{4,6},{6,4},{5,7},{7,5},{8,10},{10,8},{9,1... | collective-permute-start | bytes 7176200 | tf_op jit(solution)/shard_map/ppermute | solution.py:266
  32.5 32.6 %all-to-all-done.refs_0_.refs_2_ = bf16[32,24,1024]{2,1,0:T(8,128)(2,1)} async-done(((bf16[32,24,1024]{2,1,0:T(8,128)(2,1)}), bf16[32,24,1024]{2,1,0:T(8,128)(2,1)}, u32[]{:S(2)}, u32[]{:S(2)}) %all-to-all-start) | async-done | bytes 1572896 | tf_op jit(solution)/shard_map/all_to_all | solution.py:274
  65.2 1.4 copy-done
  66.6 1.4 copy-done.1
  68.0 1.4 copy-done.2
  69.4 1.0 copy-done.5
  70.7 12.8 %collective-permute-done.2.refs_0_ = bf16[584,2048]{1,0:T(8,128)(2,1)S(1)} collective-permute-done((bf16[584,2048]{1,0:T(8,128)(2,1)}, bf16[584,2048]{1,0:T(8,128)(2,1)S(1)}, u32[]{:S(2)}, u32[]{:S(2)}) %collective-permute-start.2) | collective-permute-done | bytes 2392096 | tf_op jit(solution)/shard_map/ppermute | solution.py:266
  83.7 6.9 %shard_map.153 = (bf16[32,16,1024]{2,1,0:T(8,128)(2,1)S(1)}, bf16[32,16,1024]{2,1,0:T(8,128)(2,1)S(1)}, f32[256,64]{1,0:T(8,128)S(1)}, f32[64,192]{1,0:T(8,128)S(1)}, f32[64,192]{1,0:T(8,128)S(1)}) custom-call(bf16[32,24,1024]{2,1,0:T(8,128)(2,1)} %all-to-all-done.refs_0_.refs_2_, bf16[32,24,1024]{2,1,0:T(8,128)(2,1)S(1)} %collective-permute-done.1.refs_1_, ...), custom_call_target="tpu_custom_call" | custom-call | flops 4000000000 | bytes 10444800 | tf_op jit(solution)/shard_map/pallas_call | solution.py:49
  91.2 2.1 %collective-permute-done.3 = bf16[32,16,1024]{2,1,0:T(8,128)(2,1)S(1)} collective-permute-done((bf16[32,16,1024]{2,1,0:T(8,128)(2,1)S(1)}, bf16[32,16,1024]{2,1,0:T(8,128)(2,1)S(1)}, u32[]{:S(2)}, u32[]{:S(2)}) %collective-permute-start.3) | collective-permute-done | bytes 1048608 | tf_op jit(solution)/shard_map/ppermute | solution.py:266
  93.4 1.4 add_convert_fusion
  94.8 9.8 %all-to-all-start.1 = ((bf16[32,16,1024]{2,1,0:T(8,128)(2,1)}), bf16[32,16,1024]{2,1,0:T(8,128)(2,1)S(1)}, u32[]{:S(2)}, u32[]{:S(2)}) async-start(bf16[32,16,1024]{2,1,0:T(8,128)(2,1)} %add_convert_fusion), calls=%async_computation.1 | async-start | bytes 2097152 | tf_op jit(solution)/shard_map/all_to_all | solution.py:274
  104.6 1.6 %shard_map.155 = f32[64,1024]{1,0:T(8,128)S(1)} custom-call(f32[256,64]{1,0:T(8,128)S(1)} %get-tuple-element.31.refs_0_, f32[256,64]{1,0:T(8,128)S(1)} %collective-permute-done.8.refs_1_, bf16[32,24,1024]{2,1,0:T(8,128)(2,1)} %all-to-all-done.refs_0_.refs_2_), custom_call_target="tpu_custom_call" | custom-call | flops 100000000 | bytes 1966080 | tf_op jit(solution)/shard_map/pallas_call | solution.py:49
  106.3 1.5 %collective-permute-done.9 = f32[64,1024]{1,0:T(8,128)S(1)} collective-permute-done((f32[64,1024]{1,0:T(8,128)S(1)}, f32[64,1024]{1,0:T(8,128)S(1)}, u32[]{:S(2)}, u32[]{:S(2)}) %collective-permute-start.9) | collective-permute-done | bytes 262176 | tf_op jit(solution)/shard_map/ppermute | solution.py:266
  108.0 3.1 %collective-permute-start.10 = (f32[64,2048]{1,0:T(8,128)S(1)}, f32[64,2048]{1,0:T(8,128)}, u32[]{:S(2)}, u32[]{:S(2)}) collective-permute-start(f32[64,2048]{1,0:T(8,128)S(1)} %pad_maximum_fusion.1), channel_id=1, source_target_pairs={{0,2},{2,0},{1,3},{3,1},{4,6},{6,4},{5,7},{7,5},{8,10},{10,8},{9,1... | collective-permute-start | bytes 1572872 | tf_op jit(solution)/shard_map/ppermute | solution.py:266
  112.1 12.8 %collective-permute-done.7 = f32[64,192]{1,0:T(8,128)S(1)} collective-permute-done((f32[64,192]{1,0:T(8,128)S(1)}, f32[64,192]{1,0:T(8,128)S(1)}, u32[]{:S(2)}, u32[]{:S(2)}) %collective-permute-start.7) | collective-permute-done | bytes 49184 | tf_op jit(solution)/shard_map/ppermute | solution.py:266
  125.0 0.7 maximum_bitcast_fusion
  125.6 1.2 select_bitcast_fusion.1
  126.8 6.5 %all-to-all-done.1.refs_2_ = bf16[32,16,1024]{2,1,0:T(8,128)(2,1)S(1)} async-done(((bf16[32,16,1024]{2,1,0:T(8,128)(2,1)}), bf16[32,16,1024]{2,1,0:T(8,128)(2,1)S(1)}, u32[]{:S(2)}, u32[]{:S(2)}) %all-to-all-start.1) | async-done | bytes 1048608 | tf_op jit(solution)/shard_map/all_to_all | solution.py:274
  133.8 3.1 %collective-permute-start.4 = (bf16[2,48,512]{2,1,0:T(8,128)(2,1)S(1)}, bf16[2,48,512]{2,1,0:T(8,128)(2,1)S(1)}, u32[]{:S(2)}, u32[]{:S(2)}) collective-permute-start(bf16[2,48,512]{2,1,0:T(8,128)(2,1)S(1)} %get-tuple-element.26), channel_id=1, source_target_pairs={{0,2},{2,0},{1,3},{3,1},{4,6},{6,4},{5,7},{7,5},{8,10},{10,8},{9,1... | collective-permute-start | bytes 294920 | tf_op jit(solution)/shard_map/ppermute | solution.py:266
  136.9 0.6 collective-permute-start.5
  138.1 1.1 pad_maximum_fusion
  139.1 1.7 %collective-permute-done.4 = bf16[2,48,512]{2,1,0:T(8,128)(2,1)S(1)} collective-permute-done((bf16[2,48,512]{2,1,0:T(8,128)(2,1)S(1)}, bf16[2,48,512]{2,1,0:T(8,128)(2,1)S(1)}, u32[]{:S(2)}, u32[]{:S(2)}) %collective-permute-start.4) | collective-permute-done | bytes 98336 | tf_op jit(solution)/shard_map/ppermute | solution.py:266
  140.8 0.7 collective-permute-done.5
  141.5 1.8 %collective-permute-done.6 = bf16[2,48,512]{2,1,0:T(8,128)(2,1)S(1)} collective-permute-done((bf16[2,48,512]{2,1,0:T(8,128)(2,1)S(1)}, bf16[2,48,512]{2,1,0:T(8,128)(2,1)S(1)}, u32[]{:S(2)}, u32[]{:S(2)}) %collective-permute-start.6) | collective-permute-done | bytes 98336 | tf_op jit(solution)/shard_map/ppermute | solution.py:270
  143.4 0.6 slice_bitcast_fusion
  (29 shorter events, 3.4 us)
Async XLA Ops:
  3.1 9.4 %collective-permute-start = (bf16[152,1024]{1,0:T(8,128)(2,1)}, bf16[152,1024]{1,0:T(8,128)(2,1)S(1)}, u32[]{:S(2)}, u32[]{:S(2)}) collective-permute-start(bf16[152,1024]{1,0:T(8,128)(2,1)} %shard_map.147.refs_0_), channel_id=1, source_target_pairs={{0,4},{4,0},{1,5},{5,1},{2,6},{6,2},{3,7},{7,3},{8,12},{12,8},{9,1... | collective-permute-start | bytes 933896 | tf_op jit(solution)/shard_map/ppermute | solution.py:266
  12.5 1.0 copy-start.3
  15.3 49.9 %all-to-all-start = ((bf16[32,24,1024]{2,1,0:T(8,128)(2,1)}), bf16[32,24,1024]{2,1,0:T(8,128)(2,1)}, u32[]{:S(2)}, u32[]{:S(2)}) async-start(bf16[32,24,1024]{2,1,0:T(8,128)(2,1)} %shard_map.149), calls=%async_computation | async-start | bytes 3145728 | tf_op jit(solution)/shard_map/all_to_all | solution.py:274
  26.7 38.5 %copy-start.6 = (bf16[2,192,64]{1,2,0:T(8,128)(2,1)S(1)}, bf16[2,192,64]{1,2,0:T(8,128)(2,1)}, u32[]{:S(2)}) copy-start(bf16[2,192,64]{1,2,0:T(8,128)(2,1)} %param.22) | copy-start | bytes 147460
  29.4 54.1 %collective-permute-start.2 = (bf16[584,2048]{1,0:T(8,128)(2,1)}, bf16[584,2048]{1,0:T(8,128)(2,1)S(1)}, u32[]{:S(2)}, u32[]{:S(2)}) collective-permute-start(bf16[584,2048]{1,0:T(8,128)(2,1)} %shard_map.151), channel_id=1, source_target_pairs={{0,2},{2,0},{1,3},{3,1},{4,6},{6,4},{5,7},{7,5},{8,10},{10,8},{9,1... | collective-permute-start | bytes 7176200 | tf_op jit(solution)/shard_map/ppermute | solution.py:266
  65.1 18.6 %collective-permute-start.1 = (bf16[32,24,1024]{2,1,0:T(8,128)(2,1)}, bf16[32,24,1024]{2,1,0:T(8,128)(2,1)S(1)}, u32[]{:S(2)}, u32[]{:S(2)}) collective-permute-start(bf16[32,24,1024]{2,1,0:T(8,128)(2,1)} %all-to-all-done.refs_0_.refs_2_), channel_id=1, source_target_pairs={{0,1},{1,0},{2,3},{3,2},{4,5},{5,4},{6,7},{7,6},{8,9},{9,8},{10,11... | collective-permute-start | bytes 4718600 | tf_op jit(solution)/shard_map/ppermute | solution.py:266
  65.1 1.4 copy-start
  66.6 1.4 copy-start.1
  68.0 1.4 copy-start.2
  69.4 1.0 copy-start.5
  90.6 2.7 %collective-permute-start.3 = (bf16[32,16,1024]{2,1,0:T(8,128)(2,1)S(1)}, bf16[32,16,1024]{2,1,0:T(8,128)(2,1)S(1)}, u32[]{:S(2)}, u32[]{:S(2)}) collective-permute-start(bf16[32,16,1024]{2,1,0:T(8,128)(2,1)S(1)} %get-tuple-element.24), channel_id=1, source_target_pairs={{0,1},{1,0},{2,3},{3,2},{4,5},{5,4},{6,7},{7,6},{8,9},{9,8},{10,11... | collective-permute-start | bytes 3145736 | tf_op jit(solution)/shard_map/ppermute | solution.py:266
  90.7 13.8 %collective-permute-start.8 = (f32[256,64]{1,0:T(8,128)S(1)}, f32[256,64]{1,0:T(8,128)S(1)}, u32[]{:S(2)}, u32[]{:S(2)}) collective-permute-start(f32[256,64]{1,0:T(8,128)S(1)} %get-tuple-element.31.refs_0_), channel_id=1, source_target_pairs={{0,1},{1,0},{2,3},{3,2},{4,5},{5,4},{6,7},{7,6},{8,9},{9,8},{10,11... | collective-permute-start | bytes 196616 | tf_op jit(solution)/shard_map/ppermute | solution.py:266
  94.8 38.6 %all-to-all-start.1 = ((bf16[32,16,1024]{2,1,0:T(8,128)(2,1)}), bf16[32,16,1024]{2,1,0:T(8,128)(2,1)S(1)}, u32[]{:S(2)}, u32[]{:S(2)}) async-start(bf16[32,16,1024]{2,1,0:T(8,128)(2,1)} %add_convert_fusion), calls=%async_computation.1 | async-start | bytes 2097152 | tf_op jit(solution)/shard_map/all_to_all | solution.py:274
  106.2 5.4 %copy-start.4 = (bf16[152,1024]{1,0:T(8,128)(2,1)S(1)}, bf16[152,1024]{1,0:T(8,128)(2,1)}, u32[]{:S(2)}) copy-start(bf16[152,1024]{1,0:T(8,128)(2,1)} %shard_map.147.refs_0_) | copy-start | bytes 933892
  106.2 1.6 %collective-permute-start.9 = (f32[64,1024]{1,0:T(8,128)S(1)}, f32[64,1024]{1,0:T(8,128)S(1)}, u32[]{:S(2)}, u32[]{:S(2)}) collective-permute-start(f32[64,1024]{1,0:T(8,128)S(1)} %shard_map.155), channel_id=1, source_target_pairs={{0,1},{1,0},{2,3},{3,2},{4,5},{5,4},{6,7},{7,6},{8,9},{9,8},{10,11... | collective-permute-start | bytes 786440 | tf_op jit(solution)/shard_map/ppermute | solution.py:266
  107.9 3.2 %copy-start.7 = (f32[64,512]{1,0:T(8,128)}, f32[64,512]{1,0:T(8,128)S(1)}, u32[]{:S(2)}) copy-start(f32[64,512]{1,0:T(8,128)S(1)} %get-tuple-element.45) | copy-start | bytes 393220
  108.0 17.6 %collective-permute-start.10 = (f32[64,2048]{1,0:T(8,128)S(1)}, f32[64,2048]{1,0:T(8,128)}, u32[]{:S(2)}, u32[]{:S(2)}) collective-permute-start(f32[64,2048]{1,0:T(8,128)S(1)} %pad_maximum_fusion.1), channel_id=1, source_target_pairs={{0,2},{2,0},{1,3},{3,1},{4,6},{6,4},{5,7},{7,5},{8,10},{10,8},{9,1... | collective-permute-start | bytes 1572872 | tf_op jit(solution)/shard_map/ppermute | solution.py:266
  111.1 13.8 %collective-permute-start.7 = (f32[64,192]{1,0:T(8,128)S(1)}, f32[64,192]{1,0:T(8,128)S(1)}, u32[]{:S(2)}, u32[]{:S(2)}) collective-permute-start(f32[64,192]{1,0:T(8,128)S(1)} %get-tuple-element.30), channel_id=1, source_target_pairs={{0,2},{2,0},{1,3},{3,1},{4,6},{6,4},{5,7},{7,5},{8,10},{10,8},{9,1... | collective-permute-start | bytes 147464 | tf_op jit(solution)/shard_map/ppermute | solution.py:266
  133.8 7.0 %collective-permute-start.4 = (bf16[2,48,512]{2,1,0:T(8,128)(2,1)S(1)}, bf16[2,48,512]{2,1,0:T(8,128)(2,1)S(1)}, u32[]{:S(2)}, u32[]{:S(2)}) collective-permute-start(bf16[2,48,512]{2,1,0:T(8,128)(2,1)S(1)} %get-tuple-element.26), channel_id=1, source_target_pairs={{0,2},{2,0},{1,3},{3,1},{4,6},{6,4},{5,7},{7,5},{8,10},{10,8},{9,1... | collective-permute-start | bytes 294920 | tf_op jit(solution)/shard_map/ppermute | solution.py:266
  136.9 4.6 %collective-permute-start.5 = (bf16[2,48,512]{2,1,0:T(8,128)(2,1)S(1)}, bf16[2,48,512]{2,1,0:T(8,128)(2,1)S(1)}, u32[]{:S(2)}, u32[]{:S(2)}) collective-permute-start(bf16[2,48,512]{2,1,0:T(8,128)(2,1)S(1)} %get-tuple-element.27), channel_id=1, source_target_pairs={{0,4},{4,0},{1,5},{5,1},{2,6},{6,2},{3,7},{7,3},{8,12},{12,8},{9,1... | collective-permute-start | bytes 294920 | tf_op jit(solution)/shard_map/ppermute | solution.py:266
  137.5 5.8 %collective-permute-start.6 = (bf16[2,48,512]{2,1,0:T(8,128)(2,1)S(1)}, bf16[2,48,512]{2,1,0:T(8,128)(2,1)S(1)}, u32[]{:S(2)}, u32[]{:S(2)}) collective-permute-start(bf16[2,48,512]{2,1,0:T(8,128)(2,1)S(1)} %get-tuple-element.28), channel_id=1, source_target_pairs={{0,6},{2,4},{4,2},{6,0},{1,7},{3,5},{5,3},{7,1},{8,14},{10,12},{12... | collective-permute-start | bytes 294920 | tf_op jit(solution)/shard_map/ppermute | solution.py:270

commit v4 on v3

--- a/solution.py
+++ b/solution.py
@@ -44,7 +44,7 @@
 
     def run(*refs):
         xl, xh = lax.axis_index("xl"), lax.axis_index("xh")
-        body((2 * xl + xh, lax.axis_index("core"), xh), *refs)
+        body((2 * xl + xh, lax.axis_index("core"), xh, xl), *refs)
 
     return pl.pallas_call(
         run,
@@ -172,13 +172,29 @@
         copy.wait()
 
 
-def home_body(where, own, other, member_p, gates_f):
-    meta_a, meta_b = own[META:, :], other[META:, :]
-    member, _ = tables(where, meta_a, meta_b, 0)
-    member_p[...] = member.T.astype(BF)
-    _, gate = tables(where, meta_a, meta_b, 1)
-    for n, piece in enumerate(pieces(gate.T)):
-        gates_f[n] = piece
+def home_body(where, own, out):
+    rows = 2 * ROWS
+    row = lax.broadcasted_iota(jnp.int32, (rows, TOK), 0)
+    expert = (2 * (row // 8) + where[2]).astype(F32)
+    r0 = lax.broadcasted_iota(jnp.int32, (TOK, TOK), 0)
+    r1 = lax.broadcasted_iota(jnp.int32, (TOK, TOK), 1)
+    earlier = jnp.where(r0 < r1, 1.0, 0.0).astype(BF)
+    values = []
+    for n in range(2):
+        part = [own[META:, 128 * (4 * n + p) : 128 * (4 * n + p) + TOK].astype(F32) for p in range(4)]
+        gates = part[1] + part[2] + part[3]
+        named = jnp.zeros((rows, TOK), F32)
+        value = jnp.zeros((rows, TOK), F32)
+        for k in range(8):
+            match = part[0][k : k + 1] == expert
+            named = named + jnp.where(match, 1.0, 0.0)
+            value = value + jnp.where(match, gates[k : k + 1] if n else 1.0, 0.0)
+        position = nn(named.astype(BF), earlier)
+        here = (position == (row % SLOT).astype(F32)) & ((row // SLOT) % 2 == n)
+        values.append(jnp.where(here, value, 0.0).T)
+    out[0] = values[0].astype(BF)
+    for n, piece in enumerate(pieces(values[1])):
+        out[1 + n] = piece
 
 
 def preload_body(where, wg, wu, wd, ad, au, w, small, up, sems):
@@ -192,11 +208,7 @@
     run_all([pltpu.make_async_copy(w2, out, sems.at[0])])
 
 
-def main_body(
-    where, mine, theirs, own, small, up, w2, give, keep, inner, down_grad, down_grad2
-):
-    c = where[1]
-
+def weights_of(own, w2, up=None):
     def weight(*kinds):
         def at(lanes):
             out = []
@@ -205,6 +217,34 @@
             return jnp.concatenate(out, axis=0)
 
         return at
+
+    return weight
+
+
+def expand(where, core, frozen, frozen_w, grads, grads_w, out):
+    first = lax.broadcasted_iota(jnp.int32, (ROWS, Q), 0) % 8 < SLOT
+    xl = where[3]
+    for h in range(2):
+        at = quarter(h, core)
+        a, b = nn(grads, grads_w(at)), nn(frozen, frozen_w(at))
+        near = jnp.where(first, a, pltpu.roll(b, SLOT, 0))
+        far = jnp.where(first, pltpu.roll(a, ROWS - SLOT, 0), b)
+        for plane, total in ((xl, near), (1 - xl, far)):
+            lanes = slice(h * Q, (h + 1) * Q)
+            out[:, pl.ds(plane, 1), :, lanes] = total.astype(BF).reshape(PEERS, 1, 8, Q)
+
+
+def keep_body(where, frozen, grads, own, w2, keep):
+    weight = weights_of(own, w2)
+    expand(where, where[1], frozen[...], weight(2), grads[...], weight(0, 1), keep)
+
+
+def main_body(
+    where, mine, theirs, own, small, up, w2, give, frozen, grads, inner, down_grad, down_grad2
+):
+    c = where[1]
+
+    weight = weights_of(own, w2, up)
 
     def dot(i, w):
         total = None
@@ -215,16 +255,10 @@
                 total = part if total is None else total + part
         return total
 
-    def expand(x, w, i):
-        for out, core in ((give, 1 - c), (keep, c)):
-            for h in range(2):
-                total = nn(x, w(quarter(h, core))).astype(BF).reshape(PEERS, 8, Q)
-                out[:, 8 * i : 8 * i + 8, h * Q : (h + 1) * Q] = total
-
     both, down, down_up = weight(0, 1), weight(2), weight(2, 3)
     pre = dot(1, both)
     gate_pre, up_pre = pre[:, :384], pre[:, 384:]
-    expand((gate_pre * jax.nn.sigmoid(gate_pre) * up_pre).astype(BF), down, 1)
+    frozen[...] = (gate_pre * jax.nn.sigmoid(gate_pre) * up_pre).astype(BF)
     tail = [w2[576:584, 256 * k : 256 * k + 192] for k in range(8)]
     adapters = jnp.concatenate([small[...], jnp.concatenate(tail, axis=0)], axis=1)
     pre = dot(0, both)
@@ -236,13 +270,26 @@
     inner[...] = nt(hidden, adapters)
     pre = dot(2, down_up)
     inner_grad = (SCALE * pre[:, 384:]).astype(BF)
-    grads = tn(inner_grad, hidden)
-    down_grad[...] = grads[:, :192]
-    down_grad2[...] = grads[:, 192:]
+    adapter_grads = tn(inner_grad, hidden)
+    down_grad[...] = adapter_grads[:, :192]
+    down_grad2[...] = adapter_grads[:, 192:]
     hidden_grad = pre[:, :384] + nn(inner_grad, adapters)
     gate_grad = (hidden_grad * slope).astype(BF)
     up_grad = (hidden_grad * activated).astype(BF)
-    expand(jnp.concatenate([gate_grad, up_grad], axis=1), both, 0)
+    both_grads = jnp.concatenate([gate_grad, up_grad], axis=1)
+    grads[...] = both_grads
+    expand(where, 1 - c, frozen[...], down, both_grads, both, give)
+
+
+def finish_body(where, keep, got, out, stage, sems):
+    copies = []
+    for n in range(4):
+        at = slice(8 * n, 8 * n + 8)
+        stage[at] = (keep[at].astype(F32) + got[at].astype(F32)).astype(BF)
+        copies.append(pltpu.make_async_copy(stage.at[at], out.at[at], sems.at[n]))
+        copies[-1].start()
+    for copy in copies:
+        copy.wait()
 
 
 def up_body(where, inner_a, inner_b, cot, out):
@@ -250,28 +297,23 @@
     out[...] = SCALE * tn(inner, cot[:, 16:24, :].reshape(ROWS, 2 * Q))
 
 
-def combine_body(where, member, gates, back, own, to_xh, to_xl, to_both):
-    for at, near, far in ((where[2], own, to_xl), (1 - where[2], to_xh, to_both)):
-        lanes = pl.ds(pl.multiple_of(at * Q, Q), Q)
-        grads = back[:, 0:8, lanes].reshape(ROWS, Q)
-        frozen = back[:, 8:16, lanes].reshape(ROWS, Q)
-        frozen = nn(gates[2], frozen) + nn(gates[1], frozen) + nn(gates[0], frozen)
-        grads = nn(member[...], grads)
-        for n, total in enumerate((frozen, grads)):
-            near[n] = total[:TOK].astype(near.dtype)
-            far[n] = total[TOK:].astype(far.dtype)
+def combine_body(where, table, back, own, to_xh):
+    for at, out in ((where[2], own), (1 - where[2], to_xh)):
+        rows = back[:, :, pl.ds(pl.multiple_of(at * Q, Q), Q)].reshape(2 * ROWS, Q)
+        out[0] = (nn(table[3], rows) + nn(table[2], rows) + nn(table[1], rows)).astype(out.dtype)
+        out[1] = nn(table[0], rows).astype(out.dtype)
 
 
 def swap(x, axis):
     return lax.ppermute(x, axis, [(0, 1), (1, 0)])
 
 
-def swap_both(x):
-    return lax.ppermute(x, ("xl", "xh"), [(i, 3 - i) for i in range(4)])
-
-
 def exchange(x):
     return lax.all_to_all(x, ("y", "z"), split_axis=0, concat_axis=0, tiled=True)
+
+
+def exchange_home(x):
+    return lax.all_to_all(x, ("y", "z", "xl"), split_axis=0, concat_axis=0, tiled=True)
 
 
 def pick(c, a, b):
@@ -303,10 +345,7 @@
         [pltpu.VMEM((PEERS, 24, 2 * Q), BF), pltpu.SemaphoreType.DMA((3,))], "vv", "h",
         limit=12 << 20,
     )
-    member_p, gates_f = vmem_call(
-        home_body, [sds((2 * TOK, ROWS), BF), sds((3, 2 * TOK, ROWS), BF)],
-        [own, other], flops=10**8, mib=8,
-    )
+    (table,) = vmem_call(home_body, [sds((4, TOK, 2 * ROWS), BF)], [own], mib=8)
     mine = exchange(sent)
     theirs = swap(mine, "core")
     own_w, small, up = kernel(
@@ -317,22 +356,23 @@
         arrive_body, [sds((584, 4 * Q), BF)], [w2], [pltpu.SemaphoreType.DMA((1,))],
         "h", "v", limit=8 << 20,
     )
-    wide = sds((PEERS, 16, 2 * Q), BF)
-    give, keep, inner, down_grad, down_grad2 = kernel(
+    wide = sds((PEERS, 2, 8, 2 * Q), BF)
+    give, frozen, grads, inner, down_grad, down_grad2 = kernel(
         main_body,
-        [wide, wide, sds((ROWS, 64), F32), sds((64, 192), F32), sds((64, 192), F32)],
-        [mine, theirs, own_w, small, up, w2], [], "vvvvvv", "vvvvv", flops=4 * 10**9, limit=28 << 20,
-    )
-    total = (keep.astype(F32) + swap(give, "core").astype(F32)).astype(BF)
-    back = exchange(total)
-    own, to_xh, to_xl, to_both = vmem_call(
-        combine_body, [sds((2, TOK, Q), F32)] + [sds((2, TOK, Q), BF)] * 3,
-        [member_p, gates_f, back], flops=10**8, mib=8,
-    )
+        [wide, sds((ROWS, 384), BF), sds((ROWS, 768), BF),
+         sds((ROWS, 64), F32), sds((64, 192), F32), sds((64, 192), F32)],
+        [mine, theirs, own_w, small, up, w2], [], "vvvvvv", "vvvvvv", flops=4 * 10**9, limit=28 << 20,
+    )
+    got = swap(give, "core")
+    (keep,) = kernel(keep_body, [wide], [frozen, grads, own_w, w2], [], "vvvv", "v", flops=10**9, limit=20 << 20)
+    (total,) = kernel(
+        finish_body, [wide], [keep, got],
+        [pltpu.VMEM(wide.shape, BF), pltpu.SemaphoreType.DMA((4,))], "vv", "h", limit=48 << 20,
+    )
+    back = exchange_home(total.reshape(2 * PEERS, 8, 2 * Q))
+    here, to_xh = vmem_call(combine_body, [sds((2, TOK, Q), F32), sds((2, TOK, Q), BF)], [table, back], mib=8)
     from_xh = swap(to_xh, "xh")
-    from_xl = swap(to_xl, "xl")
-    from_both = swap_both(to_both)
-    outs = own + from_xh.astype(F32) + from_xl.astype(F32) + from_both.astype(F32)
+    outs = here + from_xh.astype(F32)
     frozen_out, input_grad = outs[0].astype(BF), outs[1].astype(BF)
 
     (up_half,) = vmem_call(

time: 145 us -> 144 us (level)
  Pallas kernels: 17 us -> 19.2 us
    all_to_all x0 -> x1, starting transfers between devices: none -> 11.1 us  [exchange_home(): lax.all_to_all(x, ('y', 'z', 'xl'), split_axis=0, concat_axis=0, tiled=True)]
    all_to_all x2 -> x1, starting transfers between devices: 21.2 us -> 11.4 us  [exchange(): lax.all_to_all(x, ('y', 'z'), split_axis=0, concat_axis=0, tiled=True)]
    ppermute x10 -> x9, waiting for transfers between devices: 39.5 us -> 48.3 us  [swap(): return lax.ppermute(x, axis, [(0, 1), (1, 0)])]
    all_to_all x2 -> x1, waiting for transfers between devices: 39.1 us -> 32.5 us  [exchange(): lax.all_to_all(x, ('y', 'z'), split_axis=0, concat_axis=0, tiled=True)]
    pallas_call x9 -> x11, Pallas kernels: 17 us -> 19.2 us  [kernel(): pl.pallas_call(run, out_shape=outs, in_specs=[SPACES[x] for x in ins], ou...]
    ppermute x1 -> x0, waiting for transfers between devices: 1.78 us -> none  [swap_both(): return lax.ppermute(x, ('xl', 'xh'), [(i, 3 - i) for i in range(4)])]
    ppermute x10 -> x9, starting transfers between devices: 12.7 us -> 11.1 us  [swap(): return lax.ppermute(x, axis, [(0, 1), (1, 0)])]
    unnamed x16 -> x14, local copies, waits for them, and re-layouts: 6.24 us -> 5.2 us
  transfers between devices with their start and end apart: 13 -> 11, of which waited for: 10 -> 7; matrix products, arithmetic and copies ran while one was open for 3% -> 2% of each run, Pallas kernels for 4% -> 5%
where the time goes in v4:
time: 144 us; the launch traced here: 143 us
  waiting for transfers between devices  80.8 us (56%)
  starting transfers between devices  33.7 us (23%)
  Pallas kernels  19.2 us (13%)
  local copies, waits for them, and re-layouts  5.88 us (4%)
  other arithmetic  2.98 us (2%)
    ppermute x9, waiting for transfers between devices, swap(): return lax.ppermute(x, axis, [(0, 1), (1, 0)])  48.3 us
    all_to_all x1, waiting for transfers between devices, exchange(): lax.all_to_all(x, ('y', 'z'), split_axis=0, concat_axis=0, tiled=True)  32.5 us
    pallas_call x11, Pallas kernels, kernel(): pl.pallas_call(run, out_shape=outs, in_specs=[SPACES[x] for x in ins], ou...  19.2 us
    all_to_all x1, starting transfers between devices, exchange(): lax.all_to_all(x, ('y', 'z'), split_axis=0, concat_axis=0, tiled=True)  11.4 us
    ppermute x9, starting transfers between devices, swap(): return lax.ppermute(x, axis, [(0, 1), (1, 0)])  11.1 us
    all_to_all x1, starting transfers between devices, exchange_home(): lax.all_to_all(x, ('y', 'z', 'xl'), split_axis=0, concat_axis=0, tiled=True)  11.1 us
    unnamed x14, local copies, waits for them, and re-layouts  5.2 us
  transfers between devices with their start and end apart: 11, of which 7 were waited for; matrix products, arithmetic and copies ran while one was open for 2% of the time, Pallas kernels for 5%

profile of v4, /device:TPU:32, one launch (start us, length us, event | category | flops | bytes accessed | tf_op | source)
XLA Modules:
  0.0 143.4 jit_solution(3088530238147493686)
XLA Ops:
  0.6 2.5 %shard_map.147.refs_0_ = bf16[152,1024]{1,0:T(8,128)(2,1)} custom-call(bf16[48,2048]{1,0:T(8,128)(2,1)} %refs_0_.1, bf16[48,2048]{1,0:T(8,128)(2,1)} %refs_1_.1, bf16[48,2048]{1,0:T(8,128)(2,1)} %refs_2_.3, s32[8,48]{1,0:T(8,128)} %bitcast.28, f32[8,48]{1,0:T(8,128)} %bitcast.29, s32[8,48]{1,0:T(8,128)} %bitcast.30, f32[8,48]{1,0:T(8,128)} %bitcast.31), custom_call_target="tpu_custom_call" | custom-call | flops 100000000 | bytes 907264 | tf_op jit(solution)/shard_map/pallas_call | solution.py:49
  3.1 1.6 %collective-permute-start = (bf16[152,1024]{1,0:T(8,128)(2,1)}, bf16[152,1024]{1,0:T(8,128)(2,1)S(1)}, u32[]{:S(2)}, u32[]{:S(2)}) collective-permute-start(bf16[152,1024]{1,0:T(8,128)(2,1)} %shard_map.147.refs_0_), channel_id=1, source_target_pairs={{0,4},{4,0},{1,5},{5,1},{2,6},{6,2},{3,7},{7,3},{8,12},{12,8},{9,1... | collective-permute-start | bytes 933896 | tf_op jit(solution)/shard_map/ppermute | solution.py:308
  4.7 7.8 %collective-permute-done.refs_1_ = bf16[152,1024]{1,0:T(8,128)(2,1)S(1)} collective-permute-done((bf16[152,1024]{1,0:T(8,128)(2,1)}, bf16[152,1024]{1,0:T(8,128)(2,1)S(1)}, u32[]{:S(2)}, u32[]{:S(2)}) %collective-permute-start) | collective-permute-done | bytes 311328 | tf_op jit(solution)/shard_map/ppermute | solution.py:308
  12.5 1.0 copy-done.3
  13.5 1.8 %shard_map.149 = bf16[32,24,1024]{2,1,0:T(8,128)(2,1)} custom-call(bf16[152,1024]{1,0:T(8,128)(2,1)S(1)} %copy-done.3, bf16[152,1024]{1,0:T(8,128)(2,1)S(1)} %collective-permute-done.refs_1_), custom_call_target="tpu_custom_call" | custom-call | flops 100000000 | bytes 2195456 | tf_op jit(solution)/shard_map/pallas_call | solution.py:49
  15.3 11.4 %all-to-all-start = ((bf16[32,24,1024]{2,1,0:T(8,128)(2,1)}), bf16[32,24,1024]{2,1,0:T(8,128)(2,1)}, u32[]{:S(2)}, u32[]{:S(2)}) async-start(bf16[32,24,1024]{2,1,0:T(8,128)(2,1)} %shard_map.149), calls=%async_computation | async-start | bytes 3145728 | tf_op jit(solution)/shard_map/all_to_all | solution.py:312
  26.8 2.8 %shard_map.151 = bf16[584,2048]{1,0:T(8,128)(2,1)} custom-call(bf16[2,192,2048]{2,1,0:T(8,128)(2,1)} %bitcast.22, bf16[2,192,2048]{2,1,0:T(8,128)(2,1)} %bitcast.24, bf16[2,192,2048]{2,1,0:T(8,128)(2,1)} %refs_2_.5, bf16[2,64,192]{2,1,0:T(8,128)(2,1)} %bitcast.26), custom_call_target="tpu_custom_call" | custom-call | flops 100000000 | bytes 7159808 | tf_op jit(solution)/shard_map/pallas_call | solution.py:49
  29.5 3.1 %collective-permute-start.2 = (bf16[584,2048]{1,0:T(8,128)(2,1)}, bf16[584,2048]{1,0:T(8,128)(2,1)S(1)}, u32[]{:S(2)}, u32[]{:S(2)}) collective-permute-start(bf16[584,2048]{1,0:T(8,128)(2,1)} %shard_map.151), channel_id=1, source_target_pairs={{0,2},{2,0},{1,3},{3,1},{4,6},{6,4},{5,7},{7,5},{8,10},{10,8},{9,1... | collective-permute-start | bytes 7176200 | tf_op jit(solution)/shard_map/ppermute | solution.py:308
  32.6 32.5 %all-to-all-done.refs_0_.refs_2_ = bf16[32,24,1024]{2,1,0:T(8,128)(2,1)} async-done(((bf16[32,24,1024]{2,1,0:T(8,128)(2,1)}), bf16[32,24,1024]{2,1,0:T(8,128)(2,1)}, u32[]{:S(2)}, u32[]{:S(2)}) %all-to-all-start) | async-done | bytes 1572896 | tf_op jit(solution)/shard_map/all_to_all | solution.py:312
  65.2 1.4 copy-done
  66.6 1.4 copy-done.1
  68.0 1.4 copy-done.2
  69.7 13.9 %collective-permute-done.2.refs_0_ = bf16[584,2048]{1,0:T(8,128)(2,1)S(1)} collective-permute-done((bf16[584,2048]{1,0:T(8,128)(2,1)}, bf16[584,2048]{1,0:T(8,128)(2,1)S(1)}, u32[]{:S(2)}, u32[]{:S(2)}) %collective-permute-start.2) | collective-permute-done | bytes 2392096 | tf_op jit(solution)/shard_map/ppermute | solution.py:308
  83.8 6.3 %shard_map.153 = (bf16[32,2,8,1024]{3,2,1,0:T(8,128)(2,1)S(1)}, bf16[256,384]{1,0:T(8,128)(2,1)S(1)}, bf16[256,768]{1,0:T(8,128)(2,1)S(1)}, f32[256,64]{1,0:T(8,...) custom-call(bf16[32,24,1024]{2,1,0:T(8,128)(2,1)} %all-to-all-done.refs_0_.refs_2_, ...), custom_call_target="tpu_custom_call" | custom-call | flops 4000000000 | bytes 9986048 | tf_op jit(solution)/shard_map/pallas_call | solution.py:49
  90.2 0.5 collective-permute-start.6
  90.7 1.0 shard_map.154.refs_0_
  91.7 1.1 collective-permute-done.3.refs_1_
  92.9 1.1 shard_map.155
  93.9 11.1 %all-to-all-start.1 = ((bf16[64,8,1024]{2,1,0:T(8,128)(2,1)}), bf16[64,8,1024]{2,1,0:T(8,128)(2,1)S(1)}, u32[]{:S(2)}, u32[]{:S(2)}) async-start(bf16[64,8,1024]{2,1,0:T(8,128)(2,1)} %bitcast.7), calls=%async_computation.1 | async-start | bytes 2097152 | tf_op jit(solution)/shard_map/all_to_all | solution.py:316
  105.1 1.6 %shard_map.157 = f32[64,1024]{1,0:T(8,128)S(1)} custom-call(f32[256,64]{1,0:T(8,128)S(1)} %get-tuple-element.25.refs_0_, f32[256,64]{1,0:T(8,128)S(1)} %collective-permute-done.6.refs_1_, bf16[32,24,1024]{2,1,0:T(8,128)(2,1)} %all-to-all-done.refs_0_.refs_2_), custom_call_target="tpu_custom_call" | custom-call | flops 100000000 | bytes 1966080 | tf_op jit(solution)/shard_map/pallas_call | solution.py:49
  106.9 1.5 %collective-permute-done.7 = f32[64,1024]{1,0:T(8,128)S(1)} collective-permute-done((f32[64,1024]{1,0:T(8,128)S(1)}, f32[64,1024]{1,0:T(8,128)S(1)}, u32[]{:S(2)}, u32[]{:S(2)}) %collective-permute-start.7) | collective-permute-done | bytes 262176 | tf_op jit(solution)/shard_map/ppermute | solution.py:308
  108.5 2.8 %collective-permute-start.8 = (f32[64,2048]{1,0:T(8,128)S(1)}, f32[64,2048]{1,0:T(8,128)}, u32[]{:S(2)}, u32[]{:S(2)}) collective-permute-start(f32[64,2048]{1,0:T(8,128)S(1)} %pad_maximum_fusion.1), channel_id=1, source_target_pairs={{0,2},{2,0},{1,3},{3,1},{4,6},{6,4},{5,7},{7,5},{8,10},{10,8},{9,1... | collective-permute-start | bytes 1572872 | tf_op jit(solution)/shard_map/ppermute | solution.py:308
  111.3 0.8 collective-permute-start.5
  112.1 0.8 shard_map.148.refs_0_
  113.0 20.9 %collective-permute-done.5 = f32[64,192]{1,0:T(8,128)S(1)} collective-permute-done((f32[64,192]{1,0:T(8,128)S(1)}, f32[64,192]{1,0:T(8,128)S(1)}, u32[]{:S(2)}, u32[]{:S(2)}) %collective-permute-start.5) | collective-permute-done | bytes 49184 | tf_op jit(solution)/shard_map/ppermute | solution.py:308
  133.9 0.7 maximum_bitcast_fusion
  134.6 1.1 select_bitcast_fusion.1
  135.7 0.8 shard_map.156
  136.6 2.1 %collective-permute-start.4 = (bf16[2,48,512]{2,1,0:T(8,128)(2,1)S(1)}, bf16[2,48,512]{2,1,0:T(8,128)(2,1)S(1)}, u32[]{:S(2)}, u32[]{:S(2)}) collective-permute-start(bf16[2,48,512]{2,1,0:T(8,128)(2,1)S(1)} %get-tuple-element.22), channel_id=1, source_target_pairs={{0,2},{2,0},{1,3},{3,1},{4,6},{6,4},{5,7},{7,5},{8,10},{10,8},{9,1... | collective-permute-start | bytes 294920 | tf_op jit(solution)/shard_map/ppermute | solution.py:308
  138.7 1.1 pad_maximum_fusion
  139.8 3.0 %collective-permute-done.4 = bf16[2,48,512]{2,1,0:T(8,128)(2,1)S(1)} collective-permute-done((bf16[2,48,512]{2,1,0:T(8,128)(2,1)S(1)}, bf16[2,48,512]{2,1,0:T(8,128)(2,1)S(1)}, u32[]{:S(2)}, u32[]{:S(2)}) %collective-permute-start.4) | collective-permute-done | bytes 98336 | tf_op jit(solution)/shard_map/ppermute | solution.py:308
  142.8 0.6 slice_bitcast_fusion
  (24 shorter events, 0.9 us)
Async XLA Ops:
  3.1 9.4 %collective-permute-start = (bf16[152,1024]{1,0:T(8,128)(2,1)}, bf16[152,1024]{1,0:T(8,128)(2,1)S(1)}, u32[]{:S(2)}, u32[]{:S(2)}) collective-permute-start(bf16[152,1024]{1,0:T(8,128)(2,1)} %shard_map.147.refs_0_), channel_id=1, source_target_pairs={{0,4},{4,0},{1,5},{5,1},{2,6},{6,2},{3,7},{7,3},{8,12},{12,8},{9,1... | collective-permute-start | bytes 933896 | tf_op jit(solution)/shard_map/ppermute | solution.py:308
  12.5 1.0 copy-start.3
  15.3 49.9 %all-to-all-start = ((bf16[32,24,1024]{2,1,0:T(8,128)(2,1)}), bf16[32,24,1024]{2,1,0:T(8,128)(2,1)}, u32[]{:S(2)}, u32[]{:S(2)}) async-start(bf16[32,24,1024]{2,1,0:T(8,128)(2,1)} %shard_map.149), calls=%async_computation | async-start | bytes 3145728 | tf_op jit(solution)/shard_map/all_to_all | solution.py:312
  26.7 38.5 %copy-start.5 = (bf16[2,64,2048]{2,1,0:T(8,128)(2,1)S(1)}, bf16[2,64,2048]{2,1,0:T(8,128)(2,1)}, u32[]{:S(2)}) copy-start(bf16[2,64,2048]{2,1,0:T(8,128)(2,1)} %refs_4_.1) | copy-start | bytes 1572868
  26.7 38.5 %copy-start.6 = (bf16[2,192,64]{1,2,0:T(8,128)(2,1)S(1)}, bf16[2,192,64]{1,2,0:T(8,128)(2,1)}, u32[]{:S(2)}) copy-start(bf16[2,192,64]{1,2,0:T(8,128)(2,1)} %param.22) | copy-start | bytes 147460
  29.5 54.1 %collective-permute-start.2 = (bf16[584,2048]{1,0:T(8,128)(2,1)}, bf16[584,2048]{1,0:T(8,128)(2,1)S(1)}, u32[]{:S(2)}, u32[]{:S(2)}) collective-permute-start(bf16[584,2048]{1,0:T(8,128)(2,1)} %shard_map.151), channel_id=1, source_target_pairs={{0,2},{2,0},{1,3},{3,1},{4,6},{6,4},{5,7},{7,5},{8,10},{10,8},{9,1... | collective-permute-start | bytes 7176200 | tf_op jit(solution)/shard_map/ppermute | solution.py:308
  65.2 18.6 %collective-permute-start.1 = (bf16[32,24,1024]{2,1,0:T(8,128)(2,1)}, bf16[32,24,1024]{2,1,0:T(8,128)(2,1)S(1)}, u32[]{:S(2)}, u32[]{:S(2)}) collective-permute-start(bf16[32,24,1024]{2,1,0:T(8,128)(2,1)} %all-to-all-done.refs_0_.refs_2_), channel_id=1, source_target_pairs={{0,1},{1,0},{2,3},{3,2},{4,5},{5,4},{6,7},{7,6},{8,9},{9,8},{10,11... | collective-permute-start | bytes 4718600 | tf_op jit(solution)/shard_map/ppermute | solution.py:308
  65.2 1.4 copy-start
  66.6 1.4 copy-start.1
  68.0 1.4 copy-start.2
  90.1 2.7 %collective-permute-start.3 = (bf16[32,2,8,1024]{3,2,1,0:T(8,128)(2,1)S(1)}, bf16[32,2,8,1024]{3,2,1,0:T(8,128)(2,1)S(1)}, u32[]{:S(2)}, u32[]{:S(2)}) collective-permute-start(bf16[32,2,8,1024]{3,2,1,0:T(8,128)(2,1)S(1)} %get-tuple-element.20), channel_id=1, source_target_pairs={{0,1},{1,0},{2,3},{3,2},{4,5},{5,4},{6,7},{7,6},{8,9},{9,8},{10,11... | collective-permute-start | bytes 3145736 | tf_op jit(solution)/shard_map/ppermute | solution.py:308
  90.2 14.9 %collective-permute-start.6 = (f32[256,64]{1,0:T(8,128)S(1)}, f32[256,64]{1,0:T(8,128)S(1)}, u32[]{:S(2)}, u32[]{:S(2)}) collective-permute-start(f32[256,64]{1,0:T(8,128)S(1)} %get-tuple-element.25.refs_0_), channel_id=1, source_target_pairs={{0,1},{1,0},{2,3},{3,2},{4,5},{5,4},{6,7},{7,6},{8,9},{9,8},{10,11... | collective-permute-start | bytes 196616 | tf_op jit(solution)/shard_map/ppermute | solution.py:308
  93.9 41.8 %all-to-all-start.1 = ((bf16[64,8,1024]{2,1,0:T(8,128)(2,1)}), bf16[64,8,1024]{2,1,0:T(8,128)(2,1)S(1)}, u32[]{:S(2)}, u32[]{:S(2)}) async-start(bf16[64,8,1024]{2,1,0:T(8,128)(2,1)} %bitcast.7), calls=%async_computation.1 | async-start | bytes 2097152 | tf_op jit(solution)/shard_map/all_to_all | solution.py:316
  106.7 1.6 %collective-permute-start.7 = (f32[64,1024]{1,0:T(8,128)S(1)}, f32[64,1024]{1,0:T(8,128)S(1)}, u32[]{:S(2)}, u32[]{:S(2)}) collective-permute-start(f32[64,1024]{1,0:T(8,128)S(1)} %shard_map.157), channel_id=1, source_target_pairs={{0,1},{1,0},{2,3},{3,2},{4,5},{5,4},{6,7},{7,6},{8,9},{9,8},{10,11... | collective-permute-start | bytes 786440 | tf_op jit(solution)/shard_map/ppermute | solution.py:308
  106.8 5.3 %copy-start.4 = (bf16[152,1024]{1,0:T(8,128)(2,1)S(1)}, bf16[152,1024]{1,0:T(8,128)(2,1)}, u32[]{:S(2)}) copy-start(bf16[152,1024]{1,0:T(8,128)(2,1)} %shard_map.147.refs_0_) | copy-start | bytes 933892
  108.5 26.1 %collective-permute-start.8 = (f32[64,2048]{1,0:T(8,128)S(1)}, f32[64,2048]{1,0:T(8,128)}, u32[]{:S(2)}, u32[]{:S(2)}) collective-permute-start(f32[64,2048]{1,0:T(8,128)S(1)} %pad_maximum_fusion.1), channel_id=1, source_target_pairs={{0,2},{2,0},{1,3},{3,1},{4,6},{6,4},{5,7},{7,5},{8,10},{10,8},{9,1... | collective-permute-start | bytes 1572872 | tf_op jit(solution)/shard_map/ppermute | solution.py:308
  111.3 22.6 %collective-permute-start.5 = (f32[64,192]{1,0:T(8,128)S(1)}, f32[64,192]{1,0:T(8,128)S(1)}, u32[]{:S(2)}, u32[]{:S(2)}) collective-permute-start(f32[64,192]{1,0:T(8,128)S(1)} %get-tuple-element.24), channel_id=1, source_target_pairs={{0,2},{2,0},{1,3},{3,1},{4,6},{6,4},{5,7},{7,5},{8,10},{10,8},{9,1... | collective-permute-start | bytes 147464 | tf_op jit(solution)/shard_map/ppermute | solution.py:308
  136.6 6.2 %collective-permute-start.4 = (bf16[2,48,512]{2,1,0:T(8,128)(2,1)S(1)}, bf16[2,48,512]{2,1,0:T(8,128)(2,1)S(1)}, u32[]{:S(2)}, u32[]{:S(2)}) collective-permute-start(bf16[2,48,512]{2,1,0:T(8,128)(2,1)S(1)} %get-tuple-element.22), channel_id=1, source_target_pairs={{0,2},{2,0},{1,3},{3,1},{4,6},{6,4},{5,7},{7,5},{8,10},{10,8},{9,1... | collective-permute-start | bytes 294920 | tf_op jit(solution)/shard_map/ppermute | solution.py:308

commit v5 on v4

--- a/solution.py
+++ b/solution.py
@@ -292,6 +292,11 @@
         copy.wait()
 
 
+def last_body(where, here, there, frozen_out, input_grad):
+    for n, out in enumerate((frozen_out, input_grad)):
+        out[...] = (here[n] + there[n].astype(F32)).astype(BF)
+
+
 def up_body(where, inner_a, inner_b, cot, out):
     inner = (inner_a[...] + inner_b[...]).astype(BF)
     out[...] = SCALE * tn(inner, cot[:, 16:24, :].reshape(ROWS, 2 * Q))
@@ -372,8 +377,7 @@
     back = exchange_home(total.reshape(2 * PEERS, 8, 2 * Q))
     here, to_xh = vmem_call(combine_body, [sds((2, TOK, Q), F32), sds((2, TOK, Q), BF)], [table, back], mib=8)
     from_xh = swap(to_xh, "xh")
-    outs = here + from_xh.astype(F32)
-    frozen_out, input_grad = outs[0].astype(BF), outs[1].astype(BF)
+    frozen_out, input_grad = vmem_call(last_body, [sds((TOK, Q), BF)] * 2, [here, from_xh], mib=4)
 
     (up_half,) = vmem_call(
         up_body, [sds((64, 2 * Q), F32)], [inner, swap(inner, "core"), mine],

time: 144 us -> 144 us (level)
    pallas_call x11 -> x12, Pallas kernels: 19.2 us -> 19.8 us  [kernel(): pl.pallas_call(run, out_shape=outs, in_specs=[SPACES[x] for x in ins], ou...]
where the time goes in v5:
time: 144 us; the launch traced here: 143 us
  waiting for transfers between devices  80.8 us (56%)
  starting transfers between devices  33.7 us (23%)
  Pallas kernels  19.8 us (14%)
  local copies, waits for them, and re-layouts  5.24 us (4%)
  other arithmetic  2.96 us (2%)
    ppermute x9, waiting for transfers between devices, swap(): return lax.ppermute(x, axis, [(0, 1), (1, 0)])  48.3 us
    all_to_all x1, waiting for transfers between devices, exchange(): lax.all_to_all(x, ('y', 'z'), split_axis=0, concat_axis=0, tiled=True)  32.5 us
    pallas_call x12, Pallas kernels, kernel(): pl.pallas_call(run, out_shape=outs, in_specs=[SPACES[x] for x in ins], ou...  19.8 us
    all_to_all x1, starting transfers between devices, exchange(): lax.all_to_all(x, ('y', 'z'), split_axis=0, concat_axis=0, tiled=True)  11.4 us
    ppermute x9, starting transfers between devices, swap(): return lax.ppermute(x, axis, [(0, 1), (1, 0)])  11.1 us
    all_to_all x1, starting transfers between devices, exchange_home(): lax.all_to_all(x, ('y', 'z', 'xl'), split_axis=0, concat_axis=0, tiled=True)  11.1 us
    unnamed x14, local copies, waits for them, and re-layouts  5.2 us
  transfers between devices with their start and end apart: 11, of which 7 were waited for; matrix products, arithmetic and copies ran while one was open for 2% of the time, Pallas kernels for 5%

profile of v5, /device:TPU:32, one launch (start us, length us, event | category | flops | bytes accessed | tf_op | source)
XLA Modules:
  0.0 143.4 jit_solution(12894681610106652801)
XLA Ops:
  0.6 2.5 %shard_map.147.refs_0_ = bf16[152,1024]{1,0:T(8,128)(2,1)} custom-call(bf16[48,2048]{1,0:T(8,128)(2,1)} %refs_0_.1, bf16[48,2048]{1,0:T(8,128)(2,1)} %refs_1_.1, bf16[48,2048]{1,0:T(8,128)(2,1)} %refs_2_.3, s32[8,48]{1,0:T(8,128)} %bitcast.24, f32[8,48]{1,0:T(8,128)} %bitcast.25, s32[8,48]{1,0:T(8,128)} %bitcast.26, f32[8,48]{1,0:T(8,128)} %bitcast.27), custom_call_target="tpu_custom_call" | custom-call | flops 100000000 | bytes 907264 | tf_op jit(solution)/shard_map/pallas_call | solution.py:49
  3.1 1.6 %collective-permute-start = (bf16[152,1024]{1,0:T(8,128)(2,1)}, bf16[152,1024]{1,0:T(8,128)(2,1)S(1)}, u32[]{:S(2)}, u32[]{:S(2)}) collective-permute-start(bf16[152,1024]{1,0:T(8,128)(2,1)} %shard_map.147.refs_0_), channel_id=1, source_target_pairs={{0,4},{4,0},{1,5},{5,1},{2,6},{6,2},{3,7},{7,3},{8,12},{12,8},{9,1... | collective-permute-start | bytes 933896 | tf_op jit(solution)/shard_map/ppermute | solution.py:313
  4.7 7.8 %collective-permute-done.refs_1_ = bf16[152,1024]{1,0:T(8,128)(2,1)S(1)} collective-permute-done((bf16[152,1024]{1,0:T(8,128)(2,1)}, bf16[152,1024]{1,0:T(8,128)(2,1)S(1)}, u32[]{:S(2)}, u32[]{:S(2)}) %collective-permute-start) | collective-permute-done | bytes 311328 | tf_op jit(solution)/shard_map/ppermute | solution.py:313
  12.5 1.0 copy-done.3
  13.5 1.8 %shard_map.149 = bf16[32,24,1024]{2,1,0:T(8,128)(2,1)} custom-call(bf16[152,1024]{1,0:T(8,128)(2,1)S(1)} %copy-done.3, bf16[152,1024]{1,0:T(8,128)(2,1)S(1)} %collective-permute-done.refs_1_), custom_call_target="tpu_custom_call" | custom-call | flops 100000000 | bytes 2195456 | tf_op jit(solution)/shard_map/pallas_call | solution.py:49
  15.3 11.4 %all-to-all-start = ((bf16[32,24,1024]{2,1,0:T(8,128)(2,1)}), bf16[32,24,1024]{2,1,0:T(8,128)(2,1)}, u32[]{:S(2)}, u32[]{:S(2)}) async-start(bf16[32,24,1024]{2,1,0:T(8,128)(2,1)} %shard_map.149), calls=%async_computation | async-start | bytes 3145728 | tf_op jit(solution)/shard_map/all_to_all | solution.py:317
  26.8 2.8 %shard_map.151 = bf16[584,2048]{1,0:T(8,128)(2,1)} custom-call(bf16[2,192,2048]{2,1,0:T(8,128)(2,1)} %bitcast.18, bf16[2,192,2048]{2,1,0:T(8,128)(2,1)} %bitcast.20, bf16[2,192,2048]{2,1,0:T(8,128)(2,1)} %refs_2_.5, bf16[2,64,192]{2,1,0:T(8,128)(2,1)} %bitcast.22), custom_call_target="tpu_custom_call" | custom-call | flops 100000000 | bytes 7159808 | tf_op jit(solution)/shard_map/pallas_call | solution.py:49
  29.5 3.1 %collective-permute-start.2 = (bf16[584,2048]{1,0:T(8,128)(2,1)}, bf16[584,2048]{1,0:T(8,128)(2,1)S(1)}, u32[]{:S(2)}, u32[]{:S(2)}) collective-permute-start(bf16[584,2048]{1,0:T(8,128)(2,1)} %shard_map.151), channel_id=1, source_target_pairs={{0,2},{2,0},{1,3},{3,1},{4,6},{6,4},{5,7},{7,5},{8,10},{10,8},{9,1... | collective-permute-start | bytes 7176200 | tf_op jit(solution)/shard_map/ppermute | solution.py:313
  32.6 32.5 %all-to-all-done.refs_0_.refs_2_ = bf16[32,24,1024]{2,1,0:T(8,128)(2,1)} async-done(((bf16[32,24,1024]{2,1,0:T(8,128)(2,1)}), bf16[32,24,1024]{2,1,0:T(8,128)(2,1)}, u32[]{:S(2)}, u32[]{:S(2)}) %all-to-all-start) | async-done | bytes 1572896 | tf_op jit(solution)/shard_map/all_to_all | solution.py:317
  65.2 1.4 copy-done
  66.6 1.4 copy-done.1
  68.0 1.4 copy-done.2
  69.7 13.9 %collective-permute-done.2.refs_0_ = bf16[584,2048]{1,0:T(8,128)(2,1)S(1)} collective-permute-done((bf16[584,2048]{1,0:T(8,128)(2,1)}, bf16[584,2048]{1,0:T(8,128)(2,1)S(1)}, u32[]{:S(2)}, u32[]{:S(2)}) %collective-permute-start.2) | collective-permute-done | bytes 2392096 | tf_op jit(solution)/shard_map/ppermute | solution.py:313
  83.8 6.3 %shard_map.153 = (bf16[32,2,8,1024]{3,2,1,0:T(8,128)(2,1)S(1)}, bf16[256,384]{1,0:T(8,128)(2,1)S(1)}, bf16[256,768]{1,0:T(8,128)(2,1)S(1)}, f32[256,64]{1,0:T(8,...) custom-call(bf16[32,24,1024]{2,1,0:T(8,128)(2,1)} %all-to-all-done.refs_0_.refs_2_, ...), custom_call_target="tpu_custom_call" | custom-call | flops 4000000000 | bytes 9986048 | tf_op jit(solution)/shard_map/pallas_call | solution.py:49
  90.2 0.5 collective-permute-start.6
  90.7 1.0 shard_map.154.refs_0_
  91.7 1.1 collective-permute-done.3.refs_1_
  92.9 1.1 shard_map.155
  93.9 11.1 %all-to-all-start.1 = ((bf16[64,8,1024]{2,1,0:T(8,128)(2,1)}), bf16[64,8,1024]{2,1,0:T(8,128)(2,1)S(1)}, u32[]{:S(2)}, u32[]{:S(2)}) async-start(bf16[64,8,1024]{2,1,0:T(8,128)(2,1)} %bitcast.7), calls=%async_computation.1 | async-start | bytes 2097152 | tf_op jit(solution)/shard_map/all_to_all | solution.py:321
  105.1 1.6 %shard_map.158 = f32[64,1024]{1,0:T(8,128)S(1)} custom-call(f32[256,64]{1,0:T(8,128)S(1)} %get-tuple-element.29.refs_0_, f32[256,64]{1,0:T(8,128)S(1)} %collective-permute-done.6.refs_1_, bf16[32,24,1024]{2,1,0:T(8,128)(2,1)} %all-to-all-done.refs_0_.refs_2_), custom_call_target="tpu_custom_call" | custom-call | flops 100000000 | bytes 1966080 | tf_op jit(solution)/shard_map/pallas_call | solution.py:49
  106.9 1.5 %collective-permute-done.7 = f32[64,1024]{1,0:T(8,128)S(1)} collective-permute-done((f32[64,1024]{1,0:T(8,128)S(1)}, f32[64,1024]{1,0:T(8,128)S(1)}, u32[]{:S(2)}, u32[]{:S(2)}) %collective-permute-start.7) | collective-permute-done | bytes 262176 | tf_op jit(solution)/shard_map/ppermute | solution.py:313
  108.5 2.8 %collective-permute-start.8 = (f32[64,2048]{1,0:T(8,128)S(1)}, f32[64,2048]{1,0:T(8,128)}, u32[]{:S(2)}, u32[]{:S(2)}) collective-permute-start(f32[64,2048]{1,0:T(8,128)S(1)} %pad_maximum_fusion.1), channel_id=1, source_target_pairs={{0,2},{2,0},{1,3},{3,1},{4,6},{6,4},{5,7},{7,5},{8,10},{10,8},{9,1... | collective-permute-start | bytes 1572872 | tf_op jit(solution)/shard_map/ppermute | solution.py:313
  111.3 0.8 collective-permute-start.5
  112.1 0.8 shard_map.148.refs_0_
  113.0 20.9 %collective-permute-done.5 = f32[64,192]{1,0:T(8,128)S(1)} collective-permute-done((f32[64,192]{1,0:T(8,128)S(1)}, f32[64,192]{1,0:T(8,128)S(1)}, u32[]{:S(2)}, u32[]{:S(2)}) %collective-permute-start.5) | collective-permute-done | bytes 49184 | tf_op jit(solution)/shard_map/ppermute | solution.py:313
  133.9 0.7 maximum_bitcast_fusion
  134.6 1.1 select_bitcast_fusion.1
  135.7 0.8 shard_map.156
  136.6 2.1 %collective-permute-start.4 = (bf16[2,48,512]{2,1,0:T(8,128)(2,1)S(1)}, bf16[2,48,512]{2,1,0:T(8,128)(2,1)S(1)}, u32[]{:S(2)}, u32[]{:S(2)}) collective-permute-start(bf16[2,48,512]{2,1,0:T(8,128)(2,1)S(1)} %get-tuple-element.24), channel_id=1, source_target_pairs={{0,2},{2,0},{1,3},{3,1},{4,6},{6,4},{5,7},{7,5},{8,10},{10,8},{9,1... | collective-permute-start | bytes 294920 | tf_op jit(solution)/shard_map/ppermute | solution.py:313
  138.7 1.1 pad_maximum_fusion
  139.8 3.0 %collective-permute-done.4.refs_1_ = bf16[2,48,512]{2,1,0:T(8,128)(2,1)S(1)} collective-permute-done((bf16[2,48,512]{2,1,0:T(8,128)(2,1)S(1)}, bf16[2,48,512]{2,1,0:T(8,128)(2,1)S(1)}, u32[]{:S(2)}, u32[]{:S(2)}) %collective-permute-start.4) | collective-permute-done | bytes 98336 | tf_op jit(solution)/shard_map/ppermute | solution.py:313
  142.8 0.6 shard_map.157
  (23 shorter events, 0.8 us)
Async XLA Ops:
  3.1 9.4 %collective-permute-start = (bf16[152,1024]{1,0:T(8,128)(2,1)}, bf16[152,1024]{1,0:T(8,128)(2,1)S(1)}, u32[]{:S(2)}, u32[]{:S(2)}) collective-permute-start(bf16[152,1024]{1,0:T(8,128)(2,1)} %shard_map.147.refs_0_), channel_id=1, source_target_pairs={{0,4},{4,0},{1,5},{5,1},{2,6},{6,2},{3,7},{7,3},{8,12},{12,8},{9,1... | collective-permute-start | bytes 933896 | tf_op jit(solution)/shard_map/ppermute | solution.py:313
  12.5 1.0 copy-start.3
  15.3 49.9 %all-to-all-start = ((bf16[32,24,1024]{2,1,0:T(8,128)(2,1)}), bf16[32,24,1024]{2,1,0:T(8,128)(2,1)}, u32[]{:S(2)}, u32[]{:S(2)}) async-start(bf16[32,24,1024]{2,1,0:T(8,128)(2,1)} %shard_map.149), calls=%async_computation | async-start | bytes 3145728 | tf_op jit(solution)/shard_map/all_to_all | solution.py:317
  26.7 38.5 %copy-start.5 = (bf16[2,64,2048]{2,1,0:T(8,128)(2,1)S(1)}, bf16[2,64,2048]{2,1,0:T(8,128)(2,1)}, u32[]{:S(2)}) copy-start(bf16[2,64,2048]{2,1,0:T(8,128)(2,1)} %refs_4_.1) | copy-start | bytes 1572868
  26.7 38.5 %copy-start.6 = (bf16[2,192,64]{1,2,0:T(8,128)(2,1)S(1)}, bf16[2,192,64]{1,2,0:T(8,128)(2,1)}, u32[]{:S(2)}) copy-start(bf16[2,192,64]{1,2,0:T(8,128)(2,1)} %param.22) | copy-start | bytes 147460
  29.5 54.1 %collective-permute-start.2 = (bf16[584,2048]{1,0:T(8,128)(2,1)}, bf16[584,2048]{1,0:T(8,128)(2,1)S(1)}, u32[]{:S(2)}, u32[]{:S(2)}) collective-permute-start(bf16[584,2048]{1,0:T(8,128)(2,1)} %shard_map.151), channel_id=1, source_target_pairs={{0,2},{2,0},{1,3},{3,1},{4,6},{6,4},{5,7},{7,5},{8,10},{10,8},{9,1... | collective-permute-start | bytes 7176200 | tf_op jit(solution)/shard_map/ppermute | solution.py:313
  65.2 18.6 %collective-permute-start.1 = (bf16[32,24,1024]{2,1,0:T(8,128)(2,1)}, bf16[32,24,1024]{2,1,0:T(8,128)(2,1)S(1)}, u32[]{:S(2)}, u32[]{:S(2)}) collective-permute-start(bf16[32,24,1024]{2,1,0:T(8,128)(2,1)} %all-to-all-done.refs_0_.refs_2_), channel_id=1, source_target_pairs={{0,1},{1,0},{2,3},{3,2},{4,5},{5,4},{6,7},{7,6},{8,9},{9,8},{10,11... | collective-permute-start | bytes 4718600 | tf_op jit(solution)/shard_map/ppermute | solution.py:313
  65.2 1.4 copy-start
  66.6 1.4 copy-start.1
  68.0 1.4 copy-start.2
  90.1 2.7 %collective-permute-start.3 = (bf16[32,2,8,1024]{3,2,1,0:T(8,128)(2,1)S(1)}, bf16[32,2,8,1024]{3,2,1,0:T(8,128)(2,1)S(1)}, u32[]{:S(2)}, u32[]{:S(2)}) collective-permute-start(bf16[32,2,8,1024]{3,2,1,0:T(8,128)(2,1)S(1)} %get-tuple-element.22), channel_id=1, source_target_pairs={{0,1},{1,0},{2,3},{3,2},{4,5},{5,4},{6,7},{7,6},{8,9},{9,8},{10,11... | collective-permute-start | bytes 3145736 | tf_op jit(solution)/shard_map/ppermute | solution.py:313
  90.2 14.9 %collective-permute-start.6 = (f32[256,64]{1,0:T(8,128)S(1)}, f32[256,64]{1,0:T(8,128)S(1)}, u32[]{:S(2)}, u32[]{:S(2)}) collective-permute-start(f32[256,64]{1,0:T(8,128)S(1)} %get-tuple-element.29.refs_0_), channel_id=1, source_target_pairs={{0,1},{1,0},{2,3},{3,2},{4,5},{5,4},{6,7},{7,6},{8,9},{9,8},{10,11... | collective-permute-start | bytes 196616 | tf_op jit(solution)/shard_map/ppermute | solution.py:313
  93.9 41.8 %all-to-all-start.1 = ((bf16[64,8,1024]{2,1,0:T(8,128)(2,1)}), bf16[64,8,1024]{2,1,0:T(8,128)(2,1)S(1)}, u32[]{:S(2)}, u32[]{:S(2)}) async-start(bf16[64,8,1024]{2,1,0:T(8,128)(2,1)} %bitcast.7), calls=%async_computation.1 | async-start | bytes 2097152 | tf_op jit(solution)/shard_map/all_to_all | solution.py:321
  106.7 1.6 %collective-permute-start.7 = (f32[64,1024]{1,0:T(8,128)S(1)}, f32[64,1024]{1,0:T(8,128)S(1)}, u32[]{:S(2)}, u32[]{:S(2)}) collective-permute-start(f32[64,1024]{1,0:T(8,128)S(1)} %shard_map.158), channel_id=1, source_target_pairs={{0,1},{1,0},{2,3},{3,2},{4,5},{5,4},{6,7},{7,6},{8,9},{9,8},{10,11... | collective-permute-start | bytes 786440 | tf_op jit(solution)/shard_map/ppermute | solution.py:313
  106.8 5.3 %copy-start.4 = (bf16[152,1024]{1,0:T(8,128)(2,1)S(1)}, bf16[152,1024]{1,0:T(8,128)(2,1)}, u32[]{:S(2)}) copy-start(bf16[152,1024]{1,0:T(8,128)(2,1)} %shard_map.147.refs_0_) | copy-start | bytes 933892
  108.5 26.1 %collective-permute-start.8 = (f32[64,2048]{1,0:T(8,128)S(1)}, f32[64,2048]{1,0:T(8,128)}, u32[]{:S(2)}, u32[]{:S(2)}) collective-permute-start(f32[64,2048]{1,0:T(8,128)S(1)} %pad_maximum_fusion.1), channel_id=1, source_target_pairs={{0,2},{2,0},{1,3},{3,1},{4,6},{6,4},{5,7},{7,5},{8,10},{10,8},{9,1... | collective-permute-start | bytes 1572872 | tf_op jit(solution)/shard_map/ppermute | solution.py:313
  111.3 22.6 %collective-permute-start.5 = (f32[64,192]{1,0:T(8,128)S(1)}, f32[64,192]{1,0:T(8,128)S(1)}, u32[]{:S(2)}, u32[]{:S(2)}) collective-permute-start(f32[64,192]{1,0:T(8,128)S(1)} %get-tuple-element.28), channel_id=1, source_target_pairs={{0,2},{2,0},{1,3},{3,1},{4,6},{6,4},{5,7},{7,5},{8,10},{10,8},{9,1... | collective-permute-start | bytes 147464 | tf_op jit(solution)/shard_map/ppermute | solution.py:313
  136.6 6.2 %collective-permute-start.4 = (bf16[2,48,512]{2,1,0:T(8,128)(2,1)S(1)}, bf16[2,48,512]{2,1,0:T(8,128)(2,1)S(1)}, u32[]{:S(2)}, u32[]{:S(2)}) collective-permute-start(bf16[2,48,512]{2,1,0:T(8,128)(2,1)S(1)} %get-tuple-element.24), channel_id=1, source_target_pairs={{0,2},{2,0},{1,3},{3,1},{4,6},{6,4},{5,7},{7,5},{8,10},{10,8},{9,1... | collective-permute-start | bytes 294920 | tf_op jit(solution)/shard_map/ppermute | solution.py:313

commit v6 on v5

--- a/solution.py
+++ b/solution.py
@@ -1,3 +1,4 @@
+import functools
 import jax
 import jax.numpy as jnp
 from jax import lax
@@ -302,11 +303,11 @@
     out[...] = SCALE * tn(inner, cot[:, 16:24, :].reshape(ROWS, 2 * Q))
 
 
-def combine_body(where, table, back, own, to_xh):
-    for at, out in ((where[2], own), (1 - where[2], to_xh)):
-        rows = back[:, :, pl.ds(pl.multiple_of(at * Q, Q), Q)].reshape(2 * ROWS, Q)
-        out[0] = (nn(table[3], rows) + nn(table[2], rows) + nn(table[1], rows)).astype(out.dtype)
-        out[1] = nn(table[0], rows).astype(out.dtype)
+def combine_body(away, where, table, back, out):
+    at = 1 - where[2] if away else where[2]
+    rows = back[:, :, pl.ds(pl.multiple_of(at * Q, Q), Q)].reshape(2 * ROWS, Q)
+    out[0] = (nn(table[3], rows) + nn(table[2], rows) + nn(table[1], rows)).astype(out.dtype)
+    out[1] = nn(table[0], rows).astype(out.dtype)
 
 
 def swap(x, axis):
@@ -375,7 +376,8 @@
         [pltpu.VMEM(wide.shape, BF), pltpu.SemaphoreType.DMA((4,))], "vv", "h", limit=48 << 20,
     )
     back = exchange_home(total.reshape(2 * PEERS, 8, 2 * Q))
-    here, to_xh = vmem_call(combine_body, [sds((2, TOK, Q), F32), sds((2, TOK, Q), BF)], [table, back], mib=8)
+    (to_xh,) = vmem_call(functools.partial(combine_body, True), [sds((2, TOK, Q), BF)], [table, back], mib=8)
+    (here,) = vmem_call(functools.partial(combine_body, False), [sds((2, TOK, Q), F32)], [table, back], mib=8)
     from_xh = swap(to_xh, "xh")
     frozen_out, input_grad = vmem_call(last_body, [sds((TOK, Q), BF)] * 2, [here, from_xh], mib=4)
 

time: 144 us -> 144 us (level)
    pallas_call x12 -> x13, Pallas kernels: 19.8 us -> 19.9 us  [kernel(): pl.pallas_call(run, out_shape=outs, in_specs=[SPACES[x] for x in ins], ou...]
  transfers between devices with their start and end apart: 11 -> 11, of which waited for: 7 -> 7; matrix products, arithmetic and copies ran while one was open for 2% -> 2% of each run, Pallas kernels for 5% -> 6%
where the time goes in v6:
time: 144 us; the launch traced here: 143 us
  waiting for transfers between devices  80.4 us (56%)
  starting transfers between devices  33.7 us (23%)
  Pallas kernels  19.9 us (14%)
  local copies, waits for them, and re-layouts  5.24 us (4%)
  other arithmetic  2.96 us (2%)
    ppermute x9, waiting for transfers between devices, swap(): return lax.ppermute(x, axis, [(0, 1), (1, 0)])  47.8 us
    all_to_all x1, waiting for transfers between devices, exchange(): lax.all_to_all(x, ('y', 'z'), split_axis=0, concat_axis=0, tiled=True)  32.5 us
    pallas_call x13, Pallas kernels, kernel(): pl.pallas_call(run, out_shape=outs, in_specs=[SPACES[x] for x in ins], ou...  19.9 us
    all_to_all x1, starting transfers between devices, exchange(): lax.all_to_all(x, ('y', 'z'), split_axis=0, concat_axis=0, tiled=True)  11.4 us
    ppermute x9, starting transfers between devices, swap(): return lax.ppermute(x, axis, [(0, 1), (1, 0)])  11.1 us
    all_to_all x1, starting transfers between devices, exchange_home(): lax.all_to_all(x, ('y', 'z', 'xl'), split_axis=0, concat_axis=0, tiled=True)  11.1 us
    unnamed x14, local copies, waits for them, and re-layouts  5.2 us
  transfers between devices with their start and end apart: 11, of which 7 were waited for; matrix products, arithmetic and copies ran while one was open for 2% of the time, Pallas kernels for 6%

profile of v6, /device:TPU:32, one launch (start us, length us, event | category | flops | bytes accessed | tf_op | source)
XLA Modules:
  0.0 143.0 jit_solution(13537491421617313983)
XLA Ops:
  0.6 2.4 %shard_map.147.refs_0_ = bf16[152,1024]{1,0:T(8,128)(2,1)} custom-call(bf16[48,2048]{1,0:T(8,128)(2,1)} %refs_0_.1, bf16[48,2048]{1,0:T(8,128)(2,1)} %refs_1_.1, bf16[48,2048]{1,0:T(8,128)(2,1)} %refs_2_.3, s32[8,48]{1,0:T(8,128)} %bitcast.24, f32[8,48]{1,0:T(8,128)} %bitcast.25, s32[8,48]{1,0:T(8,128)} %bitcast.26, f32[8,48]{1,0:T(8,128)} %bitcast.27), custom_call_target="tpu_custom_call" | custom-call | flops 100000000 | bytes 907264 | tf_op jit(solution)/shard_map/pallas_call | solution.py:50
  3.1 1.6 %collective-permute-start = (bf16[152,1024]{1,0:T(8,128)(2,1)}, bf16[152,1024]{1,0:T(8,128)(2,1)S(1)}, u32[]{:S(2)}, u32[]{:S(2)}) collective-permute-start(bf16[152,1024]{1,0:T(8,128)(2,1)} %shard_map.147.refs_0_), channel_id=1, source_target_pairs={{0,4},{4,0},{1,5},{5,1},{2,6},{6,2},{3,7},{7,3},{8,12},{12,8},{9,1... | collective-permute-start | bytes 933896 | tf_op jit(solution)/shard_map/ppermute | solution.py:314
  4.7 7.8 %collective-permute-done.refs_1_ = bf16[152,1024]{1,0:T(8,128)(2,1)S(1)} collective-permute-done((bf16[152,1024]{1,0:T(8,128)(2,1)}, bf16[152,1024]{1,0:T(8,128)(2,1)S(1)}, u32[]{:S(2)}, u32[]{:S(2)}) %collective-permute-start) | collective-permute-done | bytes 311328 | tf_op jit(solution)/shard_map/ppermute | solution.py:314
  12.5 1.0 copy-done.3
  13.4 1.8 %shard_map.149 = bf16[32,24,1024]{2,1,0:T(8,128)(2,1)} custom-call(bf16[152,1024]{1,0:T(8,128)(2,1)S(1)} %copy-done.3, bf16[152,1024]{1,0:T(8,128)(2,1)S(1)} %collective-permute-done.refs_1_), custom_call_target="tpu_custom_call" | custom-call | flops 100000000 | bytes 2195456 | tf_op jit(solution)/shard_map/pallas_call | solution.py:50
  15.3 11.4 %all-to-all-start = ((bf16[32,24,1024]{2,1,0:T(8,128)(2,1)}), bf16[32,24,1024]{2,1,0:T(8,128)(2,1)}, u32[]{:S(2)}, u32[]{:S(2)}) async-start(bf16[32,24,1024]{2,1,0:T(8,128)(2,1)} %shard_map.149), calls=%async_computation | async-start | bytes 3145728 | tf_op jit(solution)/shard_map/all_to_all | solution.py:318
  26.7 2.8 %shard_map.151 = bf16[584,2048]{1,0:T(8,128)(2,1)} custom-call(bf16[2,192,2048]{2,1,0:T(8,128)(2,1)} %bitcast.18, bf16[2,192,2048]{2,1,0:T(8,128)(2,1)} %bitcast.20, bf16[2,192,2048]{2,1,0:T(8,128)(2,1)} %refs_2_.5, bf16[2,64,192]{2,1,0:T(8,128)(2,1)} %bitcast.22), custom_call_target="tpu_custom_call" | custom-call | flops 100000000 | bytes 7159808 | tf_op jit(solution)/shard_map/pallas_call | solution.py:50
  29.5 3.1 %collective-permute-start.2 = (bf16[584,2048]{1,0:T(8,128)(2,1)}, bf16[584,2048]{1,0:T(8,128)(2,1)S(1)}, u32[]{:S(2)}, u32[]{:S(2)}) collective-permute-start(bf16[584,2048]{1,0:T(8,128)(2,1)} %shard_map.151), channel_id=1, source_target_pairs={{0,2},{2,0},{1,3},{3,1},{4,6},{6,4},{5,7},{7,5},{8,10},{10,8},{9,1... | collective-permute-start | bytes 7176200 | tf_op jit(solution)/shard_map/ppermute | solution.py:314
  32.6 32.5 %all-to-all-done.refs_0_.refs_2_ = bf16[32,24,1024]{2,1,0:T(8,128)(2,1)} async-done(((bf16[32,24,1024]{2,1,0:T(8,128)(2,1)}), bf16[32,24,1024]{2,1,0:T(8,128)(2,1)}, u32[]{:S(2)}, u32[]{:S(2)}) %all-to-all-start) | async-done | bytes 1572896 | tf_op jit(solution)/shard_map/all_to_all | solution.py:318
  65.2 1.4 copy-done
  66.6 1.4 copy-done.1
  68.0 1.4 copy-done.2
  69.7 13.9 %collective-permute-done.2.refs_0_ = bf16[584,2048]{1,0:T(8,128)(2,1)S(1)} collective-permute-done((bf16[584,2048]{1,0:T(8,128)(2,1)}, bf16[584,2048]{1,0:T(8,128)(2,1)S(1)}, u32[]{:S(2)}, u32[]{:S(2)}) %collective-permute-start.2) | collective-permute-done | bytes 2392096 | tf_op jit(solution)/shard_map/ppermute | solution.py:314
  83.8 6.3 %shard_map.153 = (bf16[32,2,8,1024]{3,2,1,0:T(8,128)(2,1)S(1)}, bf16[256,384]{1,0:T(8,128)(2,1)S(1)}, bf16[256,768]{1,0:T(8,128)(2,1)S(1)}, f32[256,64]{1,0:T(8,...) custom-call(bf16[32,24,1024]{2,1,0:T(8,128)(2,1)} %all-to-all-done.refs_0_.refs_2_, ...), custom_call_target="tpu_custom_call" | custom-call | flops 4000000000 | bytes 9986048 | tf_op jit(solution)/shard_map/pallas_call | solution.py:50
  90.2 0.5 collective-permute-start.6
  90.7 1.0 shard_map.154.refs_0_
  91.7 1.1 collective-permute-done.3.refs_1_
  92.8 1.1 shard_map.155
  93.9 11.1 %all-to-all-start.1 = ((bf16[64,8,1024]{2,1,0:T(8,128)(2,1)}), bf16[64,8,1024]{2,1,0:T(8,128)(2,1)S(1)}, u32[]{:S(2)}, u32[]{:S(2)}) async-start(bf16[64,8,1024]{2,1,0:T(8,128)(2,1)} %bitcast.7), calls=%async_computation.1 | async-start | bytes 2097152 | tf_op jit(solution)/shard_map/all_to_all | solution.py:322
  105.0 1.6 %shard_map.159 = f32[64,1024]{1,0:T(8,128)S(1)} custom-call(f32[256,64]{1,0:T(8,128)S(1)} %get-tuple-element.25.refs_0_, f32[256,64]{1,0:T(8,128)S(1)} %collective-permute-done.6.refs_1_, bf16[32,24,1024]{2,1,0:T(8,128)(2,1)} %all-to-all-done.refs_0_.refs_2_), custom_call_target="tpu_custom_call" | custom-call | flops 100000000 | bytes 1966080 | tf_op jit(solution)/shard_map/pallas_call | solution.py:50
  106.8 1.5 %collective-permute-done.7 = f32[64,1024]{1,0:T(8,128)S(1)} collective-permute-done((f32[64,1024]{1,0:T(8,128)S(1)}, f32[64,1024]{1,0:T(8,128)S(1)}, u32[]{:S(2)}, u32[]{:S(2)}) %collective-permute-start.7) | collective-permute-done | bytes 262176 | tf_op jit(solution)/shard_map/ppermute | solution.py:314
  108.5 2.8 %collective-permute-start.8 = (f32[64,2048]{1,0:T(8,128)S(1)}, f32[64,2048]{1,0:T(8,128)}, u32[]{:S(2)}, u32[]{:S(2)}) collective-permute-start(f32[64,2048]{1,0:T(8,128)S(1)} %pad_maximum_fusion.1), channel_id=1, source_target_pairs={{0,2},{2,0},{1,3},{3,1},{4,6},{6,4},{5,7},{7,5},{8,10},{10,8},{9,1... | collective-permute-start | bytes 1572872 | tf_op jit(solution)/shard_map/ppermute | solution.py:314
  111.3 0.8 collective-permute-start.5
  112.1 0.8 shard_map.148.refs_0_
  112.9 20.9 %collective-permute-done.5 = f32[64,192]{1,0:T(8,128)S(1)} collective-permute-done((f32[64,192]{1,0:T(8,128)S(1)}, f32[64,192]{1,0:T(8,128)S(1)}, u32[]{:S(2)}, u32[]{:S(2)}) %collective-permute-start.5) | collective-permute-done | bytes 49184 | tf_op jit(solution)/shard_map/ppermute | solution.py:314
  133.9 0.7 maximum_bitcast_fusion
  134.5 1.1 select_bitcast_fusion.1
  135.7 0.5 shard_map.157
  136.2 2.1 %collective-permute-start.4 = (bf16[2,48,512]{2,1,0:T(8,128)(2,1)S(1)}, bf16[2,48,512]{2,1,0:T(8,128)(2,1)S(1)}, u32[]{:S(2)}, u32[]{:S(2)}) collective-permute-start(bf16[2,48,512]{2,1,0:T(8,128)(2,1)S(1)} %shard_map.157), channel_id=1, source_target_pairs={{0,2},{2,0},{1,3},{3,1},{4,6},{6,4},{5,7},{7,5},{8,10},{10,8},{9,1... | collective-permute-start | bytes 294920 | tf_op jit(solution)/shard_map/ppermute | solution.py:314
  138.3 1.1 pad_maximum_fusion
  139.8 2.5 %collective-permute-done.4.refs_1_ = bf16[2,48,512]{2,1,0:T(8,128)(2,1)S(1)} collective-permute-done((bf16[2,48,512]{2,1,0:T(8,128)(2,1)S(1)}, bf16[2,48,512]{2,1,0:T(8,128)(2,1)S(1)}, u32[]{:S(2)}, u32[]{:S(2)}) %collective-permute-start.4) | collective-permute-done | bytes 98336 | tf_op jit(solution)/shard_map/ppermute | solution.py:314
  142.4 0.6 shard_map.158
  (24 shorter events, 1.3 us)
Async XLA Ops:
  3.1 9.4 %collective-permute-start = (bf16[152,1024]{1,0:T(8,128)(2,1)}, bf16[152,1024]{1,0:T(8,128)(2,1)S(1)}, u32[]{:S(2)}, u32[]{:S(2)}) collective-permute-start(bf16[152,1024]{1,0:T(8,128)(2,1)} %shard_map.147.refs_0_), channel_id=1, source_target_pairs={{0,4},{4,0},{1,5},{5,1},{2,6},{6,2},{3,7},{7,3},{8,12},{12,8},{9,1... | collective-permute-start | bytes 933896 | tf_op jit(solution)/shard_map/ppermute | solution.py:314
  12.5 1.0 copy-start.3
  15.3 49.9 %all-to-all-start = ((bf16[32,24,1024]{2,1,0:T(8,128)(2,1)}), bf16[32,24,1024]{2,1,0:T(8,128)(2,1)}, u32[]{:S(2)}, u32[]{:S(2)}) async-start(bf16[32,24,1024]{2,1,0:T(8,128)(2,1)} %shard_map.149), calls=%async_computation | async-start | bytes 3145728 | tf_op jit(solution)/shard_map/all_to_all | solution.py:318
  26.7 38.5 %copy-start.5 = (bf16[2,64,2048]{2,1,0:T(8,128)(2,1)S(1)}, bf16[2,64,2048]{2,1,0:T(8,128)(2,1)}, u32[]{:S(2)}) copy-start(bf16[2,64,2048]{2,1,0:T(8,128)(2,1)} %refs_4_.1) | copy-start | bytes 1572868
  26.7 38.4 %copy-start.6 = (bf16[2,192,64]{1,2,0:T(8,128)(2,1)S(1)}, bf16[2,192,64]{1,2,0:T(8,128)(2,1)}, u32[]{:S(2)}) copy-start(bf16[2,192,64]{1,2,0:T(8,128)(2,1)} %param.22) | copy-start | bytes 147460
  29.5 54.1 %collective-permute-start.2 = (bf16[584,2048]{1,0:T(8,128)(2,1)}, bf16[584,2048]{1,0:T(8,128)(2,1)S(1)}, u32[]{:S(2)}, u32[]{:S(2)}) collective-permute-start(bf16[584,2048]{1,0:T(8,128)(2,1)} %shard_map.151), channel_id=1, source_target_pairs={{0,2},{2,0},{1,3},{3,1},{4,6},{6,4},{5,7},{7,5},{8,10},{10,8},{9,1... | collective-permute-start | bytes 7176200 | tf_op jit(solution)/shard_map/ppermute | solution.py:314
  65.1 18.6 %collective-permute-start.1 = (bf16[32,24,1024]{2,1,0:T(8,128)(2,1)}, bf16[32,24,1024]{2,1,0:T(8,128)(2,1)S(1)}, u32[]{:S(2)}, u32[]{:S(2)}) collective-permute-start(bf16[32,24,1024]{2,1,0:T(8,128)(2,1)} %all-to-all-done.refs_0_.refs_2_), channel_id=1, source_target_pairs={{0,1},{1,0},{2,3},{3,2},{4,5},{5,4},{6,7},{7,6},{8,9},{9,8},{10,11... | collective-permute-start | bytes 4718600 | tf_op jit(solution)/shard_map/ppermute | solution.py:314
  65.2 1.4 copy-start
  66.6 1.4 copy-start.1
  68.0 1.4 copy-start.2
  90.1 2.7 %collective-permute-start.3 = (bf16[32,2,8,1024]{3,2,1,0:T(8,128)(2,1)S(1)}, bf16[32,2,8,1024]{3,2,1,0:T(8,128)(2,1)S(1)}, u32[]{:S(2)}, u32[]{:S(2)}) collective-permute-start(bf16[32,2,8,1024]{3,2,1,0:T(8,128)(2,1)S(1)} %get-tuple-element.20), channel_id=1, source_target_pairs={{0,1},{1,0},{2,3},{3,2},{4,5},{5,4},{6,7},{7,6},{8,9},{9,8},{10,11... | collective-permute-start | bytes 3145736 | tf_op jit(solution)/shard_map/ppermute | solution.py:314
  90.2 14.8 %collective-permute-start.6 = (f32[256,64]{1,0:T(8,128)S(1)}, f32[256,64]{1,0:T(8,128)S(1)}, u32[]{:S(2)}, u32[]{:S(2)}) collective-permute-start(f32[256,64]{1,0:T(8,128)S(1)} %get-tuple-element.25.refs_0_), channel_id=1, source_target_pairs={{0,1},{1,0},{2,3},{3,2},{4,5},{5,4},{6,7},{7,6},{8,9},{9,8},{10,11... | collective-permute-start | bytes 196616 | tf_op jit(solution)/shard_map/ppermute | solution.py:314
  93.9 41.8 %all-to-all-start.1 = ((bf16[64,8,1024]{2,1,0:T(8,128)(2,1)}), bf16[64,8,1024]{2,1,0:T(8,128)(2,1)S(1)}, u32[]{:S(2)}, u32[]{:S(2)}) async-start(bf16[64,8,1024]{2,1,0:T(8,128)(2,1)} %bitcast.7), calls=%async_computation.1 | async-start | bytes 2097152 | tf_op jit(solution)/shard_map/all_to_all | solution.py:322
  106.7 1.6 %collective-permute-start.7 = (f32[64,1024]{1,0:T(8,128)S(1)}, f32[64,1024]{1,0:T(8,128)S(1)}, u32[]{:S(2)}, u32[]{:S(2)}) collective-permute-start(f32[64,1024]{1,0:T(8,128)S(1)} %shard_map.159), channel_id=1, source_target_pairs={{0,1},{1,0},{2,3},{3,2},{4,5},{5,4},{6,7},{7,6},{8,9},{9,8},{10,11... | collective-permute-start | bytes 786440 | tf_op jit(solution)/shard_map/ppermute | solution.py:314
  106.8 5.3 %copy-start.4 = (bf16[152,1024]{1,0:T(8,128)(2,1)S(1)}, bf16[152,1024]{1,0:T(8,128)(2,1)}, u32[]{:S(2)}) copy-start(bf16[152,1024]{1,0:T(8,128)(2,1)} %shard_map.147.refs_0_) | copy-start | bytes 933892
  108.5 26.1 %collective-permute-start.8 = (f32[64,2048]{1,0:T(8,128)S(1)}, f32[64,2048]{1,0:T(8,128)}, u32[]{:S(2)}, u32[]{:S(2)}) collective-permute-start(f32[64,2048]{1,0:T(8,128)S(1)} %pad_maximum_fusion.1), channel_id=1, source_target_pairs={{0,2},{2,0},{1,3},{3,1},{4,6},{6,4},{5,7},{7,5},{8,10},{10,8},{9,1... | collective-permute-start | bytes 1572872 | tf_op jit(solution)/shard_map/ppermute | solution.py:314
  111.3 22.6 %collective-permute-start.5 = (f32[64,192]{1,0:T(8,128)S(1)}, f32[64,192]{1,0:T(8,128)S(1)}, u32[]{:S(2)}, u32[]{:S(2)}) collective-permute-start(f32[64,192]{1,0:T(8,128)S(1)} %get-tuple-element.24), channel_id=1, source_target_pairs={{0,2},{2,0},{1,3},{3,1},{4,6},{6,4},{5,7},{7,5},{8,10},{10,8},{9,1... | collective-permute-start | bytes 147464 | tf_op jit(solution)/shard_map/ppermute | solution.py:314
  136.2 6.2 %collective-permute-start.4 = (bf16[2,48,512]{2,1,0:T(8,128)(2,1)S(1)}, bf16[2,48,512]{2,1,0:T(8,128)(2,1)S(1)}, u32[]{:S(2)}, u32[]{:S(2)}) collective-permute-start(bf16[2,48,512]{2,1,0:T(8,128)(2,1)S(1)} %shard_map.157), channel_id=1, source_target_pairs={{0,2},{2,0},{1,3},{3,1},{4,6},{6,4},{5,7},{7,5},{8,10},{10,8},{9,1... | collective-permute-start | bytes 294920 | tf_op jit(solution)/shard_map/ppermute | solution.py:314
